TPU v7x, 32 devices: a whole 2x2x4 slice. The times are simulated.
32 devices in a mesh: ctx: 8 (over y, x, core), head: 4 (over z).
Axes of the slice: x: 2, y: 2, z: 4, core: 2. Of those that a mesh axis runs over, the one named last changes fastest.
Arguments:
- queries: bfloat16 [8192, 2048], P('ctx', 'head'), may hold values from -18 to 18
- keys: bfloat16 [8192, 2048], P('ctx', 'head'), may hold values from -6 to 6
- values: bfloat16 [8192, 2048], P('ctx', 'head'), may hold values from -6 to 6
- rates: float32 [8192, 4], P('ctx', 'head'), may hold values from 0.00048828125 to 0.0048828125
- fast_w1: bfloat16 [4, 512, 512], P('head'), may hold values from -0.25 to 0.25
- fast_w2: bfloat16 [4, 512, 512], P('head'), may hold values from -2 to 2
- fast_w3: bfloat16 [4, 512, 512], P('head'), may hold values from -0.25 to 0.25
- norm_gain: bfloat16 [2048], P('head'), may hold values from 0.25 to 1.75
- out_weight: bfloat16 [2048, 2048], P('head'), may hold values from -0.125 to 0.125
Outputs:
- output: bfloat16 [8192, 2048], P(('ctx', 'head'))
All inputs are finite; a program needn't handle non-finite values.
Results may differ from a plain program's by a relative error of at most 0.014.
Values may be sent and summed in bfloat16 or wider, within the bound.
No kernel may reach another device: no remote copies, remote signals or barrier semaphores. Data moves between devices by JAX's collectives and lax.ppermute only.
A program may use at most 64 MiB of HBM per device.

v0:
```python
import math

import jax
import jax.numpy as jnp
from jax import lax
from jax.sharding import PartitionSpec as P

WINDOW = 256


EPSILON = 1e-06


def from_behind(value, axis, by):
    count = lax.axis_size(axis)
    pairs = [(i, i + by) for i in range(count) if 0 <= i + by < count]
    return lax.ppermute(value, axis, pairs)


def contract_rows(left_side, right_side):
    return lax.dot_general(
        left_side, right_side, (((0,), (0,)), ((), ())), preferred_element_type=jnp.float32
    )


def renorm(weight, push, axis_dim):
    widened = weight.astype(jnp.float32)
    updated = widened + push
    old_norm = jnp.sqrt(jnp.mean(widened * widened, axis=axis_dim, keepdims=True) + EPSILON)
    new_norm = jnp.sqrt(jnp.mean(updated * updated, axis=axis_dim, keepdims=True) + EPSILON)
    return (updated * (old_norm / new_norm)).astype(jnp.bfloat16)


def fast_pushes(key_rows, value_rows, rate_column, gate_weight, down_weight, up_weight):
    gate_part = jnp.dot(key_rows, gate_weight, preferred_element_type=jnp.float32)
    up_part = jnp.dot(key_rows, up_weight, preferred_element_type=jnp.float32)
    sigmoid_gate = jax.nn.sigmoid(gate_part)
    activation = (gate_part * sigmoid_gate * up_part).astype(jnp.bfloat16)
    scaled = (value_rows.astype(jnp.float32) * rate_column).astype(jnp.bfloat16)
    back_grad = lax.dot_general(
        scaled, down_weight, (((1,), (1,)), ((), ())), preferred_element_type=jnp.float32
    )
    grad_gate = (
        back_grad * up_part * sigmoid_gate * (1.0 + gate_part * (1.0 - sigmoid_gate))
    ).astype(jnp.bfloat16)
    grad_up = (back_grad * gate_part * sigmoid_gate).astype(jnp.bfloat16)
    return (
        contract_rows(key_rows, grad_gate),
        contract_rows(activation, scaled),
        contract_rows(key_rows, grad_up),
    )


def apply_fast(query_rows, gate_weight, down_weight, up_weight):
    gate_part = jnp.dot(query_rows, gate_weight, preferred_element_type=jnp.float32)
    up_part = jnp.dot(query_rows, up_weight, preferred_element_type=jnp.float32)
    mixed_act = (gate_part * jax.nn.sigmoid(gate_part) * up_part).astype(jnp.bfloat16)
    return jnp.dot(mixed_act, down_weight, preferred_element_type=jnp.float32)


def window_block(query_block, key_block, value_block, query_first, key_first):
    scores = lax.dot_general(
        query_block, key_block, (((1,), (1,)), ((), ())), preferred_element_type=jnp.float32
    )
    scores = scores * (1.0 / math.sqrt(query_block.shape[1]))
    query_pos = query_first + jnp.arange(query_block.shape[0], dtype=jnp.int32)
    key_pos = key_first + jnp.arange(key_block.shape[0], dtype=jnp.int32)
    allowed = (
        (key_pos[None, :] <= query_pos[:, None])
        & (key_pos[None, :] > query_pos[:, None] - WINDOW)
        & (key_pos[None, :] >= 0)
    )
    scores = jnp.where(allowed, scores, -jnp.inf)
    row_peak = jnp.max(scores, axis=1, keepdims=True)
    exponent = jnp.exp(scores - row_peak)
    weights = (exponent / jnp.sum(exponent, axis=1, keepdims=True)).astype(jnp.bfloat16)
    return jnp.dot(weights, value_block, preferred_element_type=jnp.float32)


def body(queries, keys, values, rates, fast_w1, fast_w2, fast_w3, norm_gain, out_weight):
    tok_rows = queries.shape[0]
    head_width = queries.shape[1]
    stacked = jnp.concatenate([fast_w1, fast_w2, fast_w3], axis=0)
    push_one, push_two, push_three = fast_pushes(
        keys, values, rates, fast_w1[0], fast_w2[0], fast_w3[0]
    )
    pushes = jnp.stack([push_one, push_two, push_three])
    key_tail, value_tail = from_behind(
        (keys[tok_rows - WINDOW :], values[tok_rows - WINDOW :]), "ctx", 1
    )
    owned_sum = lax.psum_scatter(pushes, "ctx", scatter_dimension=2, tiled=True)
    span_cols = owned_sum.shape[2]
    own_weight = lax.dynamic_slice_in_dim(stacked, lax.axis_index("ctx") * span_cols, span_cols, 2)
    renewed = lax.all_gather(renorm(own_weight, owned_sum, 1), "ctx", axis=2, tiled=True)
    fast_out = apply_fast(queries, renewed[0], renewed[1], renewed[2])
    key_ext = jnp.concatenate([key_tail, keys], axis=0)
    value_ext = jnp.concatenate([value_tail, values], axis=0)
    offset = lax.axis_index("ctx") * tok_rows
    block_rows = min(512, tok_rows)
    pieces = []
    for block_index in range(tok_rows // block_rows):
        first_row = block_index * block_rows
        pieces.append(
            window_block(
                queries[first_row : first_row + block_rows],
                key_ext[first_row : first_row + block_rows + WINDOW],
                value_ext[first_row : first_row + block_rows + WINDOW],
                offset + first_row,
                offset + first_row - WINDOW,
            )
        )
    window_out = jnp.concatenate(pieces, axis=0)
    combined = fast_out + window_out
    heads_count = lax.axis_size("head")
    squares = lax.psum(jnp.sum(combined * combined, axis=1), "head")
    mean_square = (squares / (head_width * heads_count))[:, None]
    normed = (combined * lax.rsqrt(mean_square + EPSILON) * norm_gain.astype(jnp.float32)).astype(
        jnp.bfloat16
    )
    return lax.psum_scatter(
        jnp.dot(normed, out_weight, preferred_element_type=jnp.float32).astype(jnp.bfloat16),
        "head",
        scatter_dimension=0,
        tiled=True,
    )


def solution(mesh):
    placed = (
        P("ctx", "head"),
        P("ctx", "head"),
        P("ctx", "head"),
        P("ctx", "head"),
        P("head", None, None),
        P("head", None, None),
        P("head", None, None),
        P("head"),
        P("head", None),
    )
    return jax.shard_map(
        body, mesh=mesh, in_specs=placed, out_specs=P(("ctx", "head"), None), check_vma=False
    )
```

profile of v0, /device:TPU:0, one launch (start us, length us, event | category | flops | bytes accessed | tf_op | source)
XLA Modules:
  0.0 200.9 jit_solution(15375525014563792223)
XLA Ops:
  6.5 2.2 %fusion.19 = f32[1024,512]{1,0:T(8,128)S(1)} fusion(bf16[1024,512]{1,0:T(8,128)(2,1)} %param.10, bf16[1,512,512]{2,1,0:T(8,128)(2,1)} %param.13), kind=kOutput, calls=%fused_computation.49 | convolution fusion | flops 536870912 | bytes 3670016 | tf_op jit(solution)/shard_map/dot_general | solution.py:35
  8.8 0.7 fusion.21
  9.5 0.3 copy-done.3
  9.8 0.3 copy-done.4
  10.2 0.8 fusion.23
  10.9 0.8 convolution_bitcast_fusion
  11.7 1.3 convolution_bitcast_fusion.2
  13.0 1.2 convolution_bitcast_fusion.1
  14.3 2.0 pad_maximum_fusion
  16.3 0.0 all-gather.2.cloned.1.call-start
  16.3 2.1 %copy.10 = bf16[1,512,512]{1,2,0:T(8,128)(2,1)} copy(bf16[1,512,512]{2,1,0:T(8,128)(2,1)} %param.13) | data formatting | bytes 1048576 | tf_op args[4]
  18.4 2.0 %copy.11 = bf16[1,512,512]{1,2,0:T(8,128)(2,1)} copy(bf16[1,512,512]{2,1,0:T(8,128)(2,1)} %param.14) | data formatting | bytes 1048576 | tf_op args[5]
  20.4 2.0 %copy.12 = bf16[1,512,512]{1,2,0:T(8,128)(2,1)} copy(bf16[1,512,512]{2,1,0:T(8,128)(2,1)} %param.15) | data formatting | bytes 1048576 | tf_op args[6]
  22.5 42.7 %reduce-scatter.3.cloned.1.call-done = f32[3,512,64]{1,2,0:T(8,128)} async-done(((f32[3,512,512]{1,2,0:T(8,128)}), f32[3,512,64]{1,2,0:T(8,128)}) %reduce-scatter.3.cloned.1.call-update) | async-done | bytes 393232 | tf_op jit(solution)/shard_map/reduce_scatter | solution.py:91
  65.2 1.2 fusion.27
  66.4 0.8 multiply_convert_fusion.11
  67.3 0.7 slice.36
  68.0 2.3 %collective-permute-start = (bf16[256,512]{1,0:T(8,128)(2,1)}, bf16[256,512]{1,0:T(8,128)(2,1)}, u32[]{:S(2)}, u32[]{:S(2)}) collective-permute-start(bf16[256,512]{1,0:T(8,128)(2,1)} %slice.36), channel_id=1, source_target_pairs={{0,4},{4,8},{8,12},{12,16},{16,20},{20,24},{24,28},{1,5},{5,9},{9,... | collective-permute-start | bytes 786440 | tf_op jit(solution)/shard_map/ppermute | solution.py:17
  70.3 1.0 slice.39
  71.3 3.8 %collective-permute-start.1 = (bf16[256,512]{1,0:T(8,128)(2,1)S(1)}, bf16[256,512]{1,0:T(8,128)(2,1)}, u32[]{:S(2)}, u32[]{:S(2)}) collective-permute-start(bf16[256,512]{1,0:T(8,128)(2,1)S(1)} %slice.39), channel_id=1, source_target_pairs={{0,4},{4,8},{8,12},{12,16},{16,20},{20,24},{24,28},{1,5},{5,9},{9,... | collective-permute-start | bytes 786440 | tf_op jit(solution)/shard_map/ppermute | solution.py:17
  75.2 2.0 fusion.37
  77.2 0.3 fusion.5
  77.5 1.6 fusion.13
  79.1 1.8 fusion.38
  80.9 0.3 fusion.4
  81.2 2.7 %fusion.10 = f32[512,512]{0,1:T(8,128)} fusion(bf16[1024,512]{1,0:T(8,128)(2,1)S(1)} %copy-done.5, bf16[256,512]{1,0:T(8,128)(2,1)} %collective-permute-done.1, f32[512,768]{0,1:T(8,128)S(1)} %get-tuple-element.11, f32[512]{0:T(512)S(1)} %fusion.4, f32[512]{0:T(512)S(1)} %get-tuple-element.10), kind=kOutput, calls=%fused_computation.36 | convolution fusion | flops 405405696 | bytes 3936256 | tf_op jit(solution)/shard_map/dot_general | solution.py:77
  83.8 10.2 %all-gather.2.cloned.1.call-done = bf16[3,512,512]{1,2,0:T(8,128)(2,1)} async-done(((bf16[3,512,64]{1,2,0:T(8,128)(2,1)}), bf16[3,512,512]{1,2,0:T(8,128)(2,1)}) %all-gather.2.cloned.1.call-update) | async-done | bytes 1572880 | tf_op jit(solution)/shard_map/all_gather | solution.py:94
  94.1 3.1 %fusion.18 = f32[512,1024]{0,1:T(8,128)} fusion(bf16[1024,512]{1,0:T(8,128)(2,1)S(1)} %copy-done.8, bf16[3,512,512]{1,2,0:T(8,128)(2,1)} %all-gather.2.cloned.1.call-done), kind=kOutput, calls=%fused_computation.48 | convolution fusion | flops 536870912 | bytes 3670016 | tf_op jit(solution)/shard_map/dot_general | solution.py:55
  97.2 5.3 %multiply_reduce_fusion = (f32[1024]{0:T(1024)S(1)}, f32[1024,512]{0,1:T(8,128)}) fusion(f32[512,512]{0,1:T(8,128)} %fusion.13, f32[512,512]{0,1:T(8,128)} %fusion.10, bf16[3,512,512]{1,2,0:T(8,128)(2,1)} %all-gather.2.cloned.1.call-done, f32[512,1024]{0,1:T(8,128)} %fusion.18, bf16[1024,512]{1,0:T(8,128)(2,1)S(1)} %copy-done.8), kind=kOutput, calls=%fused_computation.11 | convolution fusion | flops 1078983680 | bytes 8392704 | tf_op jit(solution)/shard_map/dot_general | solution.py:58
  102.5 11.7 %psum.7 = f32[1024]{0:T(1024)S(1)} all-reduce(f32[1024]{0:T(1024)S(1)} %get-tuple-element.12), channel_id=1, replica_groups=mesh['ctx'=8,'head'=4] {'head'}, use_global_device_ids=true, to_apply=%region_8.9 | all-reduce | flops 1024 | bytes 8192 | tf_op jit(solution)/shard_map/psum | solution.py:115
  114.2 6.0 %convolution_convert_fusion = bf16[1024,2048]{1,0:T(8,128)(2,1)} fusion(bf16[512,2048]{1,0:T(8,128)(2,1)S(1)} %copy-done, f32[1024,512]{0,1:T(8,128)} %get-tuple-element.13, f32[512]{0:T(512)S(1)} %convert_element_type.49, f32[1024]{0:T(1024)S(1)} %add_rsqrt_fusion), kind=kOutput, calls=%fused_computation | convolution fusion | flops 2151153664 | bytes 8394752 | tf_op jit(solution)/shard_map/dot_general | solution.py:121
  120.2 74.2 %reduce-scatter.5.cloned.1.call-done = bf16[256,2048]{1,0:T(8,128)(2,1)} async-done(((bf16[1024,2048]{1,0:T(8,128)(2,1)}), bf16[256,2048]{1,0:T(8,128)(2,1)}) %reduce-scatter.5.cloned.1.call-update) | async-done | bytes 1048592 | tf_op jit(solution)/shard_map/reduce_scatter | solution.py:120
  (36 shorter events, 0.2 us)
Async XLA Ops:
  6.5 107.6 %copy-start = (bf16[512,2048]{1,0:T(8,128)(2,1)S(1)}, bf16[512,2048]{1,0:T(8,128)(2,1)}, u32[]{:S(2)}) copy-start(bf16[512,2048]{1,0:T(8,128)(2,1)} %param.17) | copy-start | bytes 6291460
  6.5 2.2 %copy-start.1 = (bf16[1024,512]{1,0:T(8,128)(2,1)S(1)}, bf16[1024,512]{1,0:T(8,128)(2,1)}, u32[]{:S(2)}) copy-start(bf16[1024,512]{1,0:T(8,128)(2,1)} %param.10) | copy-start | bytes 3145732
  6.5 58.6 %reduce-scatter.3.cloned.1.call-start = ((), (), s32[]{:S(2)}) async-start(), calls=%async_computation.2 | async-start | bytes 3538944 | tf_op jit(solution)/shard_map/reduce_scatter | solution.py:91
  6.5 2.2 %copy-start.2 = (bf16[1,512,512]{2,1,0:T(8,128)(2,1)S(1)}, bf16[1,512,512]{2,1,0:T(8,128)(2,1)}, u32[]{:S(2)}) copy-start(bf16[1,512,512]{2,1,0:T(8,128)(2,1)} %param.15) | copy-start | bytes 1572868
  8.8 1.0 copy-start.3
  8.8 1.4 copy-start.4
  8.8 1.4 copy-start.9
  16.3 77.8 %all-gather.2.cloned.1.call-start = ((), (), s32[]{:S(2)}) async-start(), calls=%async_computation.3 | async-start | bytes 1769472 | tf_op jit(solution)/shard_map/all_gather | solution.py:94
  22.5 52.6 %copy-start.10 = (bf16[512]{0:T(512)(128)(2,1)S(1)}, bf16[512]{0:T(512)(128)(2,1)}, u32[]{:S(2)}) copy-start(bf16[512]{0:T(512)(128)(2,1)} %param.16) | copy-start | bytes 3076
  65.2 1.3 copy-start.6
  67.2 127.1 %reduce-scatter.5.cloned.1.call-start = ((), (), s32[]{:S(2)}) async-start(), calls=%async_computation.4 | async-start | bytes 5242880 | tf_op jit(solution)/shard_map/reduce_scatter | solution.py:120
  68.0 11.1 %collective-permute-start = (bf16[256,512]{1,0:T(8,128)(2,1)}, bf16[256,512]{1,0:T(8,128)(2,1)}, u32[]{:S(2)}, u32[]{:S(2)}) collective-permute-start(bf16[256,512]{1,0:T(8,128)(2,1)} %slice.36), channel_id=1, source_target_pairs={{0,4},{4,8},{8,12},{12,16},{16,20},{20,24},{24,28},{1,5},{5,9},{9,... | collective-permute-start | bytes 786440 | tf_op jit(solution)/shard_map/ppermute | solution.py:17
  71.3 9.9 %collective-permute-start.1 = (bf16[256,512]{1,0:T(8,128)(2,1)S(1)}, bf16[256,512]{1,0:T(8,128)(2,1)}, u32[]{:S(2)}, u32[]{:S(2)}) collective-permute-start(bf16[256,512]{1,0:T(8,128)(2,1)S(1)} %slice.39), channel_id=1, source_target_pairs={{0,4},{4,8},{8,12},{12,16},{16,20},{20,24},{24,28},{1,5},{5,9},{9,... | collective-permute-start | bytes 786440 | tf_op jit(solution)/shard_map/ppermute | solution.py:17
  75.2 2.3 %copy-start.5 = (bf16[1024,512]{1,0:T(8,128)(2,1)S(1)}, bf16[1024,512]{1,0:T(8,128)(2,1)}, u32[]{:S(2)}) copy-start(bf16[1024,512]{1,0:T(8,128)(2,1)} %param.11) | copy-start | bytes 3145732
  77.4 1.6 copy-start.7
  81.1 12.9 %copy-start.8 = (bf16[1024,512]{1,0:T(8,128)(2,1)S(1)}, bf16[1024,512]{1,0:T(8,128)(2,1)}, u32[]{:S(2)}) copy-start(bf16[1024,512]{1,0:T(8,128)(2,1)} %param.9) | copy-start | bytes 3145732
Sparse Core Ops, SparseCore 0:
  16.4 48.7 reduce-scatter.2
  67.4 26.6 all-gather.1
  120.3 74.0 reduce-scatter.4
where the time goes:
time: 201 us
  waiting for transfers between devices  127 us (63%)
  matrix products  29.4 us (15%)
  between operations  13.3 us (7%)
  blocking collectives  11.7 us (6%)
  local copies, waits for them, and re-layouts  8.54 us (4%)
  starting transfers between devices  6.21 us (3%)
  other arithmetic  4.6 us (2%)
    reduce_scatter x1, waiting for transfers between devices, body(): lax.psum_scatter(jnp.dot(normed, out_weight, preferred_element_type=jnp.f...  74.2 us
    reduce_scatter x1, waiting for transfers between devices, body(): owned_sum = lax.psum_scatter(pushes, 'ctx', scatter_dimension=2, tiled=True)  42.7 us
    psum x1, blocking collectives, body(): squares = lax.psum(jnp.sum(combined * combined, axis=1), 'head')  11.7 us
    all_gather x1, waiting for transfers between devices, body(): lax.all_gather(renorm(own_weight, owned_sum, 1), 'ctx', axis=2, tiled=True)  10.2 us
    unnamed x25, local copies, waits for them, and re-layouts  6.86 us
    ppermute x2, starting transfers between devices, from_behind(): return lax.ppermute(value, axis, pairs)  6.12 us
    dot_general x1, matrix products, body(): jnp.dot(normed, out_weight, preferred_element_type=jnp.float32)  5.99 us
    dot_general x1, matrix products, apply_fast(): return jnp.dot(mixed_act, down_weight, preferred_element_type=jnp.float32)  5.28 us
  transfers between devices with their start and end apart: 5, of which 3 were waited for; matrix products, arithmetic and copies ran while one was open for 8% of the time, Pallas kernels for 0%

commit v1 on v0

v1 whole, which is shorter than its diff:
```python
import functools
import math

import jax
import jax.numpy as jnp
from jax import lax
from jax.experimental import pallas as pl
from jax.experimental.pallas import tpu as pltpu
from jax.sharding import PartitionSpec as P


WINDOW = 256
EPSILON = 1e-06

VMEM = pl.BlockSpec(memory_space=pltpu.VMEM)
SMEM = pl.BlockSpec(memory_space=pltpu.SMEM)
HBM = pl.BlockSpec(memory_space=pltpu.HBM)


def near_core(*arrays):
    return [pltpu.with_memory_space_constraint(a, pltpu.VMEM) for a in arrays]


def far_core(*arrays):
    return [pltpu.with_memory_space_constraint(a, pltpu.HBM) for a in arrays]


def grant(mib):
    return pltpu.CompilerParams(vmem_limit_bytes=mib << 20)


def swap(value, axis, mask):
    return lax.ppermute(value, axis, [(i, i ^ mask) for i in range(lax.axis_size(axis))])


def dot(left, right, left_dim=1, right_dim=0):
    return lax.dot_general(
        left, right, (((left_dim,), (right_dim,)), ((), ())), preferred_element_type=jnp.float32
    )


def push_kernel(core_ref, k_hbm, v_hbm, r_hbm, w1_hbm, w2_hbm, w3_hbm, give_ref, keep_ref, tail_hbm,
                k_ref, v_ref, r_ref, w1_ref, w2_ref, w3_ref, act_ref, g1_ref, g3_ref, sc_ref, sem):
    rows, width = k_ref.shape
    steps = 4
    block = rows // steps
    half = width // 2
    sources = [(w1_hbm, w1_ref), (w3_hbm, w3_ref), (w2_hbm, w2_ref)]
    copies = [pltpu.make_async_copy(src.at[0], dst, sem.at[j]) for j, (src, dst) in enumerate(sources)]
    copies.append(pltpu.make_async_copy(r_hbm, r_ref, sem.at[3]))
    streams = []
    for i in range(steps):
        at = pl.ds(i * block, block)
        streams.append([
            pltpu.make_async_copy(src.at[at, :], dst.at[at, :], sem.at[4 + 2 * i + j])
            for j, (src, dst) in enumerate([(k_hbm, k_ref), (v_hbm, v_ref)])
        ])
    last = pl.ds(rows - WINDOW, WINDOW)
    tails = [
        pltpu.make_async_copy(src.at[last, :], tail_hbm.at[pl.ds(j * WINDOW, WINDOW), :], sem.at[12 + j])
        for j, src in enumerate((k_hbm, v_hbm))
    ]
    streams[0][0].start()
    for copy in copies:
        copy.start()
    for i in range(steps):
        for copy in streams[i][1 if i == 0 else 0:]:
            copy.start()
    for copy in tails:
        copy.start()
    for i in range(steps):
        at = slice(i * block, (i + 1) * block)
        if i == 0:
            streams[0][0].wait()
            copies[0].wait()
            copies[1].wait()
        else:
            streams[i][0].wait()
        k = k_ref[at, :]
        gate = dot(k, w1_ref[...])
        up = dot(k, w3_ref[...])
        if i == 0:
            copies[2].wait()
            copies[3].wait()
        streams[i][1].wait()
        rate = jnp.transpose(jnp.broadcast_to(r_ref[:, at], (128, block)))
        rate = jnp.concatenate([rate] * (width // 128), axis=1)
        scaled = (v_ref[at, :].astype(jnp.float32) * rate).astype(jnp.bfloat16)
        back = dot(scaled, w2_ref[...], 1, 1)
        s = jax.nn.sigmoid(gate)
        gs = gate * s
        act_ref[at, :] = (gs * up).astype(jnp.bfloat16)
        sc_ref[at, :] = scaled
        g1_ref[at, :] = (back * up * (s + gs * (1.0 - s))).astype(jnp.bfloat16)
        g3_ref[at, :] = (back * gs).astype(jnp.bfloat16)
    core = core_ref[0]
    theirs = pl.ds(pl.multiple_of((1 - core) * half, half), half)
    mine = pl.ds(pl.multiple_of(core * half, half), half)
    for j, (left, right) in enumerate([(k_ref, g1_ref), (act_ref, sc_ref), (k_ref, g3_ref)]):
        left = left[...]
        give_ref[j] = dot(left, right[:, theirs], 0, 0).astype(jnp.bfloat16)
        keep_ref[j] = dot(left, right[:, mine], 0, 0)
    for copy in tails:
        copy.wait()


def pushes(core, keys, values, rates, w1, w2, w3):
    rows, width = keys.shape
    half = width // 2
    wide = pltpu.VMEM((rows, width), jnp.bfloat16)
    weight = pltpu.VMEM((width, width), jnp.bfloat16)
    return pl.pallas_call(
        push_kernel,
        out_shape=(
            pltpu.VMEM((3, width, half), jnp.bfloat16),
            pltpu.VMEM((3, width, half), jnp.float32),
            jax.ShapeDtypeStruct((2 * WINDOW, width), jnp.bfloat16),
        ),
        compiler_params=grant(24),
        in_specs=[SMEM] + [HBM] * 6,
        out_specs=(VMEM, VMEM, HBM),
        scratch_shapes=[wide, wide, pltpu.VMEM((1, rows), jnp.float32), weight, weight, weight,
                        wide, wide, wide, wide, pltpu.SemaphoreType.DMA((14,))],
        name="pushes",
    )(core, *far_core(keys, values, rates.reshape(1, rows), w1, w2, w3))


def first_add_kernel(keep_ref, got_ref, sum_ref, a_ref, b_ref):
    quarter = a_ref.shape[2]
    total = keep_ref[...] + got_ref[...].astype(jnp.float32)
    sum_ref[...] = total
    a_ref[...] = total[:, :, :quarter].astype(jnp.bfloat16)
    b_ref[...] = total[:, :, quarter:].astype(jnp.bfloat16)


def later_add_kernel(keep_ref, got_a_ref, got_b_ref, sum_ref, a_ref, b_ref):
    quarter = a_ref.shape[2]
    first = keep_ref[:, :, :quarter] + got_a_ref[...].astype(jnp.float32)
    second = keep_ref[:, :, quarter:] + got_b_ref[...].astype(jnp.float32)
    sum_ref[:, :, :quarter] = first
    sum_ref[:, :, quarter:] = second
    a_ref[...] = first.astype(jnp.bfloat16)
    b_ref[...] = second.astype(jnp.bfloat16)


def add(keep, *got):
    stream = pltpu.VMEM(keep.shape[:2] + (keep.shape[2] // 2,), jnp.bfloat16)
    return pl.pallas_call(
        first_add_kernel if len(got) == 1 else later_add_kernel,
        out_shape=(pltpu.VMEM(keep.shape, jnp.float32), stream, stream),
        compiler_params=grant(16),
        in_specs=[VMEM] * (1 + len(got)),
        out_specs=(VMEM,) * 3,
    )(*near_core(keep, *got))


def renorm_kernel(core_ref, keep_ref, got_a_ref, got_b_ref, w1_ref, w2_ref, w3_ref, out_ref):
    quarter = got_a_ref.shape[2]
    core = core_ref[0]
    for j, w_ref in enumerate((w1_ref, w2_ref, w3_ref)):
        for part, got_ref in enumerate((got_a_ref, got_b_ref)):
            at = slice(part * quarter, (part + 1) * quarter)
            start = pl.multiple_of(core * 2 * quarter + part * quarter, quarter)
            old = w_ref[0, :, pl.ds(start, quarter)].astype(jnp.float32)
            new = old + (keep_ref[j, :, at] + got_ref[j].astype(jnp.float32))
            old_norm = jnp.sqrt(jnp.mean(old * old, axis=0, keepdims=True) + EPSILON)
            new_norm = jnp.sqrt(jnp.mean(new * new, axis=0, keepdims=True) + EPSILON)
            out_ref[j, :, at] = (new * (old_norm / new_norm)).astype(jnp.bfloat16)


def renorm(core, keep, got_a, got_b, w1, w2, w3):
    return pl.pallas_call(
        renorm_kernel,
        out_shape=pltpu.VMEM(keep.shape, jnp.bfloat16),
        compiler_params=grant(16),
        in_specs=[SMEM] + [VMEM] * 6,
        out_specs=VMEM,
        name="renorm",
    )(core, *near_core(keep, got_a, got_b), w1, w2, w3)


def window_kernel(me_ref, q_hbm, k_hbm, v_hbm, tail_ref, out_ref, q_ref, k_ref, v_ref, sem):
    rows, width = q_ref.shape
    scale = 1.0 / math.sqrt(width)
    query = lax.broadcasted_iota(jnp.int32, (WINDOW, 2 * WINDOW), 0)
    key = lax.broadcasted_iota(jnp.int32, (WINDOW, 2 * WINDOW), 1)
    allowed = (key > query) & (key <= query + WINDOW)
    allowed_first = allowed & ((key >= WINDOW) | (me_ref[0] > 0))
    count = rows // WINDOW
    loads = [[
        pltpu.make_async_copy(tail_ref.at[pl.ds(j * WINDOW, WINDOW), :], dst.at[pl.ds(0, WINDOW), :], sem.at[j])
        for j, dst in enumerate((k_ref, v_ref))
    ]]
    for i in range(count):
        at, after = pl.ds(i * WINDOW, WINDOW), pl.ds((i + 1) * WINDOW, WINDOW)
        loads.append([
            pltpu.make_async_copy(q_hbm.at[at, :], q_ref.at[at, :], sem.at[3 * i + 2]),
            pltpu.make_async_copy(k_hbm.at[at, :], k_ref.at[after, :], sem.at[3 * i + 3]),
            pltpu.make_async_copy(v_hbm.at[at, :], v_ref.at[after, :], sem.at[3 * i + 4]),
        ])
    for group in loads:
        for load in group:
            load.start()
    for load in loads[0]:
        load.wait()
    for i in range(count):
        for load in loads[i + 1]:
            load.wait()
        at = slice(i * WINDOW, (i + 1) * WINDOW)
        seen = slice(i * WINDOW, (i + 2) * WINDOW)
        scores = dot(q_ref[at, :], k_ref[seen, :], 1, 1) * scale
        scores = jnp.where(allowed_first if i == 0 else allowed, scores, -jnp.inf)
        peak = jnp.max(scores, axis=1, keepdims=True)
        exponent = jnp.exp(scores - peak)
        weights = exponent / jnp.sum(exponent, axis=1, keepdims=True)
        out_ref[at, :] = dot(weights.astype(jnp.bfloat16), v_ref[seen, :])


def window(me, queries, keys, values, tail):
    rows, width = queries.shape
    return pl.pallas_call(
        window_kernel,
        out_shape=pltpu.VMEM(queries.shape, jnp.float32),
        compiler_params=grant(24),
        in_specs=[SMEM] + [HBM] * 3 + [VMEM],
        out_specs=VMEM,
        scratch_shapes=[pltpu.VMEM((rows, width), jnp.bfloat16)]
        + [pltpu.VMEM((rows + WINDOW, width), jnp.bfloat16)] * 2
        + [pltpu.SemaphoreType.DMA((2 + 3 * (rows // WINDOW),))],
        name="window",
    )(me, *far_core(queries, keys, values), *near_core(tail))


def apply_kernel(slot, core_ref, head_ref, q_ref, seen_ref, mine_ref, other_ref, out_ref):
    rows = out_ref.shape[0]
    half = mine_ref.shape[2]
    core = core_ref[0]
    own = pl.ds(pl.multiple_of(core * half, half), half)
    rest = pl.ds(pl.multiple_of((1 - core) * half, half), half)
    here = pl.ds(pl.multiple_of((head_ref[0] ^ slot) * rows, rows), rows)
    q = q_ref[here, :]

    def mixed(ref):
        gate = dot(q, ref[0])
        up = dot(q, ref[2])
        return (gate * jax.nn.sigmoid(gate) * up).astype(jnp.bfloat16)

    first, second = mixed(mine_ref), mixed(other_ref)
    for ref, at in ((mine_ref, own), (other_ref, rest)):
        fast = dot(first, ref[1, own, :]) + dot(second, ref[1, rest, :])
        out_ref[:, at] = (fast + seen_ref[here, at]).astype(jnp.bfloat16)


def apply_fast(slot, core, head, queries, seen, mine, other, rows):
    return pl.pallas_call(
        functools.partial(apply_kernel, slot),
        out_shape=pltpu.VMEM((rows, queries.shape[1]), jnp.bfloat16),
        compiler_params=grant(16),
        in_specs=[SMEM] * 2 + [VMEM] * 4,
        out_specs=VMEM,
        name="apply",
    )(core, head, *near_core(queries, seen, mine, other))


def own_project_kernel(x_ref, gain_ref, w_ref, out_ref, squares_ref):
    wide = x_ref[...].astype(jnp.float32)
    squares_ref[...] = jnp.sum(wide * wide, axis=1, keepdims=True)
    x = (wide * gain_ref[...].astype(jnp.float32)).astype(jnp.bfloat16)
    out_ref[...] = dot(x, w_ref[...])


def own_project(x, gain, weight):
    return pl.pallas_call(
        own_project_kernel,
        out_shape=(
            pltpu.VMEM((x.shape[0], weight.shape[1]), jnp.float32),
            pltpu.VMEM((x.shape[0], 1), jnp.float32),
        ),
        compiler_params=grant(16),
        in_specs=[VMEM] * 3,
        out_specs=(VMEM, VMEM),
        name="own_project",
    )(*near_core(x), gain, weight)


def project_kernel(part_ref, *refs):
    *xs, base_ref, squares_ref, near, near_c, far, far_c, out_ref, w_ref = refs
    rows = near.shape[1]
    heads = len(xs) + 1
    squares = squares_ref[...]
    for k in range(heads - 1):
        for j, src in enumerate((near, near_c, far, far_c)):
            place = pl.multiple_of((part_ref[0] ^ j) * rows, rows)
            w_ref[k, pl.ds(place, rows), :] = src[k]
        wide = xs[k][...].astype(jnp.float32)
        squares = squares + jnp.sum(wide * wide, axis=1, keepdims=True)
    scale = lax.rsqrt(squares / (heads * 4 * rows) + EPSILON)
    block = 512
    for start in range(0, out_ref.shape[1], block):
        at = slice(start, start + block)
        total = base_ref[:, at]
        for k in range(heads - 1):
            total = total + dot(xs[k][...], w_ref[k, :, at])
        out_ref[:, at] = (total * scale).astype(out_ref.dtype)


def project(part, xs, base, squares, pieces):
    rows, columns = base.shape
    count, piece_rows, _ = pieces[0].shape
    return pl.pallas_call(
        project_kernel,
        out_shape=jax.ShapeDtypeStruct((rows, columns), jnp.bfloat16),
        in_specs=[SMEM] + [VMEM] * (len(xs) + 6),
        out_specs=VMEM,
        scratch_shapes=[pltpu.VMEM((count, 4 * piece_rows, columns), jnp.bfloat16)],
        compiler_params=grant(16),
        name="project",
    )(part, *near_core(*xs, base, squares, *pieces))


def step(queries, keys, values, rates, fast_w1, fast_w2, fast_w3, norm_gain, out_weight):
    tok_rows, width = queries.shape
    ctx_count = lax.axis_size("ctx")
    heads = lax.axis_size("head")
    me = lax.axis_index("ctx").astype(jnp.int32)
    head = lax.axis_index("head").astype(jnp.int32)
    bits = ctx_count.bit_length() - 1
    assert ctx_count == 1 << bits and bits >= 3
    core = me & 1
    parity = ((me >> 1) ^ (me >> 2)) & 1
    part = 2 * parity + core
    core1 = core.reshape(1)

    give, keep, tail = pushes(core1, keys, values, rates, fast_w1, fast_w2, fast_w3)
    got = [swap(give, "ctx", 1)]
    masks = [1 << b for b in range(1, bits)]
    for forward, backward in zip(masks, masks[::-1]):
        keep, first, second = add(keep, *got)
        got = []
        got.append(swap(first, "ctx", forward))
        got.append(swap(second, "ctx", backward))
    mine = renorm(core1, keep, *got, fast_w1, fast_w2, fast_w3)
    other = swap(mine, "ctx", 1)

    tail = lax.ppermute(tail, "ctx", [(i, i + 1) for i in range(ctx_count - 1)])
    part_rows = width // 4
    piece = lax.dynamic_slice_in_dim(out_weight, part * part_rows, part_rows, 0)
    gain = lax.dynamic_slice_in_dim(norm_gain, part * part_rows, part_rows, 0)
    piece = (piece.astype(jnp.float32) * gain.astype(jnp.float32)[:, None]).astype(jnp.bfloat16)
    near = []
    for k in range(1, heads):
        near.append(swap(piece, "head", k))
    near = jnp.stack(near)
    far = lax.ppermute(near, "ctx", [(i, i ^ (4 if i & 1 else 2)) for i in range(ctx_count)])
    near_c = swap(near, "ctx", 1)
    far_c = swap(far, "ctx", 1)

    seen = window(me.reshape(1), queries, keys, values, tail)

    rows = tok_rows // heads
    blocks = [None] * heads
    for k in list(range(heads - 1, 0, -1)) + [0]:
        combined = apply_fast(k, core1, head.reshape(1), queries, seen, mine, other, rows)
        blocks[k] = swap(combined, "head", k) if k else combined
    base, squares = own_project(blocks[0], norm_gain.reshape(1, width), out_weight)
    return project(part.reshape(1), blocks[1:], base, squares, [near, near_c, far, far_c])


def solution(mesh):
    placed = (
        P("ctx", "head"),
        P("ctx", "head"),
        P("ctx", "head"),
        P("ctx", "head"),
        P("head", None, None),
        P("head", None, None),
        P("head", None, None),
        P("head"),
        P("head", None),
    )
    return jax.shard_map(
        step, mesh=mesh, in_specs=placed, out_specs=P(("ctx", "head"), None), check_vma=False
    )
```

time: 201 us -> 138 us (0.69)
  the two profiles are of different devices: /device:TPU:0 before, /device:TPU:2 now
where the time goes in v1:
time: 138 us; the launch traced here: 137 us
  waiting for transfers between devices  75.5 us (55%)
  Pallas kernels  32.8 us (24%)
  starting transfers between devices  25.7 us (19%)
  other arithmetic  2.12 us (2%)
    ppermute x14, waiting for transfers between devices, swap(): lax.ppermute(value, axis, [(i, i ^ mask) for i in range(lax.axis_size(axi...  67.3 us
    ppermute x14, starting transfers between devices, swap(): lax.ppermute(value, axis, [(i, i ^ mask) for i in range(lax.axis_size(axi...  22.5 us
    pallas_call x1, Pallas kernels, pushes(): pl.pallas_call(push_kernel, out_shape=(pltpu.VMEM((3, width, half), jnp.b...  17.1 us
    ppermute x1, waiting for transfers between devices, step(): tail = lax.ppermute(tail, 'ctx', [(i, i + 1) for i in range(ctx_count - 1)])  8.23 us
    pallas_call x1, Pallas kernels, project(): pl.pallas_call(project_kernel, out_shape=jax.ShapeDtypeStruct((rows, colu...  5.72 us
    pallas_call x1, Pallas kernels, window(): pl.pallas_call(window_kernel, out_shape=pltpu.VMEM(queries.shape, jnp.flo...  5.49 us
  transfers between devices with their start and end apart: 16, of which 9 were waited for; matrix products, arithmetic and copies ran while one was open for 0% of the time, Pallas kernels for 20%

profile of v1, /device:TPU:2, one launch (start us, length us, event | category | flops | bytes accessed | tf_op | source)
XLA Modules:
  0.0 137.3 jit_solution(17542139504135109866)
XLA Ops:
  0.0 0.8 dynamic-slice_convert_fusion
  0.8 1.2 multiply_convert_fusion
  1.9 1.6 %collective-permute-start.10 = (bf16[128,2048]{1,0:T(8,128)(2,1)S(1)}, bf16[128,2048]{1,0:T(8,128)(2,1)S(1)}, u32[]{:S(2)}, u32[]{:S(2)}) collective-permute-start(bf16[128,2048]{1,0:T(8,128)(2,1)S(1)} %multiply_convert_fusion), channel_id=1, source_target_pairs={{0,1},{1,0},{2,3},{3,2},{4,5},{5,4},{6,7},{7,6},{8,9},{9,8},{10,11... | collective-permute-start | bytes 1572872 | tf_op jit(solution)/shard_map/ppermute | solution.py:33
  3.6 2.6 %collective-permute-start.11 = (bf16[128,2048]{1,0:T(8,128)(2,1)S(1)}, bf16[128,2048]{1,0:T(8,128)(2,1)S(1)}, u32[]{:S(2)}, u32[]{:S(2)}) collective-permute-start(bf16[128,2048]{1,0:T(8,128)(2,1)S(1)} %multiply_convert_fusion), channel_id=1, source_target_pairs={{0,2},{1,3},{2,0},{3,1},{4,6},{5,7},{6,4},{7,5},{8,10},{9,11},{10,... | collective-permute-start | bytes 1572872 | tf_op jit(solution)/shard_map/ppermute | solution.py:33
  6.4 19.8 %collective-permute-done.10 = bf16[128,2048]{1,0:T(8,128)(2,1)S(1)} collective-permute-done((bf16[128,2048]{1,0:T(8,128)(2,1)S(1)}, bf16[128,2048]{1,0:T(8,128)(2,1)S(1)}, u32[]{:S(2)}, u32[]{:S(2)}) %collective-permute-start.10) | collective-permute-done | bytes 524320 | tf_op jit(solution)/shard_map/ppermute | solution.py:33
  26.2 15.6 %collective-permute-done.11 = bf16[128,2048]{1,0:T(8,128)(2,1)S(1)} collective-permute-done((bf16[128,2048]{1,0:T(8,128)(2,1)S(1)}, bf16[128,2048]{1,0:T(8,128)(2,1)S(1)}, u32[]{:S(2)}, u32[]{:S(2)}) %collective-permute-start.11) | collective-permute-done | bytes 524320 | tf_op jit(solution)/shard_map/ppermute | solution.py:33
  41.9 0.6 collective-permute-start.14
  42.5 17.1 %pushes.1 = (bf16[3,512,256]{2,1,0:T(8,128)(2,1)S(1)}, f32[3,512,256]{2,1,0:T(8,128)S(1)}, bf16[512,512]{1,0:T(8,128)(2,1)}) custom-call(s32[1]{0:T(128)} %bitcast.1.core_ref, bf16[1024,512]{1,0:T(8,128)(2,1)} %k_hbm.3, bf16[1024,512]{1,0:T(8,128)(2,1)} %v_hbm.3, f32[1,1024]{1,0:T(1,128)} %bitcast.11, bf16[1,512,512]{2,1,0:T(8,128)(2,1)} %w1_ref.1, ...), custom_call_target="tpu_custom_call" | custom-call | tf_op jit(solution)/shard_map/pushes/pallas_call | solution.py:112
  59.7 2.3 %collective-permute-done.1.got_ref = bf16[3,512,256]{2,1,0:T(8,128)(2,1)S(1)} collective-permute-done((bf16[3,512,256]{2,1,0:T(8,128)(2,1)S(1)}, bf16[3,512,256]{2,1,0:T(8,128)(2,1)S(1)}, u32[]{:S(2)}, u32[]{:S(2)}) %collective-permute-start.1) | collective-permute-done | bytes 786464 | tf_op jit(solution)/shard_map/ppermute | solution.py:33
  62.3 1.6 %collective-permute-start.2 = (bf16[3,512,128]{2,1,0:T(8,128)(2,1)S(1)}, bf16[3,512,128]{2,1,0:T(8,128)(2,1)S(1)}, u32[]{:S(2)}, u32[]{:S(2)}) collective-permute-start(bf16[3,512,128]{2,1,0:T(8,128)(2,1)S(1)} %get-tuple-element.20), channel_id=1, source_target_pairs={{0,8},{4,12},{8,0},{12,4},{16,24},{20,28},{24,16},{28,20},{1,9},{5... | collective-permute-start | bytes 1179656 | tf_op jit(solution)/shard_map/ppermute | solution.py:33
  63.9 1.5 %collective-permute-start.3 = (bf16[3,512,128]{2,1,0:T(8,128)(2,1)S(1)}, bf16[3,512,128]{2,1,0:T(8,128)(2,1)S(1)}, u32[]{:S(2)}, u32[]{:S(2)}) collective-permute-start(bf16[3,512,128]{2,1,0:T(8,128)(2,1)S(1)} %get-tuple-element.21), channel_id=1, source_target_pairs={{0,16},{4,20},{8,24},{12,28},{16,0},{20,4},{24,8},{28,12},{1,17},{... | collective-permute-start | bytes 1179656 | tf_op jit(solution)/shard_map/ppermute | solution.py:33
  65.4 0.5 collective-permute-start.15
  65.9 7.6 %collective-permute-done.2.got_a_ref = bf16[3,512,128]{2,1,0:T(8,128)(2,1)S(1)} collective-permute-done((bf16[3,512,128]{2,1,0:T(8,128)(2,1)S(1)}, bf16[3,512,128]{2,1,0:T(8,128)(2,1)S(1)}, u32[]{:S(2)}, u32[]{:S(2)}) %collective-permute-start.2) | collective-permute-done | bytes 393248 | tf_op jit(solution)/shard_map/ppermute | solution.py:33
  73.5 1.2 collective-permute-done.3.got_b_ref
  75.0 1.6 %collective-permute-start.4 = (bf16[3,512,128]{2,1,0:T(8,128)(2,1)S(1)}, bf16[3,512,128]{2,1,0:T(8,128)(2,1)S(1)}, u32[]{:S(2)}, u32[]{:S(2)}) collective-permute-start(bf16[3,512,128]{2,1,0:T(8,128)(2,1)S(1)} %get-tuple-element.23), channel_id=1, source_target_pairs={{0,16},{4,20},{8,24},{12,28},{16,0},{20,4},{24,8},{28,12},{1,17},{... | collective-permute-start | bytes 1179656 | tf_op jit(solution)/shard_map/ppermute | solution.py:33
  76.6 0.5 collective-permute-start.5
  77.1 8.0 %collective-permute-done.4.got_a_ref = bf16[3,512,128]{2,1,0:T(8,128)(2,1)S(1)} collective-permute-done((bf16[3,512,128]{2,1,0:T(8,128)(2,1)S(1)}, bf16[3,512,128]{2,1,0:T(8,128)(2,1)S(1)}, u32[]{:S(2)}, u32[]{:S(2)}) %collective-permute-start.4) | collective-permute-done | bytes 393248 | tf_op jit(solution)/shard_map/ppermute | solution.py:33
  85.1 1.2 collective-permute-done.5.got_b_ref
  86.3 0.6 renorm.1.mine_ref
  87.0 2.6 %collective-permute-start = (bf16[512,512]{1,0:T(8,128)(2,1)}, bf16[512,512]{1,0:T(8,128)(2,1)}, u32[]{:S(2)}, u32[]{:S(2)}) collective-permute-start(bf16[512,512]{1,0:T(8,128)(2,1)} %get-tuple-element.16), channel_id=1, source_target_pairs={{0,4},{4,8},{8,12},{12,16},{16,20},{20,24},{24,28},{1,5},{5,9},{9,... | collective-permute-start | bytes 1572872 | tf_op jit(solution)/shard_map/ppermute | solution.py:345
  89.6 8.2 %collective-permute-done.tail_ref = bf16[512,512]{1,0:T(8,128)(2,1)} collective-permute-done((bf16[512,512]{1,0:T(8,128)(2,1)}, bf16[512,512]{1,0:T(8,128)(2,1)}, u32[]{:S(2)}, u32[]{:S(2)}) %collective-permute-start) | collective-permute-done | bytes 524320 | tf_op jit(solution)/shard_map/ppermute | solution.py:345
  97.8 5.5 %window.1.seen_ref = f32[1024,512]{1,0:T(8,128)S(1)} custom-call(s32[1]{0:T(128)} %bitcast.3.me_ref, bf16[1024,512]{1,0:T(8,128)(2,1)} %q_ref.7, bf16[1024,512]{1,0:T(8,128)(2,1)} %k_hbm.3, bf16[1024,512]{1,0:T(8,128)(2,1)} %v_hbm.3, bf16[512,512]{1,0:T(8,128)(2,1)} %collective-permute-done.tail_ref), custom_call_target="tpu_custom_call" | custom-call | tf_op jit(solution)/shard_map/window/pallas_call | solution.py:221
  103.4 0.7 apply.6
  104.0 2.5 %collective-permute-start.9 = (bf16[256,512]{1,0:T(8,128)(2,1)S(1)}, bf16[256,512]{1,0:T(8,128)(2,1)S(1)}, u32[]{:S(2)}, u32[]{:S(2)}) collective-permute-start(bf16[256,512]{1,0:T(8,128)(2,1)S(1)} %apply.6), channel_id=1, source_target_pairs={{0,3},{1,2},{2,1},{3,0},{4,7},{5,6},{6,5},{7,4},{8,11},{9,10},{10,... | collective-permute-start | bytes 786440 | tf_op jit(solution)/shard_map/ppermute | solution.py:33
  106.6 0.7 apply.5
  107.3 9.5 %collective-permute-start.8 = (bf16[256,512]{1,0:T(8,128)(2,1)S(1)}, bf16[256,512]{1,0:T(8,128)(2,1)S(1)}, u32[]{:S(2)}, u32[]{:S(2)}) collective-permute-start(bf16[256,512]{1,0:T(8,128)(2,1)S(1)} %apply.5), channel_id=1, source_target_pairs={{0,2},{1,3},{2,0},{3,1},{4,6},{5,7},{6,4},{7,5},{8,10},{9,11},{10,... | collective-permute-start | bytes 786440 | tf_op jit(solution)/shard_map/ppermute | solution.py:33
  116.7 0.7 apply.4
  117.6 0.7 apply.7.x_ref
  118.3 0.9 copy-done.1
  119.2 0.7 own_project.1
  120.0 11.6 %collective-permute-done.8.refs_1_ = bf16[256,512]{1,0:T(8,128)(2,1)S(1)} collective-permute-done((bf16[256,512]{1,0:T(8,128)(2,1)S(1)}, bf16[256,512]{1,0:T(8,128)(2,1)S(1)}, u32[]{:S(2)}, u32[]{:S(2)}) %collective-permute-start.8) | collective-permute-done | bytes 262176 | tf_op jit(solution)/shard_map/ppermute | solution.py:33
  131.6 5.7 %project.1 = bf16[256,2048]{1,0:T(8,128)(2,1)} custom-call(s32[1]{0:T(128)} %bitcast.part_ref, bf16[256,512]{1,0:T(8,128)(2,1)S(1)} %collective-permute-done.7.refs_0_, bf16[256,512]{1,0:T(8,128)(2,1)S(1)} %collective-permute-done.8.refs_1_, bf16[256,512]{1,0:T(8,128)(2,1)S(1)} %collective-permute-done.9.refs_2_, f32[256,2048]{1,0:T(8,128)S(1)} %get-tuple-element.25.refs_3_, ...), custom_call_target="tpu_custom_call" | custom-call | tf_op jit(solution)/shard_map/project/pallas_call | solution.py:310
  (27 shorter events, 1.3 us)
Async XLA Ops:
  1.9 24.2 %collective-permute-start.10 = (bf16[128,2048]{1,0:T(8,128)(2,1)S(1)}, bf16[128,2048]{1,0:T(8,128)(2,1)S(1)}, u32[]{:S(2)}, u32[]{:S(2)}) collective-permute-start(bf16[128,2048]{1,0:T(8,128)(2,1)S(1)} %multiply_convert_fusion), channel_id=1, source_target_pairs={{0,1},{1,0},{2,3},{3,2},{4,5},{5,4},{6,7},{7,6},{8,9},{9,8},{10,11... | collective-permute-start | bytes 1572872 | tf_op jit(solution)/shard_map/ppermute | solution.py:33
  3.6 38.2 %collective-permute-start.11 = (bf16[128,2048]{1,0:T(8,128)(2,1)S(1)}, bf16[128,2048]{1,0:T(8,128)(2,1)S(1)}, u32[]{:S(2)}, u32[]{:S(2)}) collective-permute-start(bf16[128,2048]{1,0:T(8,128)(2,1)S(1)} %multiply_convert_fusion), channel_id=1, source_target_pairs={{0,2},{1,3},{2,0},{3,1},{4,6},{5,7},{6,4},{7,5},{8,10},{9,11},{10,... | collective-permute-start | bytes 1572872 | tf_op jit(solution)/shard_map/ppermute | solution.py:33
  6.2 35.6 %collective-permute-start.12 = (bf16[128,2048]{1,0:T(8,128)(2,1)S(1)}, bf16[128,2048]{1,0:T(8,128)(2,1)S(1)}, u32[]{:S(2)}, u32[]{:S(2)}) collective-permute-start(bf16[128,2048]{1,0:T(8,128)(2,1)S(1)} %multiply_convert_fusion), channel_id=1, source_target_pairs={{0,3},{1,2},{2,1},{3,0},{4,7},{5,6},{6,5},{7,4},{8,11},{9,10},{10,... | collective-permute-start | bytes 1572872 | tf_op jit(solution)/shard_map/ppermute | solution.py:33
  41.9 23.5 %collective-permute-start.14 = (bf16[3,128,2048]{2,1,0:T(8,128)(2,1)S(1)}, bf16[3,128,2048]{2,1,0:T(8,128)(2,1)}, u32[]{:S(2)}, u32[]{:S(2)}) collective-permute-start(bf16[3,128,2048]{2,1,0:T(8,128)(2,1)S(1)} %pad_maximum_fusion.refs_5_), channel_id=1, source_target_pairs={{0,8},{4,20},{8,0},{12,28},{16,24},{20,4},{24,16},{28,12},{1,9},{5... | collective-permute-start | bytes 4718600 | tf_op jit(solution)/shard_map/ppermute | solution.py:354
  59.7 2.4 %collective-permute-start.1 = (bf16[3,512,256]{2,1,0:T(8,128)(2,1)S(1)}, bf16[3,512,256]{2,1,0:T(8,128)(2,1)S(1)}, u32[]{:S(2)}, u32[]{:S(2)}) collective-permute-start(bf16[3,512,256]{2,1,0:T(8,128)(2,1)S(1)} %get-tuple-element.18), channel_id=1, source_target_pairs={{0,4},{4,0},{8,12},{12,8},{16,20},{20,16},{24,28},{28,24},{1,5},{5... | collective-permute-start | bytes 2359304 | tf_op jit(solution)/shard_map/ppermute | solution.py:33
  62.3 24.0 %copy-start.2 = (bf16[1,512,512]{2,1,0:T(8,128)(2,1)S(1)}, bf16[1,512,512]{2,1,0:T(8,128)(2,1)}, u32[]{:S(2)}) copy-start(bf16[1,512,512]{2,1,0:T(8,128)(2,1)} %w1_ref.1) | copy-start | bytes 1572868
  62.3 24.0 %copy-start.3 = (bf16[1,512,512]{2,1,0:T(8,128)(2,1)S(1)}, bf16[1,512,512]{2,1,0:T(8,128)(2,1)}, u32[]{:S(2)}) copy-start(bf16[1,512,512]{2,1,0:T(8,128)(2,1)} %w2_ref.1) | copy-start | bytes 1572868
  62.3 24.0 %copy-start.4 = (bf16[1,512,512]{2,1,0:T(8,128)(2,1)S(1)}, bf16[1,512,512]{2,1,0:T(8,128)(2,1)}, u32[]{:S(2)}) copy-start(bf16[1,512,512]{2,1,0:T(8,128)(2,1)} %w3_ref.1) | copy-start | bytes 1572868
  62.3 11.2 %collective-permute-start.2 = (bf16[3,512,128]{2,1,0:T(8,128)(2,1)S(1)}, bf16[3,512,128]{2,1,0:T(8,128)(2,1)S(1)}, u32[]{:S(2)}, u32[]{:S(2)}) collective-permute-start(bf16[3,512,128]{2,1,0:T(8,128)(2,1)S(1)} %get-tuple-element.20), channel_id=1, source_target_pairs={{0,8},{4,12},{8,0},{12,4},{16,24},{20,28},{24,16},{28,20},{1,9},{5... | collective-permute-start | bytes 1179656 | tf_op jit(solution)/shard_map/ppermute | solution.py:33
  63.9 10.9 %collective-permute-start.3 = (bf16[3,512,128]{2,1,0:T(8,128)(2,1)S(1)}, bf16[3,512,128]{2,1,0:T(8,128)(2,1)S(1)}, u32[]{:S(2)}, u32[]{:S(2)}) collective-permute-start(bf16[3,512,128]{2,1,0:T(8,128)(2,1)S(1)} %get-tuple-element.21), channel_id=1, source_target_pairs={{0,16},{4,20},{8,24},{12,28},{16,0},{20,4},{24,8},{28,12},{1,17},{... | collective-permute-start | bytes 1179656 | tf_op jit(solution)/shard_map/ppermute | solution.py:33
  65.4 54.5 %collective-permute-start.13 = (bf16[3,128,2048]{2,1,0:T(8,128)(2,1)S(1)}, bf16[3,128,2048]{2,1,0:T(8,128)(2,1)}, u32[]{:S(2)}, u32[]{:S(2)}) collective-permute-start(bf16[3,128,2048]{2,1,0:T(8,128)(2,1)S(1)} %pad_maximum_fusion.refs_5_), channel_id=1, source_target_pairs={{0,4},{4,0},{8,12},{12,8},{16,20},{20,16},{24,28},{28,24},{1,5},{5... | collective-permute-start | bytes 4718600 | tf_op jit(solution)/shard_map/ppermute | solution.py:33
  65.4 66.2 %collective-permute-start.15 = (bf16[3,128,2048]{2,1,0:T(8,128)(2,1)}, bf16[3,128,2048]{2,1,0:T(8,128)(2,1)}, u32[]{:S(2)}, u32[]{:S(2)}) collective-permute-start(bf16[3,128,2048]{2,1,0:T(8,128)(2,1)} %collective-permute-done.14.refs_7_), channel_id=1, source_target_pairs={{0,4},{4,0},{8,12},{12,8},{16,20},{20,16},{24,28},{28,24},{1,5},{5... | collective-permute-start | bytes 4718600 | tf_op jit(solution)/shard_map/ppermute | solution.py:33
  75.0 10.1 %collective-permute-start.4 = (bf16[3,512,128]{2,1,0:T(8,128)(2,1)S(1)}, bf16[3,512,128]{2,1,0:T(8,128)(2,1)S(1)}, u32[]{:S(2)}, u32[]{:S(2)}) collective-permute-start(bf16[3,512,128]{2,1,0:T(8,128)(2,1)S(1)} %get-tuple-element.23), channel_id=1, source_target_pairs={{0,16},{4,20},{8,24},{12,28},{16,0},{20,4},{24,8},{28,12},{1,17},{... | collective-permute-start | bytes 1179656 | tf_op jit(solution)/shard_map/ppermute | solution.py:33
  76.6 9.7 %collective-permute-start.5 = (bf16[3,512,128]{2,1,0:T(8,128)(2,1)S(1)}, bf16[3,512,128]{2,1,0:T(8,128)(2,1)S(1)}, u32[]{:S(2)}, u32[]{:S(2)}) collective-permute-start(bf16[3,512,128]{2,1,0:T(8,128)(2,1)S(1)} %get-tuple-element.24), channel_id=1, source_target_pairs={{0,8},{4,12},{8,0},{12,4},{16,24},{20,28},{24,16},{28,20},{1,9},{5... | collective-permute-start | bytes 1179656 | tf_op jit(solution)/shard_map/ppermute | solution.py:33
  86.9 16.4 %collective-permute-start.6 = (bf16[3,512,256]{2,1,0:T(8,128)(2,1)S(1)}, bf16[3,512,256]{2,1,0:T(8,128)(2,1)S(1)}, u32[]{:S(2)}, u32[]{:S(2)}) collective-permute-start(bf16[3,512,256]{2,1,0:T(8,128)(2,1)S(1)} %renorm.1.mine_ref), channel_id=1, source_target_pairs={{0,4},{4,0},{8,12},{12,8},{16,20},{20,16},{24,28},{28,24},{1,5},{5... | collective-permute-start | bytes 2359304 | tf_op jit(solution)/shard_map/ppermute | solution.py:33
  87.0 10.8 %collective-permute-start = (bf16[512,512]{1,0:T(8,128)(2,1)}, bf16[512,512]{1,0:T(8,128)(2,1)}, u32[]{:S(2)}, u32[]{:S(2)}) collective-permute-start(bf16[512,512]{1,0:T(8,128)(2,1)} %get-tuple-element.16), channel_id=1, source_target_pairs={{0,4},{4,8},{8,12},{12,16},{16,20},{20,24},{24,28},{1,5},{5,9},{9,... | collective-permute-start | bytes 1572872 | tf_op jit(solution)/shard_map/ppermute | solution.py:345
  97.8 5.5 %copy-start = (bf16[1024,512]{1,0:T(8,128)(2,1)S(1)}, bf16[1024,512]{1,0:T(8,128)(2,1)}, u32[]{:S(2)}) copy-start(bf16[1024,512]{1,0:T(8,128)(2,1)} %q_ref.7) | copy-start | bytes 3145732
  104.0 15.9 %collective-permute-start.9 = (bf16[256,512]{1,0:T(8,128)(2,1)S(1)}, bf16[256,512]{1,0:T(8,128)(2,1)S(1)}, u32[]{:S(2)}, u32[]{:S(2)}) collective-permute-start(bf16[256,512]{1,0:T(8,128)(2,1)S(1)} %apply.6), channel_id=1, source_target_pairs={{0,3},{1,2},{2,1},{3,0},{4,7},{5,6},{6,5},{7,4},{8,11},{9,10},{10,... | collective-permute-start | bytes 786440 | tf_op jit(solution)/shard_map/ppermute | solution.py:33
  107.3 10.4 %copy-start.5 = (bf16[512]{0:T(512)(128)(2,1)S(1)}, bf16[512]{0:T(512)(128)(2,1)}, u32[]{:S(2)}) copy-start(bf16[512]{0:T(512)(128)(2,1)} %param.16) | copy-start | bytes 3076
  107.3 24.3 %collective-permute-start.8 = (bf16[256,512]{1,0:T(8,128)(2,1)S(1)}, bf16[256,512]{1,0:T(8,128)(2,1)S(1)}, u32[]{:S(2)}, u32[]{:S(2)}) collective-permute-start(bf16[256,512]{1,0:T(8,128)(2,1)S(1)} %apply.5), channel_id=1, source_target_pairs={{0,2},{1,3},{2,0},{3,1},{4,6},{5,7},{6,4},{7,5},{8,10},{9,11},{10,... | collective-permute-start | bytes 786440 | tf_op jit(solution)/shard_map/ppermute | solution.py:33
  117.4 14.1 %collective-permute-start.7 = (bf16[256,512]{1,0:T(8,128)(2,1)S(1)}, bf16[256,512]{1,0:T(8,128)(2,1)S(1)}, u32[]{:S(2)}, u32[]{:S(2)}) collective-permute-start(bf16[256,512]{1,0:T(8,128)(2,1)S(1)} %apply.4), channel_id=1, source_target_pairs={{0,1},{1,0},{2,3},{3,2},{4,5},{5,4},{6,7},{7,6},{8,9},{9,8},{10,11... | collective-permute-start | bytes 786440 | tf_op jit(solution)/shard_map/ppermute | solution.py:33
  117.6 1.6 %copy-start.1 = (bf16[512,2048]{1,0:T(8,128)(2,1)S(1)}, bf16[512,2048]{1,0:T(8,128)(2,1)}, u32[]{:S(2)}) copy-start(bf16[512,2048]{1,0:T(8,128)(2,1)} %w_ref.1) | copy-start | bytes 6291460

commit v2 on v1

--- a/solution.py
+++ b/solution.py
@@ -39,54 +39,58 @@
     )
 
 
-def push_kernel(core_ref, k_hbm, v_hbm, r_hbm, w1_hbm, w2_hbm, w3_hbm, give_ref, keep_ref, tail_hbm,
-                k_ref, v_ref, r_ref, w1_ref, w2_ref, w3_ref, act_ref, g1_ref, g3_ref, sc_ref, sem):
+def column(row, width):
+    tall = jnp.transpose(jnp.broadcast_to(row, (128, row.shape[1])))
+    return jnp.concatenate([tall] * (width // 128), axis=1)
+
+
+def prepare_kernel(part_ref, k_hbm, v_hbm, gain_ref, w_hbm, tail_ref, piece_ref, w_ref, sem):
+    rows, columns = piece_ref.shape
+    first = pl.multiple_of(part_ref[0] * rows, rows)
+    left = pl.multiple_of(part_ref[1] * columns, columns)
+    load = pltpu.make_async_copy(w_hbm.at[pl.ds(first, rows), pl.ds(left, columns)], w_ref, sem.at[0])
+    load.start()
+    last = pl.ds(k_hbm.shape[0] - WINDOW, WINDOW)
+    tails = [
+        pltpu.make_async_copy(src.at[last, :], tail_ref.at[pl.ds(j * WINDOW, WINDOW), :], sem.at[1 + j])
+        for j, src in enumerate((k_hbm, v_hbm))
+    ]
+    for tail in tails:
+        tail.start()
+    gain = column(gain_ref[:, pl.ds(first, rows)].astype(jnp.float32), columns)
+    load.wait()
+    piece_ref[...] = (w_ref[...].astype(jnp.float32) * gain).astype(jnp.bfloat16)
+    for tail in tails:
+        tail.wait()
+
+
+def prepare(part, keys, values, gain, weight):
+    piece = pltpu.VMEM((weight.shape[0] // 2, weight.shape[1] // 2), jnp.bfloat16)
+    return pl.pallas_call(
+        prepare_kernel,
+        out_shape=(pltpu.VMEM((2 * WINDOW, keys.shape[1]), jnp.bfloat16), piece),
+        compiler_params=grant(8),
+        in_specs=[SMEM, HBM, HBM, VMEM, HBM],
+        out_specs=(VMEM, VMEM),
+        scratch_shapes=[piece, pltpu.SemaphoreType.DMA((3,))],
+        name="prepare",
+    )(part, *far_core(keys, values), gain, *far_core(weight))
+
+
+def push_kernel(core_ref, k_ref, v_ref, r_ref, w1_ref, w2_ref, w3_ref, give_ref, keep_ref,
+                act_ref, g1_ref, g3_ref, sc_ref):
     rows, width = k_ref.shape
     steps = 4
     block = rows // steps
     half = width // 2
-    sources = [(w1_hbm, w1_ref), (w3_hbm, w3_ref), (w2_hbm, w2_ref)]
-    copies = [pltpu.make_async_copy(src.at[0], dst, sem.at[j]) for j, (src, dst) in enumerate(sources)]
-    copies.append(pltpu.make_async_copy(r_hbm, r_ref, sem.at[3]))
-    streams = []
-    for i in range(steps):
-        at = pl.ds(i * block, block)
-        streams.append([
-            pltpu.make_async_copy(src.at[at, :], dst.at[at, :], sem.at[4 + 2 * i + j])
-            for j, (src, dst) in enumerate([(k_hbm, k_ref), (v_hbm, v_ref)])
-        ])
-    last = pl.ds(rows - WINDOW, WINDOW)
-    tails = [
-        pltpu.make_async_copy(src.at[last, :], tail_hbm.at[pl.ds(j * WINDOW, WINDOW), :], sem.at[12 + j])
-        for j, src in enumerate((k_hbm, v_hbm))
-    ]
-    streams[0][0].start()
-    for copy in copies:
-        copy.start()
-    for i in range(steps):
-        for copy in streams[i][1 if i == 0 else 0:]:
-            copy.start()
-    for copy in tails:
-        copy.start()
     for i in range(steps):
         at = slice(i * block, (i + 1) * block)
-        if i == 0:
-            streams[0][0].wait()
-            copies[0].wait()
-            copies[1].wait()
-        else:
-            streams[i][0].wait()
         k = k_ref[at, :]
-        gate = dot(k, w1_ref[...])
-        up = dot(k, w3_ref[...])
-        if i == 0:
-            copies[2].wait()
-            copies[3].wait()
-        streams[i][1].wait()
-        rate = jnp.transpose(jnp.broadcast_to(r_ref[:, at], (128, block)))
-        rate = jnp.concatenate([rate] * (width // 128), axis=1)
+        gate = dot(k, w1_ref[0])
+        up = dot(k, w3_ref[0])
+        rate = column(r_ref[:, at], width)
         scaled = (v_ref[at, :].astype(jnp.float32) * rate).astype(jnp.bfloat16)
-        back = dot(scaled, w2_ref[...], 1, 1)
+        back = dot(scaled, w2_ref[0], 1, 1)
         s = jax.nn.sigmoid(gate)
         gs = gate * s
         act_ref[at, :] = (gs * up).astype(jnp.bfloat16)
@@ -100,29 +104,24 @@
         left = left[...]
         give_ref[j] = dot(left, right[:, theirs], 0, 0).astype(jnp.bfloat16)
         keep_ref[j] = dot(left, right[:, mine], 0, 0)
-    for copy in tails:
-        copy.wait()
 
 
 def pushes(core, keys, values, rates, w1, w2, w3):
     rows, width = keys.shape
     half = width // 2
     wide = pltpu.VMEM((rows, width), jnp.bfloat16)
-    weight = pltpu.VMEM((width, width), jnp.bfloat16)
     return pl.pallas_call(
         push_kernel,
         out_shape=(
             pltpu.VMEM((3, width, half), jnp.bfloat16),
             pltpu.VMEM((3, width, half), jnp.float32),
-            jax.ShapeDtypeStruct((2 * WINDOW, width), jnp.bfloat16),
         ),
-        compiler_params=grant(24),
-        in_specs=[SMEM] + [HBM] * 6,
-        out_specs=(VMEM, VMEM, HBM),
-        scratch_shapes=[wide, wide, pltpu.VMEM((1, rows), jnp.float32), weight, weight, weight,
-                        wide, wide, wide, wide, pltpu.SemaphoreType.DMA((14,))],
+        compiler_params=grant(16),
+        in_specs=[SMEM] + [VMEM] * 6,
+        out_specs=(VMEM, VMEM),
+        scratch_shapes=[wide] * 4,
         name="pushes",
-    )(core, *far_core(keys, values, rates.reshape(1, rows), w1, w2, w3))
+    )(core, *near_core(keys, values, rates.reshape(1, rows), w1, w2, w3))
 
 
 def first_add_kernel(keep_ref, got_ref, sum_ref, a_ref, b_ref):
@@ -283,39 +282,44 @@
     )(*near_core(x), gain, weight)
 
 
-def project_kernel(part_ref, *refs):
-    *xs, base_ref, squares_ref, near, near_c, far, far_c, out_ref, w_ref = refs
+def project_kernel(last, scale_by, part_ref, x_ref, base_ref, squares_ref, near, near_c, far, far_c, *outs):
     rows = near.shape[1]
-    heads = len(xs) + 1
-    squares = squares_ref[...]
-    for k in range(heads - 1):
-        for j, src in enumerate((near, near_c, far, far_c)):
-            place = pl.multiple_of((part_ref[0] ^ j) * rows, rows)
-            w_ref[k, pl.ds(place, rows), :] = src[k]
-        wide = xs[k][...].astype(jnp.float32)
-        squares = squares + jnp.sum(wide * wide, axis=1, keepdims=True)
-    scale = lax.rsqrt(squares / (heads * 4 * rows) + EPSILON)
-    block = 512
-    for start in range(0, out_ref.shape[1], block):
-        at = slice(start, start + block)
-        total = base_ref[:, at]
-        for k in range(heads - 1):
-            total = total + dot(xs[k][...], w_ref[k, :, at])
-        out_ref[:, at] = (total * scale).astype(out_ref.dtype)
-
-
-def project(part, xs, base, squares, pieces):
+    columns = near.shape[2]
+    wide = x_ref[...].astype(jnp.float32)
+    squares = squares_ref[...] + jnp.sum(wide * wide, axis=1, keepdims=True)
+    x_near = x_ref[:, pl.ds(pl.multiple_of(part_ref[0] * rows, rows), rows)]
+    x_far = x_ref[:, pl.ds(pl.multiple_of((1 - part_ref[0]) * rows, rows), rows)]
+    scale = lax.rsqrt(squares * scale_by + EPSILON)
+    for side, (w_near, w_far) in enumerate(((near, far), (near_c, far_c))):
+        start = part_ref[1] if side == 0 else 1 - part_ref[1]
+        block = columns // 2
+        for j in range(2):
+            at = pl.ds(pl.multiple_of(start * columns + j * block, block), block)
+            here = slice(j * block, (j + 1) * block)
+            total = base_ref[:, at] + dot(x_near, w_near[0, :, here]) + dot(x_far, w_far[0, :, here])
+            outs[0][:, at] = (total * scale).astype(outs[0].dtype) if last else total
+    if not last:
+        outs[1][...] = squares
+
+
+def project(last, scale_by, part, x, base, squares, index, pieces):
     rows, columns = base.shape
-    count, piece_rows, _ = pieces[0].shape
-    return pl.pallas_call(
-        project_kernel,
-        out_shape=jax.ShapeDtypeStruct((rows, columns), jnp.bfloat16),
-        in_specs=[SMEM] + [VMEM] * (len(xs) + 6),
-        out_specs=VMEM,
-        scratch_shapes=[pltpu.VMEM((count, 4 * piece_rows, columns), jnp.bfloat16)],
+    shape = jax.ShapeDtypeStruct((rows, columns), jnp.bfloat16)
+    if not last:
+        shape = (pltpu.VMEM((rows, columns), jnp.float32), pltpu.VMEM((rows, 1), jnp.float32))
+    return pl.pallas_call(
+        functools.partial(select_piece, functools.partial(project_kernel, last, scale_by), index),
+        out_shape=shape,
+        in_specs=[SMEM] + [VMEM] * 7,
+        out_specs=VMEM if last else (VMEM, VMEM),
         compiler_params=grant(16),
         name="project",
-    )(part, *near_core(*xs, base, squares, *pieces))
+    )(part, *near_core(x, base, squares, *pieces))
+
+
+def select_piece(kernel, index, part_ref, x_ref, base_ref, squares_ref, *refs):
+    pieces = [ref.at[pl.ds(index, 1)] for ref in refs[:4]]
+    kernel(part_ref, x_ref, base_ref, squares_ref, *pieces, *refs[4:])
 
 
 def step(queries, keys, values, rates, fast_w1, fast_w2, fast_w3, norm_gain, out_weight):
@@ -328,10 +332,19 @@
     assert ctx_count == 1 << bits and bits >= 3
     core = me & 1
     parity = ((me >> 1) ^ (me >> 2)) & 1
-    part = 2 * parity + core
     core1 = core.reshape(1)
-
-    give, keep, tail = pushes(core1, keys, values, rates, fast_w1, fast_w2, fast_w3)
+    part = jnp.stack([parity, core])
+    gain = norm_gain.reshape(1, width)
+
+    tail, piece = prepare(part, keys, values, gain, out_weight)
+    tail = lax.ppermute(tail, "ctx", [(i, i + 1) for i in range(ctx_count - 1)])
+
+    near = {0: piece}
+    for level in reversed(range(heads.bit_length() - 1)):
+        for k in sorted(near):
+            near[k | 1 << level] = swap(near[k], "head", 1 << level)
+
+    give, keep = pushes(core1, keys, values, rates, fast_w1, fast_w2, fast_w3)
     got = [swap(give, "ctx", 1)]
     masks = [1 << b for b in range(1, bits)]
     for forward, backward in zip(masks, masks[::-1]):
@@ -342,28 +355,32 @@
     mine = renorm(core1, keep, *got, fast_w1, fast_w2, fast_w3)
     other = swap(mine, "ctx", 1)
 
-    tail = lax.ppermute(tail, "ctx", [(i, i + 1) for i in range(ctx_count - 1)])
-    part_rows = width // 4
-    piece = lax.dynamic_slice_in_dim(out_weight, part * part_rows, part_rows, 0)
-    gain = lax.dynamic_slice_in_dim(norm_gain, part * part_rows, part_rows, 0)
-    piece = (piece.astype(jnp.float32) * gain.astype(jnp.float32)[:, None]).astype(jnp.bfloat16)
-    near = []
-    for k in range(1, heads):
-        near.append(swap(piece, "head", k))
-    near = jnp.stack(near)
-    far = lax.ppermute(near, "ctx", [(i, i ^ (4 if i & 1 else 2)) for i in range(ctx_count)])
-    near_c = swap(near, "ctx", 1)
-    far_c = swap(far, "ctx", 1)
-
     seen = window(me.reshape(1), queries, keys, values, tail)
+
+    early = jnp.stack([near[k] for k in range(1, heads - 1)])
+    late = near[heads - 1].reshape(1, *piece.shape)
+    cross = [(i, i ^ (4 if i & 1 else 2)) for i in range(ctx_count)]
+    pieces = []
+    for group in (early, late):
+        far = lax.ppermute(group, "ctx", cross)
+        near_c = swap(group, "ctx", 1)
+        far_c = swap(far, "ctx", 1)
+        pieces.append((group, near_c, far, far_c))
 
     rows = tok_rows // heads
     blocks = [None] * heads
     for k in list(range(heads - 1, 0, -1)) + [0]:
         combined = apply_fast(k, core1, head.reshape(1), queries, seen, mine, other, rows)
         blocks[k] = swap(combined, "head", k) if k else combined
-    base, squares = own_project(blocks[0], norm_gain.reshape(1, width), out_weight)
-    return project(part.reshape(1), blocks[1:], base, squares, [near, near_c, far, far_c])
+    base, squares = own_project(blocks[0], gain, out_weight)
+    scale_by = 1.0 / (heads * width)
+    for k in range(heads - 1, 0, -1):
+        which = pieces[1] if k == heads - 1 else pieces[0]
+        index = 0 if k == heads - 1 else k - 1
+        result = project(k == 1, scale_by, part, blocks[k], base, squares, index, which)
+        if k > 1:
+            base, squares = result
+    return result
 
 
 def solution(mesh):

time: 138 us -> 115 us (0.83)
  the two profiles are of different devices: /device:TPU:2 before, /device:TPU:0 now
where the time goes in v2:
time: 115 us
  waiting for transfers between devices  60.9 us (53%)
  starting transfers between devices  27.2 us (24%)
  Pallas kernels  23.5 us (20%)
  local copies, waits for them, and re-layouts  2.82 us (2%)
    ppermute x16, waiting for transfers between devices, swap(): lax.ppermute(value, axis, [(i, i ^ mask) for i in range(lax.axis_size(axi...  59 us
    ppermute x16, starting transfers between devices, swap(): lax.ppermute(value, axis, [(i, i ^ mask) for i in range(lax.axis_size(axi...  22.7 us
    pallas_call x3, Pallas kernels, project(): pl.pallas_call(functools.partial(select_piece, functools.partial(project_...  8.37 us
    pallas_call x1, Pallas kernels, window(): pl.pallas_call(window_kernel, out_shape=pltpu.VMEM(queries.shape, jnp.flo...  4.44 us
    pallas_call x1, Pallas kernels, pushes(): pl.pallas_call(push_kernel, out_shape=(pltpu.VMEM((3, width, half), jnp.b...  4.12 us
    ppermute x2, starting transfers between devices, step(): far = lax.ppermute(group, 'ctx', cross)  3.01 us
    pallas_call x4, Pallas kernels, apply_fast(): pl.pallas_call(functools.partial(apply_kernel, slot), out_shape=pltpu.VME...  2.68 us
  transfers between devices with their start and end apart: 19, of which 8 were waited for; matrix products, arithmetic and copies ran while one was open for 0% of the time, Pallas kernels for 15%

profile of v2, /device:TPU:0, one launch (start us, length us, event | category | flops | bytes accessed | tf_op | source)
XLA Modules:
  0.0 114.9 jit_solution(17913517141041306060)
XLA Ops:
  0.0 0.7 reshape.21.gain_ref
  0.8 2.0 %prepare.1 = (bf16[512,512]{1,0:T(8,128)(2,1)S(1)}, bf16[256,1024]{1,0:T(8,128)(2,1)S(1)}) custom-call(s32[2]{0:T(128)S(1)} %pad_add_fusion.part_ref, bf16[1024,512]{1,0:T(8,128)(2,1)} %k_ref.1, bf16[1024,512]{1,0:T(8,128)(2,1)} %v_ref.1, bf16[1,512]{1,0:T(2,128)(2,1)S(1)} %reshape.21.gain_ref, bf16[512,2048]{1,0:T(8,128)(2,1)} %w_ref.1), custom_call_target="tpu_custom_call" | custom-call | tf_op jit(solution)/shard_map/prepare/pallas_call | solution.py:69
  2.8 4.1 %collective-permute-start.10 = (bf16[256,1024]{1,0:T(8,128)(2,1)S(1)}, bf16[256,1024]{1,0:T(8,128)(2,1)S(1)}, u32[]{:S(2)}, u32[]{:S(2)}) collective-permute-start(bf16[256,1024]{1,0:T(8,128)(2,1)S(1)} %get-tuple-element.32), channel_id=1, source_target_pairs={{0,2},{1,3},{2,0},{3,1},{4,6},{5,7},{6,4},{7,5},{8,10},{9,11},{10,... | collective-permute-start | bytes 1572872 | tf_op jit(solution)/shard_map/ppermute | solution.py:33
  7.0 1.6 %collective-permute-start.15 = (bf16[256,1024]{1,0:T(8,128)(2,1)S(1)}, bf16[256,1024]{1,0:T(8,128)(2,1)S(1)}, u32[]{:S(2)}, u32[]{:S(2)}) collective-permute-start(bf16[256,1024]{1,0:T(8,128)(2,1)S(1)} %get-tuple-element.32), channel_id=1, source_target_pairs={{0,1},{1,0},{2,3},{3,2},{4,5},{5,4},{6,7},{7,6},{8,9},{9,8},{10,11... | collective-permute-start | bytes 1572872 | tf_op jit(solution)/shard_map/ppermute | solution.py:33
  8.6 4.1 %pushes.1 = (bf16[3,512,256]{2,1,0:T(8,128)(2,1)S(1)}, f32[3,512,256]{2,1,0:T(8,128)S(1)}) custom-call(s32[1]{0:T(128)} %bitcast.1.core_ref, bf16[1024,512]{1,0:T(8,128)(2,1)S(1)} %copy-done.1, bf16[1024,512]{1,0:T(8,128)(2,1)S(1)} %copy-done.2, f32[1,1024]{1,0:T(1,128)S(1)} %bitcast.11, bf16[1,512,512]{2,1,0:T(8,128)(2,1)S(1)} %copy-done.4, ...), custom_call_target="tpu_custom_call" | custom-call | tf_op jit(solution)/shard_map/pushes/pallas_call | solution.py:113
  12.8 17.4 %collective-permute-done.10 = bf16[256,1024]{1,0:T(8,128)(2,1)S(1)} collective-permute-done((bf16[256,1024]{1,0:T(8,128)(2,1)S(1)}, bf16[256,1024]{1,0:T(8,128)(2,1)S(1)}, u32[]{:S(2)}, u32[]{:S(2)}) %collective-permute-start.10) | collective-permute-done | bytes 524320 | tf_op jit(solution)/shard_map/ppermute | solution.py:33
  30.5 1.6 %collective-permute-start.17 = (bf16[2,256,1024]{2,1,0:T(8,128)(2,1)S(1)}, bf16[2,256,1024]{2,1,0:T(8,128)(2,1)}, u32[]{:S(2)}, u32[]{:S(2)}) collective-permute-start(bf16[2,256,1024]{2,1,0:T(8,128)(2,1)S(1)} %pad_maximum_fusion.refs_0_), channel_id=1, source_target_pairs={{0,8},{4,20},{8,0},{12,28},{16,24},{20,4},{24,16},{28,12},{1,9},{5... | collective-permute-start | bytes 3145736 | tf_op jit(solution)/shard_map/ppermute | solution.py:365
  33.0 1.6 %collective-permute-start.3 = (bf16[3,512,128]{2,1,0:T(8,128)(2,1)S(1)}, bf16[3,512,128]{2,1,0:T(8,128)(2,1)S(1)}, u32[]{:S(2)}, u32[]{:S(2)}) collective-permute-start(bf16[3,512,128]{2,1,0:T(8,128)(2,1)S(1)} %get-tuple-element.26), channel_id=1, source_target_pairs={{0,16},{4,20},{8,24},{12,28},{16,0},{20,4},{24,8},{28,12},{1,17},{... | collective-permute-start | bytes 1179656 | tf_op jit(solution)/shard_map/ppermute | solution.py:33
  34.6 1.4 %collective-permute-start.11 = (bf16[256,1024]{1,0:T(8,128)(2,1)S(1)}, bf16[256,1024]{1,0:T(8,128)(2,1)S(1)}, u32[]{:S(2)}, u32[]{:S(2)}) collective-permute-start(bf16[256,1024]{1,0:T(8,128)(2,1)S(1)} %collective-permute-done.10), channel_id=1, source_target_pairs={{0,1},{1,0},{2,3},{3,2},{4,5},{5,4},{6,7},{7,6},{8,9},{9,8},{10,11... | collective-permute-start | bytes 1572872 | tf_op jit(solution)/shard_map/ppermute | solution.py:33
  36.0 17.3 %collective-permute-done.2.got_a_ref = bf16[3,512,128]{2,1,0:T(8,128)(2,1)S(1)} collective-permute-done((bf16[3,512,128]{2,1,0:T(8,128)(2,1)S(1)}, bf16[3,512,128]{2,1,0:T(8,128)(2,1)S(1)}, u32[]{:S(2)}, u32[]{:S(2)}) %collective-permute-start.2) | collective-permute-done | bytes 393248 | tf_op jit(solution)/shard_map/ppermute | solution.py:33
  53.5 0.8 collective-permute-start.4
  54.3 1.3 %collective-permute-start.5 = (bf16[3,512,128]{2,1,0:T(8,128)(2,1)S(1)}, bf16[3,512,128]{2,1,0:T(8,128)(2,1)S(1)}, u32[]{:S(2)}, u32[]{:S(2)}) collective-permute-start(bf16[3,512,128]{2,1,0:T(8,128)(2,1)S(1)} %get-tuple-element.29), channel_id=1, source_target_pairs={{0,8},{4,12},{8,0},{12,4},{16,24},{20,28},{24,16},{28,20},{1,9},{5... | collective-permute-start | bytes 1179656 | tf_op jit(solution)/shard_map/ppermute | solution.py:33
  55.5 1.5 %collective-permute-start = (bf16[512,512]{1,0:T(8,128)(2,1)S(1)}, bf16[512,512]{1,0:T(8,128)(2,1)S(1)}, u32[]{:S(2)}, u32[]{:S(2)}) collective-permute-start(bf16[512,512]{1,0:T(8,128)(2,1)S(1)} %get-tuple-element.21), channel_id=1, source_target_pairs={{0,4},{4,8},{8,12},{12,16},{16,20},{20,24},{24,28},{1,5},{5,9},{9,... | collective-permute-start | bytes 1572872 | tf_op jit(solution)/shard_map/ppermute | solution.py:340
  57.1 1.4 %collective-permute-start.13 = (bf16[1,256,1024]{2,1,0:T(8,128)(2,1)S(1)}, bf16[1,256,1024]{2,1,0:T(8,128)(2,1)}, u32[]{:S(2)}, u32[]{:S(2)}) collective-permute-start(bf16[1,256,1024]{2,1,0:T(8,128)(2,1)S(1)} %bitcast.8), channel_id=1, source_target_pairs={{0,8},{4,20},{8,0},{12,28},{16,24},{20,4},{24,16},{28,12},{1,9},{5... | collective-permute-start | bytes 1572872 | tf_op jit(solution)/shard_map/ppermute | solution.py:365
  58.5 7.2 %collective-permute-done.4.got_a_ref = bf16[3,512,128]{2,1,0:T(8,128)(2,1)S(1)} collective-permute-done((bf16[3,512,128]{2,1,0:T(8,128)(2,1)S(1)}, bf16[3,512,128]{2,1,0:T(8,128)(2,1)S(1)}, u32[]{:S(2)}, u32[]{:S(2)}) %collective-permute-start.4) | collective-permute-done | bytes 393248 | tf_op jit(solution)/shard_map/ppermute | solution.py:33
  67.5 0.8 copy-done.7
  68.3 5.4 %collective-permute-start.12 = (bf16[1,256,1024]{2,1,0:T(8,128)(2,1)S(1)}, bf16[1,256,1024]{2,1,0:T(8,128)(2,1)}, u32[]{:S(2)}, u32[]{:S(2)}) collective-permute-start(bf16[1,256,1024]{2,1,0:T(8,128)(2,1)S(1)} %bitcast.9), channel_id=1, source_target_pairs={{0,4},{4,0},{8,12},{12,8},{16,20},{20,16},{24,28},{28,24},{1,5},{5... | collective-permute-start | bytes 1572872 | tf_op jit(solution)/shard_map/ppermute | solution.py:33
  73.8 1.9 %collective-permute-done.13.refs_2_ = bf16[1,256,1024]{2,1,0:T(8,128)(2,1)} collective-permute-done((bf16[1,256,1024]{2,1,0:T(8,128)(2,1)S(1)}, bf16[1,256,1024]{2,1,0:T(8,128)(2,1)}, u32[]{:S(2)}, u32[]{:S(2)}) %collective-permute-start.13) | collective-permute-done | bytes 524320 | tf_op jit(solution)/shard_map/ppermute | solution.py:365
  75.7 1.0 copy-done.8
  76.7 4.4 %window.1.seen_ref = f32[1024,512]{1,0:T(8,128)S(1)} custom-call(s32[1]{0:T(128)} %bitcast.3.me_ref, bf16[1024,512]{1,0:T(8,128)(2,1)} %q_ref.7, bf16[1024,512]{1,0:T(8,128)(2,1)} %k_ref.1, bf16[1024,512]{1,0:T(8,128)(2,1)} %v_ref.1, bf16[512,512]{1,0:T(8,128)(2,1)S(1)} %copy-done.8), custom_call_target="tpu_custom_call" | custom-call | tf_op jit(solution)/shard_map/window/pallas_call | solution.py:220
  81.2 0.7 apply.6
  81.9 4.5 %collective-permute-start.9 = (bf16[256,512]{1,0:T(8,128)(2,1)S(1)}, bf16[256,512]{1,0:T(8,128)(2,1)S(1)}, u32[]{:S(2)}, u32[]{:S(2)}) collective-permute-start(bf16[256,512]{1,0:T(8,128)(2,1)S(1)} %apply.6), channel_id=1, source_target_pairs={{0,3},{1,2},{2,1},{3,0},{4,7},{5,6},{6,5},{7,4},{8,11},{9,10},{10,... | collective-permute-start | bytes 786440 | tf_op jit(solution)/shard_map/ppermute | solution.py:33
  86.4 0.7 apply.5
  87.2 0.7 apply.4
  87.9 0.6 collective-permute-start.7
  88.5 0.7 apply.7.x_ref
  89.4 0.7 own_project.1
  90.2 3.5 %collective-permute-done.9.x_ref = bf16[256,512]{1,0:T(8,128)(2,1)S(1)} collective-permute-done((bf16[256,512]{1,0:T(8,128)(2,1)S(1)}, bf16[256,512]{1,0:T(8,128)(2,1)S(1)}, u32[]{:S(2)}, u32[]{:S(2)}) %collective-permute-start.9) | collective-permute-done | bytes 262176 | tf_op jit(solution)/shard_map/ppermute | solution.py:33
  93.7 2.1 %project.3 = (f32[256,2048]{1,0:T(8,128)S(1)}, f32[256,1]{1,0:T(8,128)S(1)}) custom-call(s32[2]{0:T(128)S(1)} %pad_add_fusion.part_ref, bf16[256,512]{1,0:T(8,128)(2,1)S(1)} %collective-permute-done.9.x_ref, f32[256,2048]{1,0:T(8,128)S(1)} %get-tuple-element.30.base_ref, f32[256,1]{1,0:T(8,128)S(1)} %get-tuple-element.31.squares_ref, ...), custom_call_target="tpu_custom_call" | custom-call | tf_op jit(solution)/shard_map/project/pallas_call | solution.py:310
  95.8 12.8 %collective-permute-done.8.x_ref = bf16[256,512]{1,0:T(8,128)(2,1)S(1)} collective-permute-done((bf16[256,512]{1,0:T(8,128)(2,1)S(1)}, bf16[256,512]{1,0:T(8,128)(2,1)S(1)}, u32[]{:S(2)}, u32[]{:S(2)}) %collective-permute-start.8) | collective-permute-done | bytes 262176 | tf_op jit(solution)/shard_map/ppermute | solution.py:33
  108.6 2.6 %project.4 = (f32[256,2048]{1,0:T(8,128)S(1)}, f32[256,1]{1,0:T(8,128)S(1)}) custom-call(s32[2]{0:T(128)S(1)} %pad_add_fusion.part_ref, bf16[256,512]{1,0:T(8,128)(2,1)S(1)} %collective-permute-done.8.x_ref, f32[256,2048]{1,0:T(8,128)S(1)} %get-tuple-element.33.base_ref, f32[256,1]{1,0:T(8,128)S(1)} %get-tuple-element.34.squares_ref, ...), custom_call_target="tpu_custom_call" | custom-call | tf_op jit(solution)/shard_map/project/pallas_call | solution.py:310
  111.2 3.6 %project.5 = bf16[256,2048]{1,0:T(8,128)(2,1)} custom-call(s32[2]{0:T(128)S(1)} %pad_add_fusion.part_ref, bf16[256,512]{1,0:T(8,128)(2,1)S(1)} %collective-permute-done.7.x_ref, f32[256,2048]{1,0:T(8,128)S(1)} %get-tuple-element.35.base_ref, f32[256,1]{1,0:T(8,128)S(1)} %get-tuple-element.36.squares_ref, bf16[2,256,1024]{2,1,0:T(8,128)(2,1)S(1)} %pad_maximum_fusion.refs_0_, ...), custom_call_target="tpu_custom_call" | custom-call | tf_op jit(solution)/shard_map/project/pallas_call | solution.py:310
  (43 shorter events, 3.7 us)
Async XLA Ops:
  0.8 7.8 %copy-start.1 = (bf16[1024,512]{1,0:T(8,128)(2,1)S(1)}, bf16[1024,512]{1,0:T(8,128)(2,1)}, u32[]{:S(2)}) copy-start(bf16[1024,512]{1,0:T(8,128)(2,1)} %k_ref.1) | copy-start | bytes 3145732
  0.8 7.8 %copy-start.2 = (bf16[1024,512]{1,0:T(8,128)(2,1)S(1)}, bf16[1024,512]{1,0:T(8,128)(2,1)}, u32[]{:S(2)}) copy-start(bf16[1024,512]{1,0:T(8,128)(2,1)} %v_ref.1) | copy-start | bytes 3145732
  0.8 7.8 %copy-start.4 = (bf16[1,512,512]{2,1,0:T(8,128)(2,1)S(1)}, bf16[1,512,512]{2,1,0:T(8,128)(2,1)}, u32[]{:S(2)}) copy-start(bf16[1,512,512]{2,1,0:T(8,128)(2,1)} %w1_ref.3) | copy-start | bytes 1572868
  0.8 7.8 %copy-start.5 = (bf16[1,512,512]{2,1,0:T(8,128)(2,1)S(1)}, bf16[1,512,512]{2,1,0:T(8,128)(2,1)}, u32[]{:S(2)}) copy-start(bf16[1,512,512]{2,1,0:T(8,128)(2,1)} %w2_ref.3) | copy-start | bytes 1572868
  0.8 7.8 %copy-start.6 = (bf16[1,512,512]{2,1,0:T(8,128)(2,1)S(1)}, bf16[1,512,512]{2,1,0:T(8,128)(2,1)}, u32[]{:S(2)}) copy-start(bf16[1,512,512]{2,1,0:T(8,128)(2,1)} %w3_ref.3) | copy-start | bytes 1572868
  0.8 7.8 %copy-start.9 = (f32[1024,1]{0,1:T(1,128)S(1)}, f32[1024,1]{0,1:T(1,128)}, u32[]{:S(2)}) copy-start(f32[1024,1]{0,1:T(1,128)} %param.12) | copy-start | bytes 12292
  2.8 27.4 %collective-permute-start.10 = (bf16[256,1024]{1,0:T(8,128)(2,1)S(1)}, bf16[256,1024]{1,0:T(8,128)(2,1)S(1)}, u32[]{:S(2)}, u32[]{:S(2)}) collective-permute-start(bf16[256,1024]{1,0:T(8,128)(2,1)S(1)} %get-tuple-element.32), channel_id=1, source_target_pairs={{0,2},{1,3},{2,0},{3,1},{4,6},{5,7},{6,4},{7,5},{8,10},{9,11},{10,... | collective-permute-start | bytes 1572872 | tf_op jit(solution)/shard_map/ppermute | solution.py:33
  7.0 23.5 %collective-permute-start.15 = (bf16[256,1024]{1,0:T(8,128)(2,1)S(1)}, bf16[256,1024]{1,0:T(8,128)(2,1)S(1)}, u32[]{:S(2)}, u32[]{:S(2)}) collective-permute-start(bf16[256,1024]{1,0:T(8,128)(2,1)S(1)} %get-tuple-element.32), channel_id=1, source_target_pairs={{0,1},{1,0},{2,3},{3,2},{4,5},{5,4},{6,7},{7,6},{8,9},{9,8},{10,11... | collective-permute-start | bytes 1572872 | tf_op jit(solution)/shard_map/ppermute | solution.py:33
  12.7 19.4 %collective-permute-start.1 = (bf16[3,512,256]{2,1,0:T(8,128)(2,1)S(1)}, bf16[3,512,256]{2,1,0:T(8,128)(2,1)S(1)}, u32[]{:S(2)}, u32[]{:S(2)}) collective-permute-start(bf16[3,512,256]{2,1,0:T(8,128)(2,1)S(1)} %get-tuple-element.23), channel_id=1, source_target_pairs={{0,4},{4,0},{8,12},{12,8},{16,20},{20,16},{24,28},{28,24},{1,5},{5... | collective-permute-start | bytes 2359304 | tf_op jit(solution)/shard_map/ppermute | solution.py:33
  30.5 36.9 %collective-permute-start.17 = (bf16[2,256,1024]{2,1,0:T(8,128)(2,1)S(1)}, bf16[2,256,1024]{2,1,0:T(8,128)(2,1)}, u32[]{:S(2)}, u32[]{:S(2)}) collective-permute-start(bf16[2,256,1024]{2,1,0:T(8,128)(2,1)S(1)} %pad_maximum_fusion.refs_0_), channel_id=1, source_target_pairs={{0,8},{4,20},{8,0},{12,28},{16,24},{20,4},{24,16},{28,12},{1,9},{5... | collective-permute-start | bytes 3145736 | tf_op jit(solution)/shard_map/ppermute | solution.py:365
  32.4 20.8 %collective-permute-start.2 = (bf16[3,512,128]{2,1,0:T(8,128)(2,1)S(1)}, bf16[3,512,128]{2,1,0:T(8,128)(2,1)S(1)}, u32[]{:S(2)}, u32[]{:S(2)}) collective-permute-start(bf16[3,512,128]{2,1,0:T(8,128)(2,1)S(1)} %get-tuple-element.25), channel_id=1, source_target_pairs={{0,8},{4,12},{8,0},{12,4},{16,24},{20,28},{24,16},{28,20},{1,9},{5... | collective-permute-start | bytes 1179656 | tf_op jit(solution)/shard_map/ppermute | solution.py:33
  33.0 20.3 %collective-permute-start.3 = (bf16[3,512,128]{2,1,0:T(8,128)(2,1)S(1)}, bf16[3,512,128]{2,1,0:T(8,128)(2,1)S(1)}, u32[]{:S(2)}, u32[]{:S(2)}) collective-permute-start(bf16[3,512,128]{2,1,0:T(8,128)(2,1)S(1)} %get-tuple-element.26), channel_id=1, source_target_pairs={{0,16},{4,20},{8,24},{12,28},{16,0},{20,4},{24,8},{28,12},{1,17},{... | collective-permute-start | bytes 1179656 | tf_op jit(solution)/shard_map/ppermute | solution.py:33
  34.6 22.5 %collective-permute-start.11 = (bf16[256,1024]{1,0:T(8,128)(2,1)S(1)}, bf16[256,1024]{1,0:T(8,128)(2,1)S(1)}, u32[]{:S(2)}, u32[]{:S(2)}) collective-permute-start(bf16[256,1024]{1,0:T(8,128)(2,1)S(1)} %collective-permute-done.10), channel_id=1, source_target_pairs={{0,1},{1,0},{2,3},{3,2},{4,5},{5,4},{6,7},{7,6},{8,9},{9,8},{10,11... | collective-permute-start | bytes 1572872 | tf_op jit(solution)/shard_map/ppermute | solution.py:33
  53.5 12.2 %collective-permute-start.4 = (bf16[3,512,128]{2,1,0:T(8,128)(2,1)S(1)}, bf16[3,512,128]{2,1,0:T(8,128)(2,1)S(1)}, u32[]{:S(2)}, u32[]{:S(2)}) collective-permute-start(bf16[3,512,128]{2,1,0:T(8,128)(2,1)S(1)} %get-tuple-element.28), channel_id=1, source_target_pairs={{0,16},{4,20},{8,24},{12,28},{16,0},{20,4},{24,8},{28,12},{1,17},{... | collective-permute-start | bytes 1179656 | tf_op jit(solution)/shard_map/ppermute | solution.py:33
  54.3 12.0 %collective-permute-start.5 = (bf16[3,512,128]{2,1,0:T(8,128)(2,1)S(1)}, bf16[3,512,128]{2,1,0:T(8,128)(2,1)S(1)}, u32[]{:S(2)}, u32[]{:S(2)}) collective-permute-start(bf16[3,512,128]{2,1,0:T(8,128)(2,1)S(1)} %get-tuple-element.29), channel_id=1, source_target_pairs={{0,8},{4,12},{8,0},{12,4},{16,24},{20,28},{24,16},{28,20},{1,9},{5... | collective-permute-start | bytes 1179656 | tf_op jit(solution)/shard_map/ppermute | solution.py:33
  55.5 12.0 %collective-permute-start = (bf16[512,512]{1,0:T(8,128)(2,1)S(1)}, bf16[512,512]{1,0:T(8,128)(2,1)S(1)}, u32[]{:S(2)}, u32[]{:S(2)}) collective-permute-start(bf16[512,512]{1,0:T(8,128)(2,1)S(1)} %get-tuple-element.21), channel_id=1, source_target_pairs={{0,4},{4,8},{8,12},{12,16},{16,20},{20,24},{24,28},{1,5},{5,9},{9,... | collective-permute-start | bytes 1572872 | tf_op jit(solution)/shard_map/ppermute | solution.py:340
  57.1 18.6 %collective-permute-start.13 = (bf16[1,256,1024]{2,1,0:T(8,128)(2,1)S(1)}, bf16[1,256,1024]{2,1,0:T(8,128)(2,1)}, u32[]{:S(2)}, u32[]{:S(2)}) collective-permute-start(bf16[1,256,1024]{2,1,0:T(8,128)(2,1)S(1)} %bitcast.8), channel_id=1, source_target_pairs={{0,8},{4,20},{8,0},{12,28},{16,24},{20,4},{24,16},{28,12},{1,9},{5... | collective-permute-start | bytes 1572872 | tf_op jit(solution)/shard_map/ppermute | solution.py:365
  66.9 14.3 %collective-permute-start.6 = (bf16[3,512,256]{2,1,0:T(8,128)(2,1)S(1)}, bf16[3,512,256]{2,1,0:T(8,128)(2,1)S(1)}, u32[]{:S(2)}, u32[]{:S(2)}) collective-permute-start(bf16[3,512,256]{2,1,0:T(8,128)(2,1)S(1)} %renorm.1.mine_ref), channel_id=1, source_target_pairs={{0,4},{4,0},{8,12},{12,8},{16,20},{20,16},{24,28},{28,24},{1,5},{5... | collective-permute-start | bytes 2359304 | tf_op jit(solution)/shard_map/ppermute | solution.py:33
  66.9 28.9 %collective-permute-start.16 = (bf16[2,256,1024]{2,1,0:T(8,128)(2,1)S(1)}, bf16[2,256,1024]{2,1,0:T(8,128)(2,1)}, u32[]{:S(2)}, u32[]{:S(2)}) collective-permute-start(bf16[2,256,1024]{2,1,0:T(8,128)(2,1)S(1)} %pad_maximum_fusion.refs_0_), channel_id=1, source_target_pairs={{0,4},{4,0},{8,12},{12,8},{16,20},{20,16},{24,28},{28,24},{1,5},{5... | collective-permute-start | bytes 3145736 | tf_op jit(solution)/shard_map/ppermute | solution.py:33
  67.5 41.2 %collective-permute-start.18 = (bf16[2,256,1024]{2,1,0:T(8,128)(2,1)}, bf16[2,256,1024]{2,1,0:T(8,128)(2,1)}, u32[]{:S(2)}, u32[]{:S(2)}) collective-permute-start(bf16[2,256,1024]{2,1,0:T(8,128)(2,1)} %collective-permute-done.17.refs_2_), channel_id=1, source_target_pairs={{0,4},{4,0},{8,12},{12,8},{16,20},{20,16},{24,28},{28,24},{1,5},{5... | collective-permute-start | bytes 3145736 | tf_op jit(solution)/shard_map/ppermute | solution.py:33
  67.5 0.8 copy-start.7
  68.3 18.7 %collective-permute-start.12 = (bf16[1,256,1024]{2,1,0:T(8,128)(2,1)S(1)}, bf16[1,256,1024]{2,1,0:T(8,128)(2,1)}, u32[]{:S(2)}, u32[]{:S(2)}) collective-permute-start(bf16[1,256,1024]{2,1,0:T(8,128)(2,1)S(1)} %bitcast.9), channel_id=1, source_target_pairs={{0,4},{4,0},{8,12},{12,8},{16,20},{20,16},{24,28},{28,24},{1,5},{5... | collective-permute-start | bytes 1572872 | tf_op jit(solution)/shard_map/ppermute | solution.py:33
  75.7 12.2 %collective-permute-start.14 = (bf16[1,256,1024]{2,1,0:T(8,128)(2,1)}, bf16[1,256,1024]{2,1,0:T(8,128)(2,1)}, u32[]{:S(2)}, u32[]{:S(2)}) collective-permute-start(bf16[1,256,1024]{2,1,0:T(8,128)(2,1)} %collective-permute-done.13.refs_2_), channel_id=1, source_target_pairs={{0,4},{4,0},{8,12},{12,8},{16,20},{20,16},{24,28},{28,24},{1,5},{5... | collective-permute-start | bytes 1572872 | tf_op jit(solution)/shard_map/ppermute | solution.py:33
  75.7 1.0 copy-start.8
  76.7 4.5 %copy-start = (bf16[1024,512]{1,0:T(8,128)(2,1)S(1)}, bf16[1024,512]{1,0:T(8,128)(2,1)}, u32[]{:S(2)}) copy-start(bf16[1024,512]{1,0:T(8,128)(2,1)} %q_ref.7) | copy-start | bytes 3145732
  81.9 11.8 %collective-permute-start.9 = (bf16[256,512]{1,0:T(8,128)(2,1)S(1)}, bf16[256,512]{1,0:T(8,128)(2,1)S(1)}, u32[]{:S(2)}, u32[]{:S(2)}) collective-permute-start(bf16[256,512]{1,0:T(8,128)(2,1)S(1)} %apply.6), channel_id=1, source_target_pairs={{0,3},{1,2},{2,1},{3,0},{4,7},{5,6},{6,5},{7,4},{8,11},{9,10},{10,... | collective-permute-start | bytes 786440 | tf_op jit(solution)/shard_map/ppermute | solution.py:33
  87.1 21.5 %collective-permute-start.8 = (bf16[256,512]{1,0:T(8,128)(2,1)S(1)}, bf16[256,512]{1,0:T(8,128)(2,1)S(1)}, u32[]{:S(2)}, u32[]{:S(2)}) collective-permute-start(bf16[256,512]{1,0:T(8,128)(2,1)S(1)} %apply.5), channel_id=1, source_target_pairs={{0,2},{1,3},{2,0},{3,1},{4,6},{5,7},{6,4},{7,5},{8,10},{9,11},{10,... | collective-permute-start | bytes 786440 | tf_op jit(solution)/shard_map/ppermute | solution.py:33
  87.8 1.6 %copy-start.3 = (bf16[512,2048]{1,0:T(8,128)(2,1)S(1)}, bf16[512,2048]{1,0:T(8,128)(2,1)}, u32[]{:S(2)}) copy-start(bf16[512,2048]{1,0:T(8,128)(2,1)} %w_ref.1) | copy-start | bytes 6291460
  87.9 23.4 %collective-permute-start.7 = (bf16[256,512]{1,0:T(8,128)(2,1)S(1)}, bf16[256,512]{1,0:T(8,128)(2,1)S(1)}, u32[]{:S(2)}, u32[]{:S(2)}) collective-permute-start(bf16[256,512]{1,0:T(8,128)(2,1)S(1)} %apply.4), channel_id=1, source_target_pairs={{0,1},{1,0},{2,3},{3,2},{4,5},{5,4},{6,7},{7,6},{8,9},{9,8},{10,11... | collective-permute-start | bytes 786440 | tf_op jit(solution)/shard_map/ppermute | solution.py:33

commit v3 on v2

v3 whole, which is shorter than its diff:
```python
import functools
import math

import jax
import jax.numpy as jnp
from jax import lax
from jax.experimental import pallas as pl
from jax.experimental.pallas import tpu as pltpu
from jax.sharding import PartitionSpec as P


WINDOW = 256
EPSILON = 1e-06

VMEM = pl.BlockSpec(memory_space=pltpu.VMEM)
HBM = pl.BlockSpec(memory_space=pltpu.HBM)


def near_core(*arrays):
    return [pltpu.with_memory_space_constraint(a, pltpu.VMEM) for a in arrays]


def far_core(*arrays):
    return [pltpu.with_memory_space_constraint(a, pltpu.HBM) for a in arrays]


def grant(mib):
    return pltpu.CompilerParams(vmem_limit_bytes=mib << 20)


def swap(value, axis, mask):
    return lax.ppermute(value, axis, [(i, i ^ mask) for i in range(lax.axis_size(axis))])


def dot(left, right, left_dim=1, right_dim=0):
    return lax.dot_general(
        left, right, (((left_dim,), (right_dim,)), ((), ())), preferred_element_type=jnp.float32
    )


def place():
    me = lax.axis_index("ctx").astype(jnp.int32)
    return me & 1, ((me >> 1) ^ (me >> 2)) & 1


def column(row, width):
    tall = jnp.transpose(jnp.broadcast_to(row, (128, row.shape[1])))
    return jnp.concatenate([tall] * (width // 128), axis=1)


def load_kernel(k_hbm, v_hbm, w1_hbm, w2_hbm, w3_hbm, tail_ref, k_ref, v_ref, w1_ref, w2_ref, w3_ref, sem):
    last = pl.ds(k_hbm.shape[0] - WINDOW, WINDOW)
    moves = [(k_hbm.at[last, :], tail_ref.at[pl.ds(0, WINDOW), :])]
    moves += [(v_hbm.at[last, :], tail_ref.at[pl.ds(WINDOW, WINDOW), :])]
    moves += [(w1_hbm, w1_ref), (w3_hbm, w3_ref), (k_hbm, k_ref), (v_hbm, v_ref), (w2_hbm, w2_ref)]
    copies = [pltpu.make_async_copy(src, dst, sem.at[j]) for j, (src, dst) in enumerate(moves)]
    for copy in copies:
        copy.start()
    for copy in copies:
        copy.wait()


def load(keys, values, w1, w2, w3):
    arrays = (keys, values, w1, w2, w3)
    return pl.pallas_call(
        load_kernel,
        out_shape=[pltpu.VMEM((2 * WINDOW, keys.shape[1]), jnp.bfloat16)]
        + [pltpu.VMEM(a.shape, a.dtype) for a in arrays],
        compiler_params=grant(4),
        in_specs=[HBM] * 5,
        out_specs=[VMEM] * 6,
        scratch_shapes=[pltpu.SemaphoreType.DMA((7,))],
        name="load",
    )(*far_core(*arrays))


def push_kernel(k_ref, v_ref, r_ref, w1_ref, w2_ref, w3_ref, gain_ref, w_hbm,
                give_ref, keep_ref, piece_ref, act_ref, g1_ref, g3_ref, sc_ref, w_ref, sem):
    rows, width = k_ref.shape
    piece_rows, columns = piece_ref.shape
    core, side = place()
    first = pl.multiple_of(side * piece_rows, piece_rows)
    left = pl.multiple_of(core * columns, columns)
    load = pltpu.make_async_copy(w_hbm.at[pl.ds(first, piece_rows), pl.ds(left, columns)], w_ref, sem)
    load.start()
    steps = 4
    block = rows // steps
    half = width // 2
    for i in range(steps):
        at = slice(i * block, (i + 1) * block)
        k = k_ref[at, :]
        gate = dot(k, w1_ref[0])
        up = dot(k, w3_ref[0])
        rate = column(r_ref[:, at], width)
        scaled = (v_ref[at, :].astype(jnp.float32) * rate).astype(jnp.bfloat16)
        back = dot(scaled, w2_ref[0], 1, 1)
        s = jax.nn.sigmoid(gate)
        gs = gate * s
        act_ref[at, :] = (gs * up).astype(jnp.bfloat16)
        sc_ref[at, :] = scaled
        g1_ref[at, :] = (back * up * (s + gs * (1.0 - s))).astype(jnp.bfloat16)
        g3_ref[at, :] = (back * gs).astype(jnp.bfloat16)
    load.wait()
    gain = gain_ref[...].reshape(1, width).astype(jnp.float32)
    gain = jnp.where(side == 0, gain[:, :piece_rows], gain[:, piece_rows:])
    piece_ref[...] = (w_ref[...].astype(jnp.float32) * column(gain, columns)).astype(jnp.bfloat16)
    theirs = pl.ds(pl.multiple_of((1 - core) * half, half), half)
    mine = pl.ds(pl.multiple_of(core * half, half), half)
    for j, (left, right) in enumerate([(k_ref, g1_ref), (act_ref, sc_ref), (k_ref, g3_ref)]):
        left = left[...]
        give_ref[j] = dot(left, right[:, theirs], 0, 0).astype(jnp.bfloat16)
        keep_ref[j] = dot(left, right[:, mine], 0, 0)


def pushes(keys, values, rates, w1, w2, w3, gain, weight):
    rows, width = keys.shape
    half = width // 2
    wide = pltpu.VMEM((rows, width), jnp.bfloat16)
    piece = pltpu.VMEM((weight.shape[0] // 2, weight.shape[1] // 2), jnp.bfloat16)
    return pl.pallas_call(
        push_kernel,
        out_shape=(
            pltpu.VMEM((3, width, half), jnp.bfloat16),
            pltpu.VMEM((3, width, half), jnp.float32),
            piece,
        ),
        compiler_params=grant(16),
        in_specs=[VMEM] * 7 + [HBM],
        out_specs=(VMEM,) * 3,
        scratch_shapes=[wide] * 4 + [piece, pltpu.SemaphoreType.DMA],
        name="pushes",
    )(*near_core(keys, values, rates.reshape(1, rows), w1, w2, w3, gain), *far_core(weight))


def add_kernel(keep_ref, got_ref, sum_ref, send_ref):
    total = keep_ref[...] + got_ref[...].astype(jnp.float32)
    sum_ref[...] = total
    send_ref[...] = total.astype(jnp.bfloat16)


def add(keep, got):
    return pl.pallas_call(
        add_kernel,
        out_shape=(pltpu.VMEM(keep.shape, jnp.float32), pltpu.VMEM(keep.shape, jnp.bfloat16)),
        compiler_params=grant(8),
        in_specs=[VMEM] * 2,
        out_specs=(VMEM,) * 2,
        name="add",
    )(*near_core(keep, got))


def renorm_kernel(keep_ref, got_ref, w1_ref, w2_ref, w3_ref, out_ref):
    _, half = got_ref.shape[1:]
    block = 128
    core, _ = place()
    for j, w_ref in enumerate((w1_ref, w2_ref, w3_ref)):
        for first in range(0, half, block):
            at = slice(first, first + block)
            start = pl.multiple_of(core * half + first, block)
            old = w_ref[0, :, pl.ds(start, block)].astype(jnp.float32)
            new = old + (keep_ref[j, :, at] + got_ref[j, :, at].astype(jnp.float32))
            old_norm = jnp.sqrt(jnp.mean(old * old, axis=0, keepdims=True) + EPSILON)
            new_norm = jnp.sqrt(jnp.mean(new * new, axis=0, keepdims=True) + EPSILON)
            out_ref[j, :, at] = (new * (old_norm / new_norm)).astype(jnp.bfloat16)


def renorm(keep, got, w1, w2, w3):
    return pl.pallas_call(
        renorm_kernel,
        out_shape=pltpu.VMEM(keep.shape, jnp.bfloat16),
        compiler_params=grant(8),
        in_specs=[VMEM] * 5,
        out_specs=VMEM,
        name="renorm",
    )(*near_core(keep, got, w1, w2, w3))


def window_kernel(q_hbm, k_hbm, v_hbm, tail_ref, out_ref, q_ref, k_ref, v_ref, sem):
    rows, width = q_ref.shape
    scale = 1.0 / math.sqrt(width)
    query = lax.broadcasted_iota(jnp.int32, (WINDOW, 2 * WINDOW), 0)
    key = lax.broadcasted_iota(jnp.int32, (WINDOW, 2 * WINDOW), 1)
    allowed = (key > query) & (key <= query + WINDOW)
    allowed_first = allowed & ((key >= WINDOW) | (lax.axis_index("ctx") > 0))
    count = rows // WINDOW
    loads = [[
        pltpu.make_async_copy(tail_ref.at[pl.ds(j * WINDOW, WINDOW), :], dst.at[pl.ds(0, WINDOW), :], sem.at[j])
        for j, dst in enumerate((k_ref, v_ref))
    ]]
    for i in range(count):
        at, after = pl.ds(i * WINDOW, WINDOW), pl.ds((i + 1) * WINDOW, WINDOW)
        loads.append([
            pltpu.make_async_copy(q_hbm.at[at, :], q_ref.at[at, :], sem.at[3 * i + 2]),
            pltpu.make_async_copy(k_hbm.at[at, :], k_ref.at[after, :], sem.at[3 * i + 3]),
            pltpu.make_async_copy(v_hbm.at[at, :], v_ref.at[after, :], sem.at[3 * i + 4]),
        ])
    for group in loads:
        for load in group:
            load.start()
    for load in loads[0]:
        load.wait()
    for i in range(count):
        for load in loads[i + 1]:
            load.wait()
        at = slice(i * WINDOW, (i + 1) * WINDOW)
        seen = slice(i * WINDOW, (i + 2) * WINDOW)
        scores = dot(q_ref[at, :], k_ref[seen, :], 1, 1) * scale
        scores = jnp.where(allowed_first if i == 0 else allowed, scores, -jnp.inf)
        peak = jnp.max(scores, axis=1, keepdims=True)
        exponent = jnp.exp(scores - peak)
        weights = exponent / jnp.sum(exponent, axis=1, keepdims=True)
        out_ref[at, :] = dot(weights.astype(jnp.bfloat16), v_ref[seen, :])


def window(queries, keys, values, tail):
    rows, width = queries.shape
    return pl.pallas_call(
        window_kernel,
        out_shape=pltpu.VMEM(queries.shape, jnp.float32),
        compiler_params=grant(24),
        in_specs=[HBM] * 3 + [VMEM],
        out_specs=VMEM,
        scratch_shapes=[pltpu.VMEM((rows, width), jnp.bfloat16)]
        + [pltpu.VMEM((rows + WINDOW, width), jnp.bfloat16)] * 2
        + [pltpu.SemaphoreType.DMA((2 + 3 * (rows // WINDOW),))],
        name="window",
    )(*far_core(queries, keys, values), *near_core(tail))


def apply_kernel(slot, q_ref, seen_ref, mine_ref, other_ref, out_ref):
    rows = out_ref.shape[0]
    half = mine_ref.shape[2]
    core, _ = place()
    own = pl.ds(pl.multiple_of(core * half, half), half)
    rest = pl.ds(pl.multiple_of((1 - core) * half, half), half)
    here = pl.ds(pl.multiple_of((lax.axis_index("head").astype(jnp.int32) ^ slot) * rows, rows), rows)
    q = q_ref[here, :]

    mixed = []
    for ref in (mine_ref, other_ref):
        gate = dot(q, ref[0])
        up = dot(q, ref[2])
        mixed.append((gate * jax.nn.sigmoid(gate) * up).astype(jnp.bfloat16))
    mixed = jnp.concatenate(mixed, axis=1)
    for ref, at in ((mine_ref, own), (other_ref, rest)):
        down = jnp.concatenate([ref[1, own, :], ref[1, rest, :]], axis=0)
        out_ref[:, at] = (dot(mixed, down) + seen_ref[here, at]).astype(jnp.bfloat16)


def apply_fast(slot, queries, seen, mine, other, rows):
    return pl.pallas_call(
        functools.partial(apply_kernel, slot),
        out_shape=pltpu.VMEM((rows, queries.shape[1]), jnp.bfloat16),
        compiler_params=grant(16),
        in_specs=[VMEM] * 4,
        out_specs=VMEM,
        name="apply",
    )(*near_core(queries, seen, mine, other))


def own_project_kernel(x_ref, gain_ref, w_ref, out_ref, squares_ref):
    wide = x_ref[...].astype(jnp.float32)
    squares_ref[...] = jnp.sum(wide * wide, axis=1, keepdims=True)
    gain = gain_ref[...].reshape(1, wide.shape[1]).astype(jnp.float32)
    x = (wide * gain).astype(jnp.bfloat16)
    out_ref[...] = dot(x, w_ref[...])


def own_project(x, gain, weight):
    return pl.pallas_call(
        own_project_kernel,
        out_shape=(
            pltpu.VMEM((x.shape[0], weight.shape[1]), jnp.float32),
            pltpu.VMEM((x.shape[0], 1), jnp.float32),
        ),
        compiler_params=grant(16),
        in_specs=[VMEM] * 3,
        out_specs=(VMEM, VMEM),
        name="own_project",
    )(*near_core(x, gain, weight))


def pile_kernel(*refs):
    *ins, out_ref, sem = refs
    copies = [pltpu.make_async_copy(src, out_ref.at[j], sem.at[j]) for j, src in enumerate(ins)]
    for copy in copies:
        copy.start()
    for copy in copies:
        copy.wait()


def pile(*arrays):
    return pl.pallas_call(
        pile_kernel,
        out_shape=pltpu.VMEM((len(arrays),) + arrays[0].shape, arrays[0].dtype),
        compiler_params=grant(4),
        in_specs=[VMEM] * len(arrays),
        out_specs=VMEM,
        scratch_shapes=[pltpu.SemaphoreType.DMA((len(arrays),))],
        name="pile",
    )(*near_core(*arrays))


def project_kernel(index, scale_by, x_ref, base_ref, squares_ref, near, near_c, far, far_c,
                   out_ref, *rest):
    rows, columns = near.shape[1:]
    core, half = place()
    wide = x_ref[...].astype(jnp.float32)
    squares = squares_ref[...] + jnp.sum(wide * wide, axis=1, keepdims=True)
    mine = pl.ds(pl.multiple_of(half * rows, rows), rows)
    theirs = pl.ds(pl.multiple_of((1 - half) * rows, rows), rows)
    x = jnp.concatenate([x_ref[:, mine], x_ref[:, theirs]], axis=1)
    scale = lax.rsqrt(squares * scale_by + EPSILON) if scale_by else None
    block = columns // 2
    stores = []
    for side, (w_near, w_far) in enumerate(((near, far), (near_c, far_c))):
        start = core if side == 0 else 1 - core
        for j in range(2):
            at = pl.ds(pl.multiple_of(start * columns + j * block, block), block)
            here = slice(j * block, (j + 1) * block)
            w = jnp.concatenate([w_near[index, :, here], w_far[index, :, here]], axis=0)
            total = base_ref[:, at] + dot(x, w)
            if scale_by:
                ready_ref, sem = rest
                ready_ref[2 * side + j] = (total * scale).astype(jnp.bfloat16)
                store = pltpu.make_async_copy(ready_ref.at[2 * side + j], out_ref.at[:, at], sem.at[2 * side + j])
                store.start()
                stores.append(store)
            else:
                out_ref[:, at] = total
    if not scale_by:
        rest[0][...] = squares
    for store in stores:
        store.wait()


def project(index, scale_by, x, base, squares, pieces):
    rows, columns = base.shape
    if scale_by:
        shape = jax.ShapeDtypeStruct((rows, columns), jnp.bfloat16)
        scratch = [pltpu.VMEM((4, rows, columns // 4), jnp.bfloat16), pltpu.SemaphoreType.DMA((4,))]
    else:
        shape = (pltpu.VMEM((rows, columns), jnp.float32), pltpu.VMEM((rows, 1), jnp.float32))
        scratch = []
    return pl.pallas_call(
        functools.partial(project_kernel, index, scale_by),
        out_shape=shape,
        in_specs=[VMEM] * 7,
        out_specs=HBM if scale_by else (VMEM, VMEM),
        scratch_shapes=scratch,
        compiler_params=grant(16),
        name="project",
    )(*near_core(x, base, squares, *pieces))


def step(queries, keys, values, rates, fast_w1, fast_w2, fast_w3, norm_gain, out_weight):
    tok_rows, width = queries.shape
    ctx_count = lax.axis_size("ctx")
    heads = lax.axis_size("head")
    bits = ctx_count.bit_length() - 1
    assert ctx_count == 1 << bits and bits >= 3

    tail, *loaded = load(keys, values, fast_w1, fast_w2, fast_w3)
    tail = lax.ppermute(tail, "ctx", [(i, i + 1) for i in range(ctx_count - 1)])
    give, keep, piece = pushes(
        loaded[0], loaded[1], rates, *loaded[2:], norm_gain, out_weight
    )
    got = swap(give, "ctx", 1)

    near = {0: piece}
    for level in reversed(range(heads.bit_length() - 1)):
        for k in sorted(near):
            near[k | 1 << level] = swap(near[k], "head", 1 << level)

    masks = [1 << b for b in range(1, bits)]
    crossing = [
        [(i, i ^ (backward if i & 1 else forward)) for i in range(ctx_count)]
        for forward, backward in zip(masks, masks[::-1])
    ]
    for pairs in crossing:
        keep, send = add(keep, got)
        got = lax.ppermute(send, "ctx", pairs)
    mine = renorm(keep, got, fast_w1, fast_w2, fast_w3)
    other = swap(mine, "ctx", 1)

    seen = window(queries, keys, values, tail)

    early = pile(*(near[k] for k in range(1, heads - 1)))
    late = near[heads - 1].reshape(1, *piece.shape)
    cross = [(i, i ^ (4 if i & 1 else 2)) for i in range(ctx_count)]
    pieces = []
    for group in (early, late):
        far = lax.ppermute(group, "ctx", cross)
        near_c = swap(group, "ctx", 1)
        far_c = swap(far, "ctx", 1)
        pieces.append((group, near_c, far, far_c))

    rows = tok_rows // heads
    blocks = {}
    for k in send_order(heads) + [0]:
        combined = apply_fast(k, queries, seen, mine, other, rows)
        blocks[k] = swap(combined, "head", k) if k else combined
    base, squares = own_project(blocks[0], norm_gain, out_weight)
    for k in send_order(heads):
        late_one = k == heads - 1
        index, which = (0, pieces[1]) if late_one else (k - 1, pieces[0])
        scale_by = 1.0 / (heads * width) if k == send_order(heads)[-1] else None
        result = project(index, scale_by, blocks[k], base, squares, which)
        if scale_by is None:
            base, squares = result
    return result


def send_order(heads):
    return [heads - 1] + list(range(1, heads - 1))


def solution(mesh):
    placed = (
        P("ctx", "head"),
        P("ctx", "head"),
        P("ctx", "head"),
        P("ctx", "head"),
        P("head", None, None),
        P("head", None, None),
        P("head", None, None),
        P("head"),
        P("head", None),
    )
    return jax.shard_map(
        step, mesh=mesh, in_specs=placed, out_specs=P(("ctx", "head"), None), check_vma=False
    )
```

time: 115 us -> 106 us (0.922)
  starting transfers between devices: 27.2 us -> 21.1 us
  Pallas kernels: 23.5 us -> 18.7 us
  waiting for transfers between devices: 60.9 us -> 65.3 us
  local copies, waits for them, and re-layouts: 2.82 us -> 0.39 us
    ppermute x16 -> x12, starting transfers between devices: 22.7 us -> 14.2 us  [swap(): lax.ppermute(value, axis, [(i, i ^ mask) for i in range(lax.axis_size(axi...]
    ppermute x0 -> x2, waiting for transfers between devices: none -> 8.05 us  [step(): got = lax.ppermute(send, 'ctx', pairs)]
    ppermute x16 -> x12, waiting for transfers between devices: 59 us -> 51.4 us  [swap(): lax.ppermute(value, axis, [(i, i ^ mask) for i in range(lax.axis_size(axi...]
    pallas_call x6 -> x7, Pallas kernels: 10.9 us -> 5.79 us  [the longest x3 2.99 us: project(): pl.pallas_call(functools.partial(project_kernel, index, scale_by), out_sh...]
    ppermute x2, waiting for transfers between devices: 1.92 us -> 5.84 us  [step(): far = lax.ppermute(group, 'ctx', cross)]
    ppermute x0 -> x2, starting transfers between devices: none -> 3.68 us  [step(): got = lax.ppermute(send, 'ctx', pairs)]
    unnamed x20 -> x14, local copies, waits for them, and re-layouts: 2.14 us -> 0.39 us
    ppermute x2, starting transfers between devices: 3.01 us -> 1.71 us  [step(): far = lax.ppermute(group, 'ctx', cross)]
  transfers between devices with their start and end apart: 19 -> 17, of which waited for: 8 -> 10; matrix products, arithmetic and copies ran while one was open for 0% -> 0% of each run, Pallas kernels for 15% -> 9%
where the time goes in v3:
time: 106 us
  waiting for transfers between devices  65.3 us (62%)
  starting transfers between devices  21.1 us (20%)
  Pallas kernels  18.7 us (18%)
    ppermute x12, waiting for transfers between devices, swap(): lax.ppermute(value, axis, [(i, i ^ mask) for i in range(lax.axis_size(axi...  51.4 us
    ppermute x12, starting transfers between devices, swap(): lax.ppermute(value, axis, [(i, i ^ mask) for i in range(lax.axis_size(axi...  14.2 us
    ppermute x2, waiting for transfers between devices, step(): got = lax.ppermute(send, 'ctx', pairs)  8.05 us
    ppermute x2, waiting for transfers between devices, step(): far = lax.ppermute(group, 'ctx', cross)  5.84 us
    pallas_call x1, Pallas kernels, pushes(): pl.pallas_call(push_kernel, out_shape=(pltpu.VMEM((3, width, half), jnp.b...  4.91 us
    pallas_call x1, Pallas kernels, window(): pl.pallas_call(window_kernel, out_shape=pltpu.VMEM(queries.shape, jnp.flo...  4.37 us
    ppermute x2, starting transfers between devices, step(): got = lax.ppermute(send, 'ctx', pairs)  3.68 us
    pallas_call x3, Pallas kernels, project(): pl.pallas_call(functools.partial(project_kernel, index, scale_by), out_sh...  2.99 us
  transfers between devices with their start and end apart: 17, of which 10 were waited for; matrix products, arithmetic and copies ran while one was open for 0% of the time, Pallas kernels for 9%

profile of v3, /device:TPU:0, one launch (start us, length us, event | category | flops | bytes accessed | tf_op | source)
XLA Modules:
  0.0 105.9 jit_solution(7505314098807482638)
XLA Ops:
  0.0 2.2 %load.1 = (bf16[512,512]{1,0:T(8,128)(2,1)S(1)}, bf16[1024,512]{1,0:T(8,128)(2,1)S(1)}, bf16[1024,512]{1,0:T(8,128)(2,1)S(1)}, bf16[1,512,512]{2,1,0:T(8,128)(2,...) custom-call(bf16[1024,512]{1,0:T(8,128)(2,1)} %k_hbm.3, bf16[1024,512]{1,0:T(8,128)(2,1)} %v_hbm.3, ...), custom_call_target="tpu_custom_call" | custom-call | tf_op jit(solution)/shard_map/load/pallas_call | solution.py:65
  2.3 4.9 %pushes.1 = (bf16[3,512,256]{2,1,0:T(8,128)(2,1)S(1)}, f32[3,512,256]{2,1,0:T(8,128)S(1)}, bf16[256,1024]{1,0:T(8,128)(2,1)S(1)}) custom-call(bf16[1024,512]{1,0:T(8,128)(2,1)S(1)} %get-tuple-element.25.k_ref, bf16[1024,512]{1,0:T(8,128)(2,1)S(1)} %get-tuple-element.26.v_ref, f32[1,1024]{1,0:T(1,128)S(1)} %bitcast.5, ...), custom_call_target="tpu_custom_call" | custom-call | tf_op jit(solution)/shard_map/pushes/pallas_call | solution.py:120
  7.2 0.6 collective-permute-start.1
  7.7 1.9 %collective-permute-done.1.got_ref = bf16[3,512,256]{2,1,0:T(8,128)(2,1)S(1)} collective-permute-done((bf16[3,512,256]{2,1,0:T(8,128)(2,1)S(1)}, bf16[3,512,256]{2,1,0:T(8,128)(2,1)S(1)}, u32[]{:S(2)}, u32[]{:S(2)}) %collective-permute-start.1) | collective-permute-done | bytes 786464 | tf_op jit(solution)/shard_map/ppermute | solution.py:32
  9.9 2.9 %collective-permute-start.2 = (bf16[3,512,256]{2,1,0:T(8,128)(2,1)S(1)}, bf16[3,512,256]{2,1,0:T(8,128)(2,1)S(1)}, u32[]{:S(2)}, u32[]{:S(2)}) collective-permute-start(bf16[3,512,256]{2,1,0:T(8,128)(2,1)S(1)} %get-tuple-element.33), channel_id=1, source_target_pairs={{0,8},{4,20},{8,0},{12,28},{16,24},{20,4},{24,16},{28,12},{1,9},{5... | collective-permute-start | bytes 2359304 | tf_op jit(solution)/shard_map/ppermute | solution.py:382
  12.8 2.6 %collective-permute-start.8 = (bf16[256,1024]{1,0:T(8,128)(2,1)S(1)}, bf16[256,1024]{1,0:T(8,128)(2,1)S(1)}, u32[]{:S(2)}, u32[]{:S(2)}) collective-permute-start(bf16[256,1024]{1,0:T(8,128)(2,1)S(1)} %get-tuple-element.38), channel_id=1, source_target_pairs={{0,2},{1,3},{2,0},{3,1},{4,6},{5,7},{6,4},{7,5},{8,10},{9,11},{10,... | collective-permute-start | bytes 1572872 | tf_op jit(solution)/shard_map/ppermute | solution.py:32
  15.4 1.6 %collective-permute-start.13 = (bf16[256,1024]{1,0:T(8,128)(2,1)S(1)}, bf16[256,1024]{1,0:T(8,128)(2,1)S(1)}, u32[]{:S(2)}, u32[]{:S(2)}) collective-permute-start(bf16[256,1024]{1,0:T(8,128)(2,1)S(1)} %get-tuple-element.38), channel_id=1, source_target_pairs={{0,1},{1,0},{2,3},{3,2},{4,5},{5,4},{6,7},{7,6},{8,9},{9,8},{10,11... | collective-permute-start | bytes 1572872 | tf_op jit(solution)/shard_map/ppermute | solution.py:32
  17.0 21.8 %collective-permute-done.8.refs_1_ = bf16[256,1024]{1,0:T(8,128)(2,1)S(1)} collective-permute-done((bf16[256,1024]{1,0:T(8,128)(2,1)S(1)}, bf16[256,1024]{1,0:T(8,128)(2,1)S(1)}, u32[]{:S(2)}, u32[]{:S(2)}) %collective-permute-start.8) | collective-permute-done | bytes 524320 | tf_op jit(solution)/shard_map/ppermute | solution.py:32
  39.1 1.4 %collective-permute-start.15 = (bf16[2,256,1024]{2,1,0:T(8,128)(2,1)S(1)}, bf16[2,256,1024]{2,1,0:T(8,128)(2,1)S(1)}, u32[]{:S(2)}, u32[]{:S(2)}) collective-permute-start(bf16[2,256,1024]{2,1,0:T(8,128)(2,1)S(1)} %pile.1.near), channel_id=1, source_target_pairs={{0,8},{4,20},{8,0},{12,28},{16,24},{20,4},{24,16},{28,12},{1,9},{5... | collective-permute-start | bytes 3145736 | tf_op jit(solution)/shard_map/ppermute | solution.py:393
  40.7 0.8 collective-permute-start.3
  41.4 1.4 %collective-permute-start.9 = (bf16[256,1024]{1,0:T(8,128)(2,1)S(1)}, bf16[256,1024]{1,0:T(8,128)(2,1)S(1)}, u32[]{:S(2)}, u32[]{:S(2)}) collective-permute-start(bf16[256,1024]{1,0:T(8,128)(2,1)S(1)} %collective-permute-done.8.refs_1_), channel_id=1, source_target_pairs={{0,1},{1,0},{2,3},{3,2},{4,5},{5,4},{6,7},{7,6},{8,9},{9,8},{10,11... | collective-permute-start | bytes 1572872 | tf_op jit(solution)/shard_map/ppermute | solution.py:32
  42.9 1.5 %collective-permute-start = (bf16[512,512]{1,0:T(8,128)(2,1)S(1)}, bf16[512,512]{1,0:T(8,128)(2,1)S(1)}, u32[]{:S(2)}, u32[]{:S(2)}) collective-permute-start(bf16[512,512]{1,0:T(8,128)(2,1)S(1)} %get-tuple-element.24), channel_id=1, source_target_pairs={{0,4},{4,8},{8,12},{12,16},{16,20},{20,24},{24,28},{1,5},{5,9},{9,... | collective-permute-start | bytes 1572872 | tf_op jit(solution)/shard_map/ppermute | solution.py:364
  44.4 9.8 %collective-permute-done.9 = bf16[256,1024]{1,0:T(8,128)(2,1)S(1)} collective-permute-done((bf16[256,1024]{1,0:T(8,128)(2,1)S(1)}, bf16[256,1024]{1,0:T(8,128)(2,1)S(1)}, u32[]{:S(2)}, u32[]{:S(2)}) %collective-permute-start.9) | collective-permute-done | bytes 524320 | tf_op jit(solution)/shard_map/ppermute | solution.py:32
  54.5 8.1 %collective-permute-done.3.got_ref = bf16[3,512,256]{2,1,0:T(8,128)(2,1)S(1)} collective-permute-done((bf16[3,512,256]{2,1,0:T(8,128)(2,1)S(1)}, bf16[3,512,256]{2,1,0:T(8,128)(2,1)S(1)}, u32[]{:S(2)}, u32[]{:S(2)}) %collective-permute-start.3) | collective-permute-done | bytes 786464 | tf_op jit(solution)/shard_map/ppermute | solution.py:382
  62.6 0.6 renorm.1.mine_ref
  63.8 1.4 %collective-permute-done.15.far = bf16[2,256,1024]{2,1,0:T(8,128)(2,1)S(1)} collective-permute-done((bf16[2,256,1024]{2,1,0:T(8,128)(2,1)S(1)}, bf16[2,256,1024]{2,1,0:T(8,128)(2,1)S(1)}, u32[]{:S(2)}, u32[]{:S(2)}) %collective-permute-start.15) | collective-permute-done | bytes 1048608 | tf_op jit(solution)/shard_map/ppermute | solution.py:393
  65.2 2.5 %collective-permute-start.10 = (bf16[1,256,1024]{2,1,0:T(8,128)(2,1)S(1)}, bf16[1,256,1024]{2,1,0:T(8,128)(2,1)S(1)}, u32[]{:S(2)}, u32[]{:S(2)}) collective-permute-start(bf16[1,256,1024]{2,1,0:T(8,128)(2,1)S(1)} %bitcast.3), channel_id=1, source_target_pairs={{0,4},{4,0},{8,12},{12,8},{16,20},{20,16},{24,28},{28,24},{1,5},{5... | collective-permute-start | bytes 1572872 | tf_op jit(solution)/shard_map/ppermute | solution.py:32
  67.7 4.4 %collective-permute-done.11.far = bf16[1,256,1024]{2,1,0:T(8,128)(2,1)S(1)} collective-permute-done((bf16[1,256,1024]{2,1,0:T(8,128)(2,1)S(1)}, bf16[1,256,1024]{2,1,0:T(8,128)(2,1)S(1)}, u32[]{:S(2)}, u32[]{:S(2)}) %collective-permute-start.11) | collective-permute-done | bytes 524320 | tf_op jit(solution)/shard_map/ppermute | solution.py:393
  72.2 4.4 %window.1.seen_ref = f32[1024,512]{1,0:T(8,128)S(1)} custom-call(bf16[1024,512]{1,0:T(8,128)(2,1)} %q_ref.7, bf16[1024,512]{1,0:T(8,128)(2,1)} %k_hbm.3, bf16[1024,512]{1,0:T(8,128)(2,1)} %v_hbm.3, bf16[512,512]{1,0:T(8,128)(2,1)S(1)} %collective-permute-done.tail_ref), custom_call_target="tpu_custom_call" | custom-call | tf_op jit(solution)/shard_map/window/pallas_call | solution.py:217
  76.6 0.6 apply.6
  77.2 4.2 %collective-permute-start.7 = (bf16[256,512]{1,0:T(8,128)(2,1)S(1)}, bf16[256,512]{1,0:T(8,128)(2,1)S(1)}, u32[]{:S(2)}, u32[]{:S(2)}) collective-permute-start(bf16[256,512]{1,0:T(8,128)(2,1)S(1)} %apply.6), channel_id=1, source_target_pairs={{0,3},{1,2},{2,1},{3,0},{4,7},{5,6},{6,5},{7,4},{8,11},{9,10},{10,... | collective-permute-start | bytes 786440 | tf_op jit(solution)/shard_map/ppermute | solution.py:32
  81.4 0.6 apply.5
  82.1 0.6 apply.4
  82.7 0.6 collective-permute-start.5
  83.3 0.6 apply.7.x_ref
  84.3 0.7 own_project.1
  85.0 3.7 %collective-permute-done.7.x_ref = bf16[256,512]{1,0:T(8,128)(2,1)S(1)} collective-permute-done((bf16[256,512]{1,0:T(8,128)(2,1)S(1)}, bf16[256,512]{1,0:T(8,128)(2,1)S(1)}, u32[]{:S(2)}, u32[]{:S(2)}) %collective-permute-start.7) | collective-permute-done | bytes 262176 | tf_op jit(solution)/shard_map/ppermute | solution.py:32
  88.7 0.7 project.3
  89.4 6.0 %collective-permute-done.6.x_ref = bf16[256,512]{1,0:T(8,128)(2,1)S(1)} collective-permute-done((bf16[256,512]{1,0:T(8,128)(2,1)S(1)}, bf16[256,512]{1,0:T(8,128)(2,1)S(1)}, u32[]{:S(2)}, u32[]{:S(2)}) %collective-permute-start.6) | collective-permute-done | bytes 262176 | tf_op jit(solution)/shard_map/ppermute | solution.py:32
  95.4 0.7 project.4
  96.1 8.1 %collective-permute-done.5.x_ref = bf16[256,512]{1,0:T(8,128)(2,1)S(1)} collective-permute-done((bf16[256,512]{1,0:T(8,128)(2,1)S(1)}, bf16[256,512]{1,0:T(8,128)(2,1)S(1)}, u32[]{:S(2)}, u32[]{:S(2)}) %collective-permute-start.5) | collective-permute-done | bytes 262176 | tf_op jit(solution)/shard_map/ppermute | solution.py:32
  104.2 1.5 %project.5 = bf16[256,2048]{1,0:T(8,128)(2,1)} custom-call(bf16[256,512]{1,0:T(8,128)(2,1)S(1)} %collective-permute-done.5.x_ref, f32[256,2048]{1,0:T(8,128)S(1)} %get-tuple-element.41.base_ref, f32[256,1]{1,0:T(8,128)S(1)} %get-tuple-element.42.squares_ref, bf16[2,256,1024]{2,1,0:T(8,128)(2,1)S(1)} %pile.1.near, ...), custom_call_target="tpu_custom_call" | custom-call | tf_op jit(solution)/shard_map/project/pallas_call | solution.py:345
  (31 shorter events, 2.2 us)
Async XLA Ops:
  0.0 2.2 %copy-start.5 = (f32[1024,1]{0,1:T(1,128)S(1)}, f32[1024,1]{0,1:T(1,128)}, u32[]{:S(2)}) copy-start(f32[1024,1]{0,1:T(1,128)} %param.12) | copy-start | bytes 12292
  0.0 2.3 %copy-start.6 = (bf16[512]{0:T(512)(128)(2,1)S(1)}, bf16[512]{0:T(512)(128)(2,1)}, u32[]{:S(2)}) copy-start(bf16[512]{0:T(512)(128)(2,1)} %gain_ref.3) | copy-start | bytes 3076
  7.2 2.5 %collective-permute-start.1 = (bf16[3,512,256]{2,1,0:T(8,128)(2,1)S(1)}, bf16[3,512,256]{2,1,0:T(8,128)(2,1)S(1)}, u32[]{:S(2)}, u32[]{:S(2)}) collective-permute-start(bf16[3,512,256]{2,1,0:T(8,128)(2,1)S(1)} %get-tuple-element.31), channel_id=1, source_target_pairs={{0,4},{4,0},{8,12},{12,8},{16,20},{20,16},{24,28},{28,24},{1,5},{5... | collective-permute-start | bytes 2359304 | tf_op jit(solution)/shard_map/ppermute | solution.py:32
  9.9 30.5 %collective-permute-start.2 = (bf16[3,512,256]{2,1,0:T(8,128)(2,1)S(1)}, bf16[3,512,256]{2,1,0:T(8,128)(2,1)S(1)}, u32[]{:S(2)}, u32[]{:S(2)}) collective-permute-start(bf16[3,512,256]{2,1,0:T(8,128)(2,1)S(1)} %get-tuple-element.33), channel_id=1, source_target_pairs={{0,8},{4,20},{8,0},{12,28},{16,24},{20,4},{24,16},{28,12},{1,9},{5... | collective-permute-start | bytes 2359304 | tf_op jit(solution)/shard_map/ppermute | solution.py:382
  12.8 49.7 %copy-start.2 = (bf16[1,512,512]{2,1,0:T(8,128)(2,1)S(1)}, bf16[1,512,512]{2,1,0:T(8,128)(2,1)}, u32[]{:S(2)}) copy-start(bf16[1,512,512]{2,1,0:T(8,128)(2,1)} %w1_ref.1) | copy-start | bytes 1572868
  12.8 49.7 %copy-start.3 = (bf16[1,512,512]{2,1,0:T(8,128)(2,1)S(1)}, bf16[1,512,512]{2,1,0:T(8,128)(2,1)}, u32[]{:S(2)}) copy-start(bf16[1,512,512]{2,1,0:T(8,128)(2,1)} %w2_ref.1) | copy-start | bytes 1572868
  12.8 49.7 %copy-start.4 = (bf16[1,512,512]{2,1,0:T(8,128)(2,1)S(1)}, bf16[1,512,512]{2,1,0:T(8,128)(2,1)}, u32[]{:S(2)}) copy-start(bf16[1,512,512]{2,1,0:T(8,128)(2,1)} %w3_ref.1) | copy-start | bytes 1572868
  12.8 26.0 %collective-permute-start.8 = (bf16[256,1024]{1,0:T(8,128)(2,1)S(1)}, bf16[256,1024]{1,0:T(8,128)(2,1)S(1)}, u32[]{:S(2)}, u32[]{:S(2)}) collective-permute-start(bf16[256,1024]{1,0:T(8,128)(2,1)S(1)} %get-tuple-element.38), channel_id=1, source_target_pairs={{0,2},{1,3},{2,0},{3,1},{4,6},{5,7},{6,4},{7,5},{8,10},{9,11},{10,... | collective-permute-start | bytes 1572872 | tf_op jit(solution)/shard_map/ppermute | solution.py:32
  15.4 23.6 %collective-permute-start.13 = (bf16[256,1024]{1,0:T(8,128)(2,1)S(1)}, bf16[256,1024]{1,0:T(8,128)(2,1)S(1)}, u32[]{:S(2)}, u32[]{:S(2)}) collective-permute-start(bf16[256,1024]{1,0:T(8,128)(2,1)S(1)} %get-tuple-element.38), channel_id=1, source_target_pairs={{0,1},{1,0},{2,3},{3,2},{4,5},{5,4},{6,7},{7,6},{8,9},{9,8},{10,11... | collective-permute-start | bytes 1572872 | tf_op jit(solution)/shard_map/ppermute | solution.py:32
  39.1 26.1 %collective-permute-start.15 = (bf16[2,256,1024]{2,1,0:T(8,128)(2,1)S(1)}, bf16[2,256,1024]{2,1,0:T(8,128)(2,1)S(1)}, u32[]{:S(2)}, u32[]{:S(2)}) collective-permute-start(bf16[2,256,1024]{2,1,0:T(8,128)(2,1)S(1)} %pile.1.near), channel_id=1, source_target_pairs={{0,8},{4,20},{8,0},{12,28},{16,24},{20,4},{24,16},{28,12},{1,9},{5... | collective-permute-start | bytes 3145736 | tf_op jit(solution)/shard_map/ppermute | solution.py:393
  40.7 21.9 %collective-permute-start.3 = (bf16[3,512,256]{2,1,0:T(8,128)(2,1)S(1)}, bf16[3,512,256]{2,1,0:T(8,128)(2,1)S(1)}, u32[]{:S(2)}, u32[]{:S(2)}) collective-permute-start(bf16[3,512,256]{2,1,0:T(8,128)(2,1)S(1)} %get-tuple-element.35), channel_id=1, source_target_pairs={{0,16},{4,12},{8,24},{12,4},{16,0},{20,28},{24,8},{28,20},{1,17},{... | collective-permute-start | bytes 2359304 | tf_op jit(solution)/shard_map/ppermute | solution.py:382
  41.4 12.7 %collective-permute-start.9 = (bf16[256,1024]{1,0:T(8,128)(2,1)S(1)}, bf16[256,1024]{1,0:T(8,128)(2,1)S(1)}, u32[]{:S(2)}, u32[]{:S(2)}) collective-permute-start(bf16[256,1024]{1,0:T(8,128)(2,1)S(1)} %collective-permute-done.8.refs_1_), channel_id=1, source_target_pairs={{0,1},{1,0},{2,3},{3,2},{4,5},{5,4},{6,7},{7,6},{8,9},{9,8},{10,11... | collective-permute-start | bytes 1572872 | tf_op jit(solution)/shard_map/ppermute | solution.py:32
  42.9 22.3 %collective-permute-start = (bf16[512,512]{1,0:T(8,128)(2,1)S(1)}, bf16[512,512]{1,0:T(8,128)(2,1)S(1)}, u32[]{:S(2)}, u32[]{:S(2)}) collective-permute-start(bf16[512,512]{1,0:T(8,128)(2,1)S(1)} %get-tuple-element.24), channel_id=1, source_target_pairs={{0,4},{4,8},{8,12},{12,16},{16,20},{20,24},{24,28},{1,5},{5,9},{9,... | collective-permute-start | bytes 1572872 | tf_op jit(solution)/shard_map/ppermute | solution.py:364
  54.2 18.0 %collective-permute-start.11 = (bf16[1,256,1024]{2,1,0:T(8,128)(2,1)S(1)}, bf16[1,256,1024]{2,1,0:T(8,128)(2,1)S(1)}, u32[]{:S(2)}, u32[]{:S(2)}) collective-permute-start(bf16[1,256,1024]{2,1,0:T(8,128)(2,1)S(1)} %bitcast.2), channel_id=1, source_target_pairs={{0,8},{4,20},{8,0},{12,28},{16,24},{20,4},{24,16},{28,12},{1,9},{5... | collective-permute-start | bytes 1572872 | tf_op jit(solution)/shard_map/ppermute | solution.py:393
  63.2 13.4 %copy-start = (bf16[1024,512]{1,0:T(8,128)(2,1)S(1)}, bf16[1024,512]{1,0:T(8,128)(2,1)}, u32[]{:S(2)}) copy-start(bf16[1024,512]{1,0:T(8,128)(2,1)} %q_ref.7) | copy-start | bytes 3145732
  63.2 13.3 %collective-permute-start.4 = (bf16[3,512,256]{2,1,0:T(8,128)(2,1)S(1)}, bf16[3,512,256]{2,1,0:T(8,128)(2,1)S(1)}, u32[]{:S(2)}, u32[]{:S(2)}) collective-permute-start(bf16[3,512,256]{2,1,0:T(8,128)(2,1)S(1)} %renorm.1.mine_ref), channel_id=1, source_target_pairs={{0,4},{4,0},{8,12},{12,8},{16,20},{20,16},{24,28},{28,24},{1,5},{5... | collective-permute-start | bytes 2359304 | tf_op jit(solution)/shard_map/ppermute | solution.py:32
  63.3 26.1 %collective-permute-start.14 = (bf16[2,256,1024]{2,1,0:T(8,128)(2,1)S(1)}, bf16[2,256,1024]{2,1,0:T(8,128)(2,1)S(1)}, u32[]{:S(2)}, u32[]{:S(2)}) collective-permute-start(bf16[2,256,1024]{2,1,0:T(8,128)(2,1)S(1)} %pile.1.near), channel_id=1, source_target_pairs={{0,4},{4,0},{8,12},{12,8},{16,20},{20,16},{24,28},{28,24},{1,5},{5... | collective-permute-start | bytes 3145736 | tf_op jit(solution)/shard_map/ppermute | solution.py:32
  65.2 24.2 %collective-permute-start.16 = (bf16[2,256,1024]{2,1,0:T(8,128)(2,1)S(1)}, bf16[2,256,1024]{2,1,0:T(8,128)(2,1)S(1)}, u32[]{:S(2)}, u32[]{:S(2)}) collective-permute-start(bf16[2,256,1024]{2,1,0:T(8,128)(2,1)S(1)} %collective-permute-done.15.far), channel_id=1, source_target_pairs={{0,4},{4,0},{8,12},{12,8},{16,20},{20,16},{24,28},{28,24},{1,5},{5... | collective-permute-start | bytes 3145736 | tf_op jit(solution)/shard_map/ppermute | solution.py:32
  65.2 16.8 %collective-permute-start.10 = (bf16[1,256,1024]{2,1,0:T(8,128)(2,1)S(1)}, bf16[1,256,1024]{2,1,0:T(8,128)(2,1)S(1)}, u32[]{:S(2)}, u32[]{:S(2)}) collective-permute-start(bf16[1,256,1024]{2,1,0:T(8,128)(2,1)S(1)} %bitcast.3), channel_id=1, source_target_pairs={{0,4},{4,0},{8,12},{12,8},{16,20},{20,16},{24,28},{28,24},{1,5},{5... | collective-permute-start | bytes 1572872 | tf_op jit(solution)/shard_map/ppermute | solution.py:32
  72.2 10.5 %collective-permute-start.12 = (bf16[1,256,1024]{2,1,0:T(8,128)(2,1)S(1)}, bf16[1,256,1024]{2,1,0:T(8,128)(2,1)S(1)}, u32[]{:S(2)}, u32[]{:S(2)}) collective-permute-start(bf16[1,256,1024]{2,1,0:T(8,128)(2,1)S(1)} %collective-permute-done.11.far), channel_id=1, source_target_pairs={{0,4},{4,0},{8,12},{12,8},{16,20},{20,16},{24,28},{28,24},{1,5},{5... | collective-permute-start | bytes 1572872 | tf_op jit(solution)/shard_map/ppermute | solution.py:32
  77.2 11.5 %collective-permute-start.7 = (bf16[256,512]{1,0:T(8,128)(2,1)S(1)}, bf16[256,512]{1,0:T(8,128)(2,1)S(1)}, u32[]{:S(2)}, u32[]{:S(2)}) collective-permute-start(bf16[256,512]{1,0:T(8,128)(2,1)S(1)} %apply.6), channel_id=1, source_target_pairs={{0,3},{1,2},{2,1},{3,0},{4,7},{5,6},{6,5},{7,4},{8,11},{9,10},{10,... | collective-permute-start | bytes 786440 | tf_op jit(solution)/shard_map/ppermute | solution.py:32
  82.0 13.4 %collective-permute-start.6 = (bf16[256,512]{1,0:T(8,128)(2,1)S(1)}, bf16[256,512]{1,0:T(8,128)(2,1)S(1)}, u32[]{:S(2)}, u32[]{:S(2)}) collective-permute-start(bf16[256,512]{1,0:T(8,128)(2,1)S(1)} %apply.5), channel_id=1, source_target_pairs={{0,1},{1,0},{2,3},{3,2},{4,5},{5,4},{6,7},{7,6},{8,9},{9,8},{10,11... | collective-permute-start | bytes 786440 | tf_op jit(solution)/shard_map/ppermute | solution.py:32
  82.7 1.6 %copy-start.1 = (bf16[512,2048]{1,0:T(8,128)(2,1)S(1)}, bf16[512,2048]{1,0:T(8,128)(2,1)}, u32[]{:S(2)}) copy-start(bf16[512,2048]{1,0:T(8,128)(2,1)} %w_ref.1) | copy-start | bytes 6291460
  82.7 21.5 %collective-permute-start.5 = (bf16[256,512]{1,0:T(8,128)(2,1)S(1)}, bf16[256,512]{1,0:T(8,128)(2,1)S(1)}, u32[]{:S(2)}, u32[]{:S(2)}) collective-permute-start(bf16[256,512]{1,0:T(8,128)(2,1)S(1)} %apply.4), channel_id=1, source_target_pairs={{0,2},{1,3},{2,0},{3,1},{4,6},{5,7},{6,4},{7,5},{8,10},{9,11},{10,... | collective-permute-start | bytes 786440 | tf_op jit(solution)/shard_map/ppermute | solution.py:32

commit v4 on v3

--- a/solution.py
+++ b/solution.py
@@ -48,44 +48,56 @@
     return jnp.concatenate([tall] * (width // 128), axis=1)
 
 
-def load_kernel(k_hbm, v_hbm, w1_hbm, w2_hbm, w3_hbm, tail_ref, k_ref, v_ref, w1_ref, w2_ref, w3_ref, sem):
+def load_kernel(k_hbm, v_hbm, w1_hbm, w2_hbm, w3_hbm, gain_hbm, w_hbm,
+                tail_ref, piece_ref, k_ref, v_ref, w1_ref, w2_ref, w3_ref, w_ref, gain_ref, sem):
+    rows, columns = piece_ref.shape
+    core, side = place()
+    first = pl.multiple_of(side * rows, rows)
+    left = pl.multiple_of(core * columns, columns)
     last = pl.ds(k_hbm.shape[0] - WINDOW, WINDOW)
-    moves = [(k_hbm.at[last, :], tail_ref.at[pl.ds(0, WINDOW), :])]
+    moves = [(gain_hbm, gain_ref), (w_hbm.at[pl.ds(first, rows), pl.ds(left, columns)], w_ref)]
+    moves += [(k_hbm.at[last, :], tail_ref.at[pl.ds(0, WINDOW), :])]
     moves += [(v_hbm.at[last, :], tail_ref.at[pl.ds(WINDOW, WINDOW), :])]
     moves += [(w1_hbm, w1_ref), (w3_hbm, w3_ref), (k_hbm, k_ref), (v_hbm, v_ref), (w2_hbm, w2_ref)]
     copies = [pltpu.make_async_copy(src, dst, sem.at[j]) for j, (src, dst) in enumerate(moves)]
     for copy in copies:
         copy.start()
-    for copy in copies:
+    copies[0].wait()
+    gain = gain_ref[...].reshape(1, 2 * rows).astype(jnp.float32)
+    gain = column(jnp.where(side == 0, gain[:, :rows], gain[:, rows:]), columns)
+    copies[1].wait()
+    piece_ref[...] = (w_ref[...].astype(jnp.float32) * gain).astype(jnp.bfloat16)
+    for copy in copies[2:]:
         copy.wait()
 
 
-def load(keys, values, w1, w2, w3):
+def load(keys, values, w1, w2, w3, gain, weight):
     arrays = (keys, values, w1, w2, w3)
+    piece = pltpu.VMEM((weight.shape[0] // 2, weight.shape[1] // 2), jnp.bfloat16)
     return pl.pallas_call(
         load_kernel,
-        out_shape=[pltpu.VMEM((2 * WINDOW, keys.shape[1]), jnp.bfloat16)]
+        out_shape=[pltpu.VMEM((2 * WINDOW, keys.shape[1]), jnp.bfloat16), piece]
         + [pltpu.VMEM(a.shape, a.dtype) for a in arrays],
-        compiler_params=grant(4),
-        in_specs=[HBM] * 5,
-        out_specs=[VMEM] * 6,
-        scratch_shapes=[pltpu.SemaphoreType.DMA((7,))],
+        compiler_params=grant(8),
+        in_specs=[HBM] * 7,
+        out_specs=[VMEM] * 7,
+        scratch_shapes=[piece, pltpu.VMEM(gain.shape, gain.dtype), pltpu.SemaphoreType.DMA((9,))],
         name="load",
-    )(*far_core(*arrays))
-
-
-def push_kernel(k_ref, v_ref, r_ref, w1_ref, w2_ref, w3_ref, gain_ref, w_hbm,
-                give_ref, keep_ref, piece_ref, act_ref, g1_ref, g3_ref, sc_ref, w_ref, sem):
+    )(*far_core(*arrays, gain, weight))
+
+
+def halves(width):
+    core, _ = place()
+    half = width // 2
+    mine = pl.ds(pl.multiple_of(core * half, half), half)
+    theirs = pl.ds(pl.multiple_of((1 - core) * half, half), half)
+    return mine, theirs
+
+
+def push_kernel(k_ref, v_ref, r_ref, w1_ref, w2_ref, w3_ref, give_ref, act_ref, sc_ref, g1_ref, g3_ref):
     rows, width = k_ref.shape
-    piece_rows, columns = piece_ref.shape
-    core, side = place()
-    first = pl.multiple_of(side * piece_rows, piece_rows)
-    left = pl.multiple_of(core * columns, columns)
-    load = pltpu.make_async_copy(w_hbm.at[pl.ds(first, piece_rows), pl.ds(left, columns)], w_ref, sem)
-    load.start()
     steps = 4
     block = rows // steps
-    half = width // 2
     for i in range(steps):
         at = slice(i * block, (i + 1) * block)
         k = k_ref[at, :]
@@ -100,79 +112,96 @@
         sc_ref[at, :] = scaled
         g1_ref[at, :] = (back * up * (s + gs * (1.0 - s))).astype(jnp.bfloat16)
         g3_ref[at, :] = (back * gs).astype(jnp.bfloat16)
-    load.wait()
-    gain = gain_ref[...].reshape(1, width).astype(jnp.float32)
-    gain = jnp.where(side == 0, gain[:, :piece_rows], gain[:, piece_rows:])
-    piece_ref[...] = (w_ref[...].astype(jnp.float32) * column(gain, columns)).astype(jnp.bfloat16)
-    theirs = pl.ds(pl.multiple_of((1 - core) * half, half), half)
-    mine = pl.ds(pl.multiple_of(core * half, half), half)
+    _, theirs = halves(width)
     for j, (left, right) in enumerate([(k_ref, g1_ref), (act_ref, sc_ref), (k_ref, g3_ref)]):
-        left = left[...]
-        give_ref[j] = dot(left, right[:, theirs], 0, 0).astype(jnp.bfloat16)
-        keep_ref[j] = dot(left, right[:, mine], 0, 0)
-
-
-def pushes(keys, values, rates, w1, w2, w3, gain, weight):
+        give_ref[j] = dot(left[...], right[:, theirs], 0, 0).astype(jnp.bfloat16)
+
+
+def pushes(keys, values, rates, w1, w2, w3):
     rows, width = keys.shape
-    half = width // 2
     wide = pltpu.VMEM((rows, width), jnp.bfloat16)
-    piece = pltpu.VMEM((weight.shape[0] // 2, weight.shape[1] // 2), jnp.bfloat16)
     return pl.pallas_call(
         push_kernel,
-        out_shape=(
-            pltpu.VMEM((3, width, half), jnp.bfloat16),
-            pltpu.VMEM((3, width, half), jnp.float32),
-            piece,
-        ),
+        out_shape=[pltpu.VMEM((3, width, width // 2), jnp.bfloat16)] + [wide] * 4,
         compiler_params=grant(16),
-        in_specs=[VMEM] * 7 + [HBM],
-        out_specs=(VMEM,) * 3,
-        scratch_shapes=[wide] * 4 + [piece, pltpu.SemaphoreType.DMA],
+        in_specs=[VMEM] * 6,
+        out_specs=[VMEM] * 5,
         name="pushes",
-    )(*near_core(keys, values, rates.reshape(1, rows), w1, w2, w3, gain), *far_core(weight))
-
-
-def add_kernel(keep_ref, got_ref, sum_ref, send_ref):
+    )(*near_core(keys, values, rates.reshape(1, rows), w1, w2, w3))
+
+
+def keep_kernel(k_ref, act_ref, sc_ref, g1_ref, g3_ref, keep_ref):
+    mine, _ = halves(k_ref.shape[1])
+    for j, (left, right) in enumerate([(k_ref, g1_ref), (act_ref, sc_ref), (k_ref, g3_ref)]):
+        keep_ref[j] = dot(left[...], right[:, mine], 0, 0)
+
+
+def kept(*arrays):
+    width = arrays[0].shape[1]
+    return pl.pallas_call(
+        keep_kernel,
+        out_shape=pltpu.VMEM((3, width, width // 2), jnp.float32),
+        compiler_params=grant(16),
+        in_specs=[VMEM] * 5,
+        out_specs=VMEM,
+        name="kept",
+    )(*near_core(*arrays))
+
+
+def first_add_kernel(keep_ref, got_ref, sum_ref, a_ref, b_ref):
+    quarter = a_ref.shape[2]
     total = keep_ref[...] + got_ref[...].astype(jnp.float32)
     sum_ref[...] = total
-    send_ref[...] = total.astype(jnp.bfloat16)
-
-
-def add(keep, got):
-    return pl.pallas_call(
-        add_kernel,
-        out_shape=(pltpu.VMEM(keep.shape, jnp.float32), pltpu.VMEM(keep.shape, jnp.bfloat16)),
+    a_ref[...] = total[:, :, :quarter].astype(jnp.bfloat16)
+    b_ref[...] = total[:, :, quarter:].astype(jnp.bfloat16)
+
+
+def later_add_kernel(keep_ref, got_a_ref, got_b_ref, sum_ref, a_ref, b_ref):
+    quarter = a_ref.shape[2]
+    first = keep_ref[:, :, :quarter] + got_a_ref[...].astype(jnp.float32)
+    second = keep_ref[:, :, quarter:] + got_b_ref[...].astype(jnp.float32)
+    sum_ref[:, :, :quarter] = first
+    sum_ref[:, :, quarter:] = second
+    a_ref[...] = first.astype(jnp.bfloat16)
+    b_ref[...] = second.astype(jnp.bfloat16)
+
+
+def add(keep, *got):
+    stream = pltpu.VMEM(keep.shape[:2] + (keep.shape[2] // 2,), jnp.bfloat16)
+    return pl.pallas_call(
+        first_add_kernel if len(got) == 1 else later_add_kernel,
+        out_shape=(pltpu.VMEM(keep.shape, jnp.float32), stream, stream),
         compiler_params=grant(8),
-        in_specs=[VMEM] * 2,
-        out_specs=(VMEM,) * 2,
+        in_specs=[VMEM] * (1 + len(got)),
+        out_specs=(VMEM,) * 3,
         name="add",
-    )(*near_core(keep, got))
-
-
-def renorm_kernel(keep_ref, got_ref, w1_ref, w2_ref, w3_ref, out_ref):
-    _, half = got_ref.shape[1:]
-    block = 128
+    )(*near_core(keep, *got))
+
+
+def renorm_kernel(keep_ref, got_a_ref, got_b_ref, w1_ref, w2_ref, w3_ref, out_ref):
+    half = keep_ref.shape[2]
+    block = got_a_ref.shape[2]
     core, _ = place()
     for j, w_ref in enumerate((w1_ref, w2_ref, w3_ref)):
-        for first in range(0, half, block):
+        for first, got_ref in ((0, got_a_ref), (block, got_b_ref)):
             at = slice(first, first + block)
             start = pl.multiple_of(core * half + first, block)
             old = w_ref[0, :, pl.ds(start, block)].astype(jnp.float32)
-            new = old + (keep_ref[j, :, at] + got_ref[j, :, at].astype(jnp.float32))
+            new = old + (keep_ref[j, :, at] + got_ref[j].astype(jnp.float32))
             old_norm = jnp.sqrt(jnp.mean(old * old, axis=0, keepdims=True) + EPSILON)
             new_norm = jnp.sqrt(jnp.mean(new * new, axis=0, keepdims=True) + EPSILON)
             out_ref[j, :, at] = (new * (old_norm / new_norm)).astype(jnp.bfloat16)
 
 
-def renorm(keep, got, w1, w2, w3):
+def renorm(keep, *others):
     return pl.pallas_call(
         renorm_kernel,
         out_shape=pltpu.VMEM(keep.shape, jnp.bfloat16),
         compiler_params=grant(8),
-        in_specs=[VMEM] * 5,
+        in_specs=[VMEM] * 6,
         out_specs=VMEM,
         name="renorm",
-    )(*near_core(keep, got, w1, w2, w3))
+    )(*near_core(keep, *others))
 
 
 def window_kernel(q_hbm, k_hbm, v_hbm, tail_ref, out_ref, q_ref, k_ref, v_ref, sem):
@@ -360,27 +389,26 @@
     bits = ctx_count.bit_length() - 1
     assert ctx_count == 1 << bits and bits >= 3
 
-    tail, *loaded = load(keys, values, fast_w1, fast_w2, fast_w3)
+    tail, piece, k_near, *loaded = load(
+        keys, values, fast_w1, fast_w2, fast_w3, norm_gain, out_weight
+    )
     tail = lax.ppermute(tail, "ctx", [(i, i + 1) for i in range(ctx_count - 1)])
-    give, keep, piece = pushes(
-        loaded[0], loaded[1], rates, *loaded[2:], norm_gain, out_weight
-    )
-    got = swap(give, "ctx", 1)
 
     near = {0: piece}
     for level in reversed(range(heads.bit_length() - 1)):
         for k in sorted(near):
             near[k | 1 << level] = swap(near[k], "head", 1 << level)
 
+    give, *factors = pushes(k_near, loaded[0], rates, *loaded[1:])
+    got = [swap(give, "ctx", 1)]
+    keep = kept(k_near, *factors)
+
     masks = [1 << b for b in range(1, bits)]
-    crossing = [
-        [(i, i ^ (backward if i & 1 else forward)) for i in range(ctx_count)]
-        for forward, backward in zip(masks, masks[::-1])
-    ]
-    for pairs in crossing:
-        keep, send = add(keep, got)
-        got = lax.ppermute(send, "ctx", pairs)
-    mine = renorm(keep, got, fast_w1, fast_w2, fast_w3)
+    for forward, backward in zip(masks, masks[::-1]):
+        keep, first, second = add(keep, *got)
+        got = [swap(first, "ctx", forward)]
+        got.append(swap(second, "ctx", backward))
+    mine = renorm(keep, *got, fast_w1, fast_w2, fast_w3)
     other = swap(mine, "ctx", 1)
 
     seen = window(queries, keys, values, tail)

time: 106 us -> 113 us (1.066)
  starting transfers between devices: 21.1 us -> 25.3 us
  waiting for transfers between devices: 65.3 us -> 68.8 us
    ppermute x12 -> x16, waiting for transfers between devices: 51.4 us -> 65.2 us  [swap(): lax.ppermute(value, axis, [(i, i ^ mask) for i in range(lax.axis_size(axi...]
    ppermute x2 -> x0, waiting for transfers between devices: 8.05 us -> none  [step(): got = lax.ppermute(send, 'ctx', pairs)]
    ppermute x12 -> x16, starting transfers between devices: 14.2 us -> 20.9 us  [swap(): lax.ppermute(value, axis, [(i, i ^ mask) for i in range(lax.axis_size(axi...]
    ppermute x2 -> x0, starting transfers between devices: 3.68 us -> none  [step(): got = lax.ppermute(send, 'ctx', pairs)]
    ppermute x2, waiting for transfers between devices: 5.84 us -> 3.62 us  [step(): far = lax.ppermute(group, 'ctx', cross)]
    pallas_call x3 -> x4, Pallas kernels: 5.38 us -> 4.89 us  [the longest x1 3.42 us: pushes(): pl.pallas_call(push_kernel, out_shape=[pltpu.VMEM((3, width, width // 2),...]
  transfers between devices with their start and end apart: 17 -> 19, of which waited for: 10 -> 8; matrix products, arithmetic and copies ran while one was open for 0% -> 0% of each run, Pallas kernels for 9% -> 10%
where the time goes in v4:
time: 113 us
  waiting for transfers between devices  68.8 us (61%)
  starting transfers between devices  25.3 us (22%)
  Pallas kernels  18.4 us (16%)
    ppermute x16, waiting for transfers between devices, swap(): lax.ppermute(value, axis, [(i, i ^ mask) for i in range(lax.axis_size(axi...  65.2 us
    ppermute x16, starting transfers between devices, swap(): lax.ppermute(value, axis, [(i, i ^ mask) for i in range(lax.axis_size(axi...  20.9 us
    pallas_call x1, Pallas kernels, window(): pl.pallas_call(window_kernel, out_shape=pltpu.VMEM(queries.shape, jnp.flo...  4.36 us
    ppermute x2, waiting for transfers between devices, step(): far = lax.ppermute(group, 'ctx', cross)  3.62 us
    pallas_call x1, Pallas kernels, pushes(): pl.pallas_call(push_kernel, out_shape=[pltpu.VMEM((3, width, width // 2),...  3.42 us
    pallas_call x3, Pallas kernels, project(): pl.pallas_call(functools.partial(project_kernel, index, scale_by), out_sh...  3.01 us
    ppermute x2, starting transfers between devices, step(): far = lax.ppermute(group, 'ctx', cross)  2.84 us
    pallas_call x1, Pallas kernels, load(): pl.pallas_call(load_kernel, out_shape=[pltpu.VMEM((2 * WINDOW, keys.shape...  2.41 us
  transfers between devices with their start and end apart: 19, of which 8 were waited for; matrix products, arithmetic and copies ran while one was open for 0% of the time, Pallas kernels for 10%

profile of v4, /device:TPU:0, one launch (start us, length us, event | category | flops | bytes accessed | tf_op | source)
XLA Modules:
  0.0 113.2 jit_solution(18156590499151326905)
XLA Ops:
  0.0 2.4 %load.1 = (bf16[512,512]{1,0:T(8,128)(2,1)S(1)}, bf16[256,1024]{1,0:T(8,128)(2,1)S(1)}, bf16[1024,512]{1,0:T(8,128)(2,1)S(1)}, bf16[1024,512]{1,0:T(8,128)(2,1)S...) custom-call(bf16[1024,512]{1,0:T(8,128)(2,1)} %k_hbm.3, ...), custom_call_target="tpu_custom_call" | custom-call | tf_op jit(solution)/shard_map/load/pallas_call | solution.py:77
  2.4 3.4 %pushes.1 = (bf16[3,512,256]{2,1,0:T(8,128)(2,1)S(1)}, bf16[1024,512]{1,0:T(8,128)(2,1)S(1)}, bf16[1024,512]{1,0:T(8,128)(2,1)S(1)}, bf16[1024,512]{1,0:T(8,128)(2,1)S(1)}, bf16[1024,512]{1,0:T(8,128)(2,1)S(1)}) custom-call(bf16[1024,512]{1,0:T(8,128)(2,1)S(1)} %get-tuple-element.30.k_ref, bf16[1024,512]{1,0:T(8,128)(2,1)S(1)} %get-tuple-element.31.v_ref, ...), custom_call_target="tpu_custom_call" | custom-call | tf_op jit(solution)/shard_map/pushes/pallas_call | solution.py:123
  5.9 0.6 collective-permute-start.1
  6.4 3.6 %collective-permute-start.10 = (bf16[256,1024]{1,0:T(8,128)(2,1)S(1)}, bf16[256,1024]{1,0:T(8,128)(2,1)S(1)}, u32[]{:S(2)}, u32[]{:S(2)}) collective-permute-start(bf16[256,1024]{1,0:T(8,128)(2,1)S(1)} %get-tuple-element.48), channel_id=1, source_target_pairs={{0,2},{1,3},{2,0},{3,1},{4,6},{5,7},{6,4},{7,5},{8,10},{9,11},{10,... | collective-permute-start | bytes 1572872 | tf_op jit(solution)/shard_map/ppermute | solution.py:32
  10.1 1.6 %collective-permute-start.15 = (bf16[256,1024]{1,0:T(8,128)(2,1)S(1)}, bf16[256,1024]{1,0:T(8,128)(2,1)S(1)}, u32[]{:S(2)}, u32[]{:S(2)}) collective-permute-start(bf16[256,1024]{1,0:T(8,128)(2,1)S(1)} %get-tuple-element.48), channel_id=1, source_target_pairs={{0,1},{1,0},{2,3},{3,2},{4,5},{5,4},{6,7},{7,6},{8,9},{9,8},{10,11... | collective-permute-start | bytes 1572872 | tf_op jit(solution)/shard_map/ppermute | solution.py:32
  11.6 22.3 %collective-permute-done.10.refs_1_ = bf16[256,1024]{1,0:T(8,128)(2,1)S(1)} collective-permute-done((bf16[256,1024]{1,0:T(8,128)(2,1)S(1)}, bf16[256,1024]{1,0:T(8,128)(2,1)S(1)}, u32[]{:S(2)}, u32[]{:S(2)}) %collective-permute-start.10) | collective-permute-done | bytes 524320 | tf_op jit(solution)/shard_map/ppermute | solution.py:32
  34.2 1.6 %collective-permute-start.17 = (bf16[2,256,1024]{2,1,0:T(8,128)(2,1)S(1)}, bf16[2,256,1024]{2,1,0:T(8,128)(2,1)S(1)}, u32[]{:S(2)}, u32[]{:S(2)}) collective-permute-start(bf16[2,256,1024]{2,1,0:T(8,128)(2,1)S(1)} %pile.1.near), channel_id=1, source_target_pairs={{0,8},{4,20},{8,0},{12,28},{16,24},{20,4},{24,16},{28,12},{1,9},{5... | collective-permute-start | bytes 3145736 | tf_op jit(solution)/shard_map/ppermute | solution.py:421
  35.8 1.0 kept.1.keep_ref
  37.7 1.6 %collective-permute-start.3 = (bf16[3,512,128]{2,1,0:T(8,128)(2,1)S(1)}, bf16[3,512,128]{2,1,0:T(8,128)(2,1)S(1)}, u32[]{:S(2)}, u32[]{:S(2)}) collective-permute-start(bf16[3,512,128]{2,1,0:T(8,128)(2,1)S(1)} %get-tuple-element.42), channel_id=1, source_target_pairs={{0,16},{4,20},{8,24},{12,28},{16,0},{20,4},{24,8},{28,12},{1,17},{... | collective-permute-start | bytes 1179656 | tf_op jit(solution)/shard_map/ppermute | solution.py:32
  39.3 1.4 %collective-permute-start.11 = (bf16[256,1024]{1,0:T(8,128)(2,1)S(1)}, bf16[256,1024]{1,0:T(8,128)(2,1)S(1)}, u32[]{:S(2)}, u32[]{:S(2)}) collective-permute-start(bf16[256,1024]{1,0:T(8,128)(2,1)S(1)} %collective-permute-done.10.refs_1_), channel_id=1, source_target_pairs={{0,1},{1,0},{2,3},{3,2},{4,5},{5,4},{6,7},{7,6},{8,9},{9,8},{10,11... | collective-permute-start | bytes 1572872 | tf_op jit(solution)/shard_map/ppermute | solution.py:32
  40.7 16.8 %collective-permute-done.2.got_a_ref = bf16[3,512,128]{2,1,0:T(8,128)(2,1)S(1)} collective-permute-done((bf16[3,512,128]{2,1,0:T(8,128)(2,1)S(1)}, bf16[3,512,128]{2,1,0:T(8,128)(2,1)S(1)}, u32[]{:S(2)}, u32[]{:S(2)}) %collective-permute-start.2) | collective-permute-done | bytes 393248 | tf_op jit(solution)/shard_map/ppermute | solution.py:32
  57.7 1.6 %collective-permute-start.4 = (bf16[3,512,128]{2,1,0:T(8,128)(2,1)S(1)}, bf16[3,512,128]{2,1,0:T(8,128)(2,1)S(1)}, u32[]{:S(2)}, u32[]{:S(2)}) collective-permute-start(bf16[3,512,128]{2,1,0:T(8,128)(2,1)S(1)} %get-tuple-element.44), channel_id=1, source_target_pairs={{0,16},{4,20},{8,24},{12,28},{16,0},{20,4},{24,8},{28,12},{1,17},{... | collective-permute-start | bytes 1179656 | tf_op jit(solution)/shard_map/ppermute | solution.py:32
  59.4 1.5 %collective-permute-start.5 = (bf16[3,512,128]{2,1,0:T(8,128)(2,1)S(1)}, bf16[3,512,128]{2,1,0:T(8,128)(2,1)S(1)}, u32[]{:S(2)}, u32[]{:S(2)}) collective-permute-start(bf16[3,512,128]{2,1,0:T(8,128)(2,1)S(1)} %get-tuple-element.45), channel_id=1, source_target_pairs={{0,8},{4,12},{8,0},{12,4},{16,24},{20,28},{24,16},{28,20},{1,9},{5... | collective-permute-start | bytes 1179656 | tf_op jit(solution)/shard_map/ppermute | solution.py:32
  60.8 1.5 %collective-permute-start = (bf16[512,512]{1,0:T(8,128)(2,1)S(1)}, bf16[512,512]{1,0:T(8,128)(2,1)S(1)}, u32[]{:S(2)}, u32[]{:S(2)}) collective-permute-start(bf16[512,512]{1,0:T(8,128)(2,1)S(1)} %get-tuple-element.29), channel_id=1, source_target_pairs={{0,4},{4,8},{8,12},{12,16},{16,20},{20,24},{24,28},{1,5},{5,9},{9,... | collective-permute-start | bytes 1572872 | tf_op jit(solution)/shard_map/ppermute | solution.py:395
  62.3 1.2 %collective-permute-start.13 = (bf16[1,256,1024]{2,1,0:T(8,128)(2,1)S(1)}, bf16[1,256,1024]{2,1,0:T(8,128)(2,1)S(1)}, u32[]{:S(2)}, u32[]{:S(2)}) collective-permute-start(bf16[1,256,1024]{2,1,0:T(8,128)(2,1)S(1)} %bitcast.2), channel_id=1, source_target_pairs={{0,8},{4,20},{8,0},{12,28},{16,24},{20,4},{24,16},{28,12},{1,9},{5... | collective-permute-start | bytes 1572872 | tf_op jit(solution)/shard_map/ppermute | solution.py:421
  63.6 8.2 %collective-permute-done.4.got_a_ref = bf16[3,512,128]{2,1,0:T(8,128)(2,1)S(1)} collective-permute-done((bf16[3,512,128]{2,1,0:T(8,128)(2,1)S(1)}, bf16[3,512,128]{2,1,0:T(8,128)(2,1)S(1)}, u32[]{:S(2)}, u32[]{:S(2)}) %collective-permute-start.4) | collective-permute-done | bytes 393248 | tf_op jit(solution)/shard_map/ppermute | solution.py:32
  71.8 0.6 renorm.1.mine_ref
  73.1 3.1 %collective-permute-start.12 = (bf16[1,256,1024]{2,1,0:T(8,128)(2,1)S(1)}, bf16[1,256,1024]{2,1,0:T(8,128)(2,1)S(1)}, u32[]{:S(2)}, u32[]{:S(2)}) collective-permute-start(bf16[1,256,1024]{2,1,0:T(8,128)(2,1)S(1)} %bitcast.3), channel_id=1, source_target_pairs={{0,4},{4,0},{8,12},{12,8},{16,20},{20,16},{24,28},{28,24},{1,5},{5... | collective-permute-start | bytes 1572872 | tf_op jit(solution)/shard_map/ppermute | solution.py:32
  76.2 3.6 %collective-permute-done.13.far = bf16[1,256,1024]{2,1,0:T(8,128)(2,1)S(1)} collective-permute-done((bf16[1,256,1024]{2,1,0:T(8,128)(2,1)S(1)}, bf16[1,256,1024]{2,1,0:T(8,128)(2,1)S(1)}, u32[]{:S(2)}, u32[]{:S(2)}) %collective-permute-start.13) | collective-permute-done | bytes 524320 | tf_op jit(solution)/shard_map/ppermute | solution.py:421
  79.8 4.4 %window.1.seen_ref = f32[1024,512]{1,0:T(8,128)S(1)} custom-call(bf16[1024,512]{1,0:T(8,128)(2,1)} %q_ref.7, bf16[1024,512]{1,0:T(8,128)(2,1)} %k_hbm.3, bf16[1024,512]{1,0:T(8,128)(2,1)} %v_hbm.3, bf16[512,512]{1,0:T(8,128)(2,1)S(1)} %collective-permute-done.tail_ref), custom_call_target="tpu_custom_call" | custom-call | tf_op jit(solution)/shard_map/window/pallas_call | solution.py:246
  84.2 0.6 apply.6
  84.8 4.0 %collective-permute-start.9 = (bf16[256,512]{1,0:T(8,128)(2,1)S(1)}, bf16[256,512]{1,0:T(8,128)(2,1)S(1)}, u32[]{:S(2)}, u32[]{:S(2)}) collective-permute-start(bf16[256,512]{1,0:T(8,128)(2,1)S(1)} %apply.6), channel_id=1, source_target_pairs={{0,3},{1,2},{2,1},{3,0},{4,7},{5,6},{6,5},{7,4},{8,11},{9,10},{10,... | collective-permute-start | bytes 786440 | tf_op jit(solution)/shard_map/ppermute | solution.py:32
  88.8 0.6 apply.5
  89.5 0.6 apply.4
  90.1 0.6 collective-permute-start.7
  91.7 0.7 own_project.1
  92.4 3.7 %collective-permute-done.9.x_ref = bf16[256,512]{1,0:T(8,128)(2,1)S(1)} collective-permute-done((bf16[256,512]{1,0:T(8,128)(2,1)S(1)}, bf16[256,512]{1,0:T(8,128)(2,1)S(1)}, u32[]{:S(2)}, u32[]{:S(2)}) %collective-permute-start.9) | collective-permute-done | bytes 262176 | tf_op jit(solution)/shard_map/ppermute | solution.py:32
  96.1 0.7 project.3
  96.8 6.0 %collective-permute-done.8.x_ref = bf16[256,512]{1,0:T(8,128)(2,1)S(1)} collective-permute-done((bf16[256,512]{1,0:T(8,128)(2,1)S(1)}, bf16[256,512]{1,0:T(8,128)(2,1)S(1)}, u32[]{:S(2)}, u32[]{:S(2)}) %collective-permute-start.8) | collective-permute-done | bytes 262176 | tf_op jit(solution)/shard_map/ppermute | solution.py:32
  102.8 0.7 project.4
  103.5 8.0 %collective-permute-done.7.x_ref = bf16[256,512]{1,0:T(8,128)(2,1)S(1)} collective-permute-done((bf16[256,512]{1,0:T(8,128)(2,1)S(1)}, bf16[256,512]{1,0:T(8,128)(2,1)S(1)}, u32[]{:S(2)}, u32[]{:S(2)}) %collective-permute-start.7) | collective-permute-done | bytes 262176 | tf_op jit(solution)/shard_map/ppermute | solution.py:32
  111.6 1.5 %project.5 = bf16[256,2048]{1,0:T(8,128)(2,1)} custom-call(bf16[256,512]{1,0:T(8,128)(2,1)S(1)} %collective-permute-done.7.x_ref, f32[256,2048]{1,0:T(8,128)S(1)} %get-tuple-element.51.base_ref, f32[256,1]{1,0:T(8,128)S(1)} %get-tuple-element.52.squares_ref, bf16[2,256,1024]{2,1,0:T(8,128)(2,1)S(1)} %pile.1.near, ...), custom_call_target="tpu_custom_call" | custom-call | tf_op jit(solution)/shard_map/project/pallas_call | solution.py:374
  (36 shorter events, 3.0 us)
Async XLA Ops:
  0.0 2.4 %copy-start.6 = (f32[1024,1]{0,1:T(1,128)S(1)}, f32[1024,1]{0,1:T(1,128)}, u32[]{:S(2)}) copy-start(f32[1024,1]{0,1:T(1,128)} %param.12) | copy-start | bytes 12292
  5.9 31.0 %collective-permute-start.1 = (bf16[3,512,256]{2,1,0:T(8,128)(2,1)S(1)}, bf16[3,512,256]{2,1,0:T(8,128)(2,1)S(1)}, u32[]{:S(2)}, u32[]{:S(2)}) collective-permute-start(bf16[3,512,256]{2,1,0:T(8,128)(2,1)S(1)} %get-tuple-element.39), channel_id=1, source_target_pairs={{0,4},{4,0},{8,12},{12,8},{16,20},{20,16},{24,28},{28,24},{1,5},{5... | collective-permute-start | bytes 2359304 | tf_op jit(solution)/shard_map/ppermute | solution.py:32
  6.4 27.5 %collective-permute-start.10 = (bf16[256,1024]{1,0:T(8,128)(2,1)S(1)}, bf16[256,1024]{1,0:T(8,128)(2,1)S(1)}, u32[]{:S(2)}, u32[]{:S(2)}) collective-permute-start(bf16[256,1024]{1,0:T(8,128)(2,1)S(1)} %get-tuple-element.48), channel_id=1, source_target_pairs={{0,2},{1,3},{2,0},{3,1},{4,6},{5,7},{6,4},{7,5},{8,10},{9,11},{10,... | collective-permute-start | bytes 1572872 | tf_op jit(solution)/shard_map/ppermute | solution.py:32
  10.1 24.0 %collective-permute-start.15 = (bf16[256,1024]{1,0:T(8,128)(2,1)S(1)}, bf16[256,1024]{1,0:T(8,128)(2,1)S(1)}, u32[]{:S(2)}, u32[]{:S(2)}) collective-permute-start(bf16[256,1024]{1,0:T(8,128)(2,1)S(1)} %get-tuple-element.48), channel_id=1, source_target_pairs={{0,1},{1,0},{2,3},{3,2},{4,5},{5,4},{6,7},{7,6},{8,9},{9,8},{10,11... | collective-permute-start | bytes 1572872 | tf_op jit(solution)/shard_map/ppermute | solution.py:32
  34.2 38.8 %collective-permute-start.17 = (bf16[2,256,1024]{2,1,0:T(8,128)(2,1)S(1)}, bf16[2,256,1024]{2,1,0:T(8,128)(2,1)S(1)}, u32[]{:S(2)}, u32[]{:S(2)}) collective-permute-start(bf16[2,256,1024]{2,1,0:T(8,128)(2,1)S(1)} %pile.1.near), channel_id=1, source_target_pairs={{0,8},{4,20},{8,0},{12,28},{16,24},{20,4},{24,16},{28,12},{1,9},{5... | collective-permute-start | bytes 3145736 | tf_op jit(solution)/shard_map/ppermute | solution.py:421
  36.9 34.9 %copy-start.2 = (bf16[1,512,512]{2,1,0:T(8,128)(2,1)S(1)}, bf16[1,512,512]{2,1,0:T(8,128)(2,1)}, u32[]{:S(2)}) copy-start(bf16[1,512,512]{2,1,0:T(8,128)(2,1)} %w1_ref.1) | copy-start | bytes 1572868
  36.9 34.9 %copy-start.3 = (bf16[1,512,512]{2,1,0:T(8,128)(2,1)S(1)}, bf16[1,512,512]{2,1,0:T(8,128)(2,1)}, u32[]{:S(2)}) copy-start(bf16[1,512,512]{2,1,0:T(8,128)(2,1)} %w2_ref.1) | copy-start | bytes 1572868
  36.9 34.9 %copy-start.4 = (bf16[1,512,512]{2,1,0:T(8,128)(2,1)S(1)}, bf16[1,512,512]{2,1,0:T(8,128)(2,1)}, u32[]{:S(2)}) copy-start(bf16[1,512,512]{2,1,0:T(8,128)(2,1)} %w3_ref.1) | copy-start | bytes 1572868
  37.1 20.4 %collective-permute-start.2 = (bf16[3,512,128]{2,1,0:T(8,128)(2,1)S(1)}, bf16[3,512,128]{2,1,0:T(8,128)(2,1)S(1)}, u32[]{:S(2)}, u32[]{:S(2)}) collective-permute-start(bf16[3,512,128]{2,1,0:T(8,128)(2,1)S(1)} %get-tuple-element.41), channel_id=1, source_target_pairs={{0,8},{4,12},{8,0},{12,4},{16,24},{20,28},{24,16},{28,20},{1,9},{5... | collective-permute-start | bytes 1179656 | tf_op jit(solution)/shard_map/ppermute | solution.py:32
  37.7 19.8 %collective-permute-start.3 = (bf16[3,512,128]{2,1,0:T(8,128)(2,1)S(1)}, bf16[3,512,128]{2,1,0:T(8,128)(2,1)S(1)}, u32[]{:S(2)}, u32[]{:S(2)}) collective-permute-start(bf16[3,512,128]{2,1,0:T(8,128)(2,1)S(1)} %get-tuple-element.42), channel_id=1, source_target_pairs={{0,16},{4,20},{8,24},{12,28},{16,0},{20,4},{24,8},{28,12},{1,17},{... | collective-permute-start | bytes 1179656 | tf_op jit(solution)/shard_map/ppermute | solution.py:32
  39.3 23.1 %collective-permute-start.11 = (bf16[256,1024]{1,0:T(8,128)(2,1)S(1)}, bf16[256,1024]{1,0:T(8,128)(2,1)S(1)}, u32[]{:S(2)}, u32[]{:S(2)}) collective-permute-start(bf16[256,1024]{1,0:T(8,128)(2,1)S(1)} %collective-permute-done.10.refs_1_), channel_id=1, source_target_pairs={{0,1},{1,0},{2,3},{3,2},{4,5},{5,4},{6,7},{7,6},{8,9},{9,8},{10,11... | collective-permute-start | bytes 1572872 | tf_op jit(solution)/shard_map/ppermute | solution.py:32
  57.7 14.0 %collective-permute-start.4 = (bf16[3,512,128]{2,1,0:T(8,128)(2,1)S(1)}, bf16[3,512,128]{2,1,0:T(8,128)(2,1)S(1)}, u32[]{:S(2)}, u32[]{:S(2)}) collective-permute-start(bf16[3,512,128]{2,1,0:T(8,128)(2,1)S(1)} %get-tuple-element.44), channel_id=1, source_target_pairs={{0,16},{4,20},{8,24},{12,28},{16,0},{20,4},{24,8},{28,12},{1,17},{... | collective-permute-start | bytes 1179656 | tf_op jit(solution)/shard_map/ppermute | solution.py:32
  59.4 12.4 %collective-permute-start.5 = (bf16[3,512,128]{2,1,0:T(8,128)(2,1)S(1)}, bf16[3,512,128]{2,1,0:T(8,128)(2,1)S(1)}, u32[]{:S(2)}, u32[]{:S(2)}) collective-permute-start(bf16[3,512,128]{2,1,0:T(8,128)(2,1)S(1)} %get-tuple-element.45), channel_id=1, source_target_pairs={{0,8},{4,12},{8,0},{12,4},{16,24},{20,28},{24,16},{28,20},{1,9},{5... | collective-permute-start | bytes 1179656 | tf_op jit(solution)/shard_map/ppermute | solution.py:32
  60.8 12.2 %collective-permute-start = (bf16[512,512]{1,0:T(8,128)(2,1)S(1)}, bf16[512,512]{1,0:T(8,128)(2,1)S(1)}, u32[]{:S(2)}, u32[]{:S(2)}) collective-permute-start(bf16[512,512]{1,0:T(8,128)(2,1)S(1)} %get-tuple-element.29), channel_id=1, source_target_pairs={{0,4},{4,8},{8,12},{12,16},{16,20},{20,24},{24,28},{1,5},{5,9},{9,... | collective-permute-start | bytes 1572872 | tf_op jit(solution)/shard_map/ppermute | solution.py:395
  62.3 17.5 %collective-permute-start.13 = (bf16[1,256,1024]{2,1,0:T(8,128)(2,1)S(1)}, bf16[1,256,1024]{2,1,0:T(8,128)(2,1)S(1)}, u32[]{:S(2)}, u32[]{:S(2)}) collective-permute-start(bf16[1,256,1024]{2,1,0:T(8,128)(2,1)S(1)} %bitcast.2), channel_id=1, source_target_pairs={{0,8},{4,20},{8,0},{12,28},{16,24},{20,4},{24,16},{28,12},{1,9},{5... | collective-permute-start | bytes 1572872 | tf_op jit(solution)/shard_map/ppermute | solution.py:421
  72.4 11.8 %copy-start = (bf16[1024,512]{1,0:T(8,128)(2,1)S(1)}, bf16[1024,512]{1,0:T(8,128)(2,1)}, u32[]{:S(2)}) copy-start(bf16[1024,512]{1,0:T(8,128)(2,1)} %q_ref.7) | copy-start | bytes 3145732
  72.4 11.8 %collective-permute-start.6 = (bf16[3,512,256]{2,1,0:T(8,128)(2,1)S(1)}, bf16[3,512,256]{2,1,0:T(8,128)(2,1)S(1)}, u32[]{:S(2)}, u32[]{:S(2)}) collective-permute-start(bf16[3,512,256]{2,1,0:T(8,128)(2,1)S(1)} %renorm.1.mine_ref), channel_id=1, source_target_pairs={{0,4},{4,0},{8,12},{12,8},{16,20},{20,16},{24,28},{28,24},{1,5},{5... | collective-permute-start | bytes 2359304 | tf_op jit(solution)/shard_map/ppermute | solution.py:32
  72.5 24.3 %collective-permute-start.16 = (bf16[2,256,1024]{2,1,0:T(8,128)(2,1)S(1)}, bf16[2,256,1024]{2,1,0:T(8,128)(2,1)S(1)}, u32[]{:S(2)}, u32[]{:S(2)}) collective-permute-start(bf16[2,256,1024]{2,1,0:T(8,128)(2,1)S(1)} %pile.1.near), channel_id=1, source_target_pairs={{0,4},{4,0},{8,12},{12,8},{16,20},{20,16},{24,28},{28,24},{1,5},{5... | collective-permute-start | bytes 3145736 | tf_op jit(solution)/shard_map/ppermute | solution.py:32
  73.0 29.8 %collective-permute-start.18 = (bf16[2,256,1024]{2,1,0:T(8,128)(2,1)S(1)}, bf16[2,256,1024]{2,1,0:T(8,128)(2,1)S(1)}, u32[]{:S(2)}, u32[]{:S(2)}) collective-permute-start(bf16[2,256,1024]{2,1,0:T(8,128)(2,1)S(1)} %collective-permute-done.17.far), channel_id=1, source_target_pairs={{0,4},{4,0},{8,12},{12,8},{16,20},{20,16},{24,28},{28,24},{1,5},{5... | collective-permute-start | bytes 3145736 | tf_op jit(solution)/shard_map/ppermute | solution.py:32
  73.1 16.3 %collective-permute-start.12 = (bf16[1,256,1024]{2,1,0:T(8,128)(2,1)S(1)}, bf16[1,256,1024]{2,1,0:T(8,128)(2,1)S(1)}, u32[]{:S(2)}, u32[]{:S(2)}) collective-permute-start(bf16[1,256,1024]{2,1,0:T(8,128)(2,1)S(1)} %bitcast.3), channel_id=1, source_target_pairs={{0,4},{4,0},{8,12},{12,8},{16,20},{20,16},{24,28},{28,24},{1,5},{5... | collective-permute-start | bytes 1572872 | tf_op jit(solution)/shard_map/ppermute | solution.py:32
  79.8 10.3 %collective-permute-start.14 = (bf16[1,256,1024]{2,1,0:T(8,128)(2,1)S(1)}, bf16[1,256,1024]{2,1,0:T(8,128)(2,1)S(1)}, u32[]{:S(2)}, u32[]{:S(2)}) collective-permute-start(bf16[1,256,1024]{2,1,0:T(8,128)(2,1)S(1)} %collective-permute-done.13.far), channel_id=1, source_target_pairs={{0,4},{4,0},{8,12},{12,8},{16,20},{20,16},{24,28},{28,24},{1,5},{5... | collective-permute-start | bytes 1572872 | tf_op jit(solution)/shard_map/ppermute | solution.py:32
  84.8 11.2 %collective-permute-start.9 = (bf16[256,512]{1,0:T(8,128)(2,1)S(1)}, bf16[256,512]{1,0:T(8,128)(2,1)S(1)}, u32[]{:S(2)}, u32[]{:S(2)}) collective-permute-start(bf16[256,512]{1,0:T(8,128)(2,1)S(1)} %apply.6), channel_id=1, source_target_pairs={{0,3},{1,2},{2,1},{3,0},{4,7},{5,6},{6,5},{7,4},{8,11},{9,10},{10,... | collective-permute-start | bytes 786440 | tf_op jit(solution)/shard_map/ppermute | solution.py:32
  89.4 13.4 %collective-permute-start.8 = (bf16[256,512]{1,0:T(8,128)(2,1)S(1)}, bf16[256,512]{1,0:T(8,128)(2,1)S(1)}, u32[]{:S(2)}, u32[]{:S(2)}) collective-permute-start(bf16[256,512]{1,0:T(8,128)(2,1)S(1)} %apply.5), channel_id=1, source_target_pairs={{0,1},{1,0},{2,3},{3,2},{4,5},{5,4},{6,7},{7,6},{8,9},{9,8},{10,11... | collective-permute-start | bytes 786440 | tf_op jit(solution)/shard_map/ppermute | solution.py:32
  90.1 1.6 %copy-start.1 = (bf16[512,2048]{1,0:T(8,128)(2,1)S(1)}, bf16[512,2048]{1,0:T(8,128)(2,1)}, u32[]{:S(2)}) copy-start(bf16[512,2048]{1,0:T(8,128)(2,1)} %w_ref.1) | copy-start | bytes 6291460
  90.1 1.6 %copy-start.5 = (bf16[512]{0:T(512)(128)(2,1)S(1)}, bf16[512]{0:T(512)(128)(2,1)}, u32[]{:S(2)}) copy-start(bf16[512]{0:T(512)(128)(2,1)} %gain_ref.1) | copy-start | bytes 3076
  90.1 21.5 %collective-permute-start.7 = (bf16[256,512]{1,0:T(8,128)(2,1)S(1)}, bf16[256,512]{1,0:T(8,128)(2,1)S(1)}, u32[]{:S(2)}, u32[]{:S(2)}) collective-permute-start(bf16[256,512]{1,0:T(8,128)(2,1)S(1)} %apply.4), channel_id=1, source_target_pairs={{0,2},{1,3},{2,0},{3,1},{4,6},{5,7},{6,4},{7,5},{8,10},{9,11},{10,... | collective-permute-start | bytes 786440 | tf_op jit(solution)/shard_map/ppermute | solution.py:32

commit v5 on v4

--- a/solution.py
+++ b/solution.py
@@ -48,42 +48,46 @@
     return jnp.concatenate([tall] * (width // 128), axis=1)
 
 
-def load_kernel(k_hbm, v_hbm, w1_hbm, w2_hbm, w3_hbm, gain_hbm, w_hbm,
-                tail_ref, piece_ref, k_ref, v_ref, w1_ref, w2_ref, w3_ref, w_ref, gain_ref, sem):
+def load_kernel(k_hbm, v_hbm, gain_hbm, w_hbm, tail_ref, piece_ref, w_ref, gain_ref, sem):
     rows, columns = piece_ref.shape
-    core, side = place()
+    _, side = place()
     first = pl.multiple_of(side * rows, rows)
-    left = pl.multiple_of(core * columns, columns)
     last = pl.ds(k_hbm.shape[0] - WINDOW, WINDOW)
-    moves = [(gain_hbm, gain_ref), (w_hbm.at[pl.ds(first, rows), pl.ds(left, columns)], w_ref)]
+    steps = 4
+    block = rows // steps
+    moves = [(gain_hbm, gain_ref)]
+    for i in range(steps):
+        at = pl.ds(i * block, block)
+        moves.append((w_hbm.at[pl.ds(first + i * block, block), :], w_ref.at[at, :]))
     moves += [(k_hbm.at[last, :], tail_ref.at[pl.ds(0, WINDOW), :])]
     moves += [(v_hbm.at[last, :], tail_ref.at[pl.ds(WINDOW, WINDOW), :])]
-    moves += [(w1_hbm, w1_ref), (w3_hbm, w3_ref), (k_hbm, k_ref), (v_hbm, v_ref), (w2_hbm, w2_ref)]
     copies = [pltpu.make_async_copy(src, dst, sem.at[j]) for j, (src, dst) in enumerate(moves)]
     for copy in copies:
         copy.start()
     copies[0].wait()
     gain = gain_ref[...].reshape(1, 2 * rows).astype(jnp.float32)
-    gain = column(jnp.where(side == 0, gain[:, :rows], gain[:, rows:]), columns)
-    copies[1].wait()
-    piece_ref[...] = (w_ref[...].astype(jnp.float32) * gain).astype(jnp.bfloat16)
-    for copy in copies[2:]:
+    gain = jnp.transpose(jnp.broadcast_to(jnp.where(side == 0, gain[:, :rows], gain[:, rows:]), (128, rows)))
+    for i in range(steps):
+        at = slice(i * block, (i + 1) * block)
+        copies[1 + i].wait()
+        for left in range(0, columns, 128):
+            here = slice(left, left + 128)
+            piece_ref[at, here] = (w_ref[at, here].astype(jnp.float32) * gain[at, :]).astype(jnp.bfloat16)
+    for copy in copies[1 + steps :]:
         copy.wait()
 
 
-def load(keys, values, w1, w2, w3, gain, weight):
-    arrays = (keys, values, w1, w2, w3)
-    piece = pltpu.VMEM((weight.shape[0] // 2, weight.shape[1] // 2), jnp.bfloat16)
+def load(keys, values, gain, weight):
+    piece = pltpu.VMEM((weight.shape[0] // 2, weight.shape[1]), jnp.bfloat16)
     return pl.pallas_call(
         load_kernel,
-        out_shape=[pltpu.VMEM((2 * WINDOW, keys.shape[1]), jnp.bfloat16), piece]
-        + [pltpu.VMEM(a.shape, a.dtype) for a in arrays],
+        out_shape=[pltpu.VMEM((2 * WINDOW, keys.shape[1]), jnp.bfloat16), piece],
         compiler_params=grant(8),
-        in_specs=[HBM] * 7,
-        out_specs=[VMEM] * 7,
-        scratch_shapes=[piece, pltpu.VMEM(gain.shape, gain.dtype), pltpu.SemaphoreType.DMA((9,))],
+        in_specs=[HBM] * 4,
+        out_specs=[VMEM] * 2,
+        scratch_shapes=[piece, pltpu.VMEM(gain.shape, gain.dtype), pltpu.SemaphoreType.DMA((7,))],
         name="load",
-    )(*far_core(*arrays, gain, weight))
+    )(*far_core(keys, values, gain, weight))
 
 
 def halves(width):
@@ -309,30 +313,40 @@
     )(*near_core(x, gain, weight))
 
 
-def pile_kernel(*refs):
-    *ins, out_ref, sem = refs
-    copies = [pltpu.make_async_copy(src, out_ref.at[j], sem.at[j]) for j, src in enumerate(ins)]
-    for copy in copies:
+def pick_kernel(early_ref, early_c_ref, out_ref, sem):
+    columns = out_ref.shape[1]
+    core, _ = place()
+    here = pl.ds(pl.multiple_of(core * columns, columns), columns)
+
+    @pl.when(core == 1)
+    def _():
+        copy = pltpu.make_async_copy(early_ref.at[:, here], out_ref, sem)
         copy.start()
-    for copy in copies:
         copy.wait()
 
-
-def pile(*arrays):
-    return pl.pallas_call(
-        pile_kernel,
-        out_shape=pltpu.VMEM((len(arrays),) + arrays[0].shape, arrays[0].dtype),
+    @pl.when(core == 0)
+    def _():
+        copy = pltpu.make_async_copy(early_c_ref.at[:, here], out_ref, sem)
+        copy.start()
+        copy.wait()
+
+
+def pick(early, early_c):
+    return pl.pallas_call(
+        pick_kernel,
+        out_shape=pltpu.VMEM((early.shape[0], early.shape[1] // 2), early.dtype),
         compiler_params=grant(4),
-        in_specs=[VMEM] * len(arrays),
+        in_specs=[VMEM] * 2,
         out_specs=VMEM,
-        scratch_shapes=[pltpu.SemaphoreType.DMA((len(arrays),))],
-        name="pile",
-    )(*near_core(*arrays))
-
-
-def project_kernel(index, scale_by, x_ref, base_ref, squares_ref, near, near_c, far, far_c,
+        scratch_shapes=[pltpu.SemaphoreType.DMA],
+        name="pick",
+    )(*near_core(early, early_c))
+
+
+def project_kernel(holder, scale_by, x_ref, base_ref, squares_ref, near, near_c, far, far_c,
                    out_ref, *rest):
-    rows, columns = near.shape[1:]
+    rows = near.shape[0]
+    columns = out_ref.shape[1] // 2
     core, half = place()
     wide = x_ref[...].astype(jnp.float32)
     squares = squares_ref[...] + jnp.sum(wide * wide, axis=1, keepdims=True)
@@ -342,12 +356,18 @@
     scale = lax.rsqrt(squares * scale_by + EPSILON) if scale_by else None
     block = columns // 2
     stores = []
-    for side, (w_near, w_far) in enumerate(((near, far), (near_c, far_c))):
-        start = core if side == 0 else 1 - core
+    for side in range(2):
         for j in range(2):
-            at = pl.ds(pl.multiple_of(start * columns + j * block, block), block)
-            here = slice(j * block, (j + 1) * block)
-            w = jnp.concatenate([w_near[index, :, here], w_far[index, :, here]], axis=0)
+            if holder is None:
+                w_near, w_far = ((near, far), (near_c, far_c))[side]
+                start = core if side == 0 else 1 - core
+                here = slice(j * block, (j + 1) * block)
+                w = jnp.concatenate([w_near[:, here], w_far[:, here]], axis=0)
+                at = pl.ds(pl.multiple_of(start * columns + j * block, block), block)
+            else:
+                at = slice(side * columns + j * block, side * columns + (j + 1) * block)
+                w = [jnp.where(core == holder, a[:, at], b[:, at]) for a, b in ((near, near_c), (far, far_c))]
+                w = jnp.concatenate(w, axis=0)
             total = base_ref[:, at] + dot(x, w)
             if scale_by:
                 ready_ref, sem = rest
@@ -363,7 +383,7 @@
         store.wait()
 
 
-def project(index, scale_by, x, base, squares, pieces):
+def project(holder, scale_by, x, base, squares, pieces):
     rows, columns = base.shape
     if scale_by:
         shape = jax.ShapeDtypeStruct((rows, columns), jnp.bfloat16)
@@ -372,7 +392,7 @@
         shape = (pltpu.VMEM((rows, columns), jnp.float32), pltpu.VMEM((rows, 1), jnp.float32))
         scratch = []
     return pl.pallas_call(
-        functools.partial(project_kernel, index, scale_by),
+        functools.partial(project_kernel, holder, scale_by),
         out_shape=shape,
         in_specs=[VMEM] * 7,
         out_specs=HBM if scale_by else (VMEM, VMEM),
@@ -387,21 +407,28 @@
     ctx_count = lax.axis_size("ctx")
     heads = lax.axis_size("head")
     bits = ctx_count.bit_length() - 1
-    assert ctx_count == 1 << bits and bits >= 3
-
-    tail, piece, k_near, *loaded = load(
-        keys, values, fast_w1, fast_w2, fast_w3, norm_gain, out_weight
-    )
+    assert ctx_count == 1 << bits and bits >= 3 and heads == 4
+
+    tail, piece = load(keys, values, norm_gain, out_weight)
     tail = lax.ppermute(tail, "ctx", [(i, i + 1) for i in range(ctx_count - 1)])
 
-    near = {0: piece}
-    for level in reversed(range(heads.bit_length() - 1)):
-        for k in sorted(near):
-            near[k | 1 << level] = swap(near[k], "head", 1 << level)
-
-    give, *factors = pushes(k_near, loaded[0], rates, *loaded[1:])
+    over = [(i, i ^ (2 if i // heads & 1 else 1)) for i in range(ctx_count * heads)]
+    early = lax.ppermute(piece, ("ctx", "head"), over)
+    early_c = swap(early, "ctx", 1)
+    late = pick(early, early_c)
+    late = swap(late, "head", 1)
+    cross = [(i, i ^ (4 if i & 1 else 2)) for i in range(ctx_count)]
+    early_far = lax.ppermute(early, "ctx", cross)
+    late_far = lax.ppermute(late, "ctx", cross)
+    late_c = swap(late, "ctx", 1)
+    early_far_c = swap(early_far, "ctx", 1)
+    late_far_c = swap(late_far, "ctx", 1)
+    early_pieces = (early, early_c, early_far, early_far_c)
+    late_pieces = (late, late_c, late_far, late_far_c)
+
+    give, *factors = pushes(keys, values, rates, fast_w1, fast_w2, fast_w3)
     got = [swap(give, "ctx", 1)]
-    keep = kept(k_near, *factors)
+    keep = kept(keys, *factors)
 
     masks = [1 << b for b in range(1, bits)]
     for forward, backward in zip(masks, masks[::-1]):
@@ -413,16 +440,6 @@
 
     seen = window(queries, keys, values, tail)
 
-    early = pile(*(near[k] for k in range(1, heads - 1)))
-    late = near[heads - 1].reshape(1, *piece.shape)
-    cross = [(i, i ^ (4 if i & 1 else 2)) for i in range(ctx_count)]
-    pieces = []
-    for group in (early, late):
-        far = lax.ppermute(group, "ctx", cross)
-        near_c = swap(group, "ctx", 1)
-        far_c = swap(far, "ctx", 1)
-        pieces.append((group, near_c, far, far_c))
-
     rows = tok_rows // heads
     blocks = {}
     for k in send_order(heads) + [0]:
@@ -430,10 +447,9 @@
         blocks[k] = swap(combined, "head", k) if k else combined
     base, squares = own_project(blocks[0], norm_gain, out_weight)
     for k in send_order(heads):
-        late_one = k == heads - 1
-        index, which = (0, pieces[1]) if late_one else (k - 1, pieces[0])
+        holder, pieces = (None, late_pieces) if k == heads - 1 else (k - 1, early_pieces)
         scale_by = 1.0 / (heads * width) if k == send_order(heads)[-1] else None
-        result = project(index, scale_by, blocks[k], base, squares, which)
+        result = project(holder, scale_by, blocks[k], base, squares, pieces)
         if scale_by is None:
             base, squares = result
     return result
@@ -455,6 +471,4 @@
         P("head"),
         P("head", None),
     )
-    return jax.shard_map(
-        step, mesh=mesh, in_specs=placed, out_specs=P(("ctx", "head"), None), check_vma=False
-    )
+    return jax.shard_map(step, mesh=mesh, in_specs=placed, out_specs=P(("ctx", "head"), None), check_vma=False)

time: 113 us -> 111 us (0.982)
  waiting for transfers between devices: 68.8 us -> 65.2 us
  starting transfers between devices: 25.3 us -> 27.4 us
    ppermute x16 -> x14, waiting for transfers between devices: 65.2 us -> 38.2 us  [swap(): lax.ppermute(value, axis, [(i, i ^ mask) for i in range(lax.axis_size(axi...]
    ppermute x2 -> x3, waiting for transfers between devices: 3.62 us -> 27 us  [the longest x1 19.7 us: step(): early = lax.ppermute(piece, ('ctx', 'head'), over)]
    ppermute x1, starting transfers between devices: 1.49 us -> 2.99 us  [step(): tail = lax.ppermute(tail, 'ctx', [(i, i + 1) for i in range(ctx_count - 1)])]
    ppermute x2 -> x3, starting transfers between devices: 2.84 us -> 4.24 us  [the longest x1 3.13 us: step(): early = lax.ppermute(piece, ('ctx', 'head'), over)]
    ppermute x16 -> x14, starting transfers between devices: 20.9 us -> 20.2 us  [swap(): lax.ppermute(value, axis, [(i, i ^ mask) for i in range(lax.axis_size(axi...]
  transfers between devices with their start and end apart: 19 -> 18, of which waited for: 8 -> 8; matrix products, arithmetic and copies ran while one was open for 0% -> 0% of each run, Pallas kernels for 10% -> 13%
where the time goes in v5:
time: 111 us
  waiting for transfers between devices  65.2 us (59%)
  starting transfers between devices  27.4 us (25%)
  Pallas kernels  17.5 us (16%)
    ppermute x14, waiting for transfers between devices, swap(): lax.ppermute(value, axis, [(i, i ^ mask) for i in range(lax.axis_size(axi...  38.2 us
    ppermute x14, starting transfers between devices, swap(): lax.ppermute(value, axis, [(i, i ^ mask) for i in range(lax.axis_size(axi...  20.2 us
    ppermute x1, waiting for transfers between devices, step(): early = lax.ppermute(piece, ('ctx', 'head'), over)  19.7 us
    ppermute x1, waiting for transfers between devices, step(): late_far = lax.ppermute(late, 'ctx', cross)  7.31 us
    pallas_call x1, Pallas kernels, window(): pl.pallas_call(window_kernel, out_shape=pltpu.VMEM(queries.shape, jnp.flo...  4.36 us
    pallas_call x1, Pallas kernels, pushes(): pl.pallas_call(push_kernel, out_shape=[pltpu.VMEM((3, width, width // 2),...  3.33 us
    ppermute x1, starting transfers between devices, step(): early = lax.ppermute(piece, ('ctx', 'head'), over)  3.13 us
    pallas_call x3, Pallas kernels, project(): pl.pallas_call(functools.partial(project_kernel, holder, scale_by), out_s...  3.08 us
  transfers between devices with their start and end apart: 18, of which 8 were waited for; matrix products, arithmetic and copies ran while one was open for 0% of the time, Pallas kernels for 13%

profile of v5, /device:TPU:0, one launch (start us, length us, event | category | flops | bytes accessed | tf_op | source)
XLA Modules:
  0.0 110.6 jit_solution(1015874627808816445)
XLA Ops:
  0.0 1.6 %load.1 = (bf16[512,512]{1,0:T(8,128)(2,1)S(1)}, bf16[256,2048]{1,0:T(8,128)(2,1)S(1)}) custom-call(bf16[1024,512]{1,0:T(8,128)(2,1)} %k_ref.3, bf16[1024,512]{1,0:T(8,128)(2,1)} %v_ref.1, bf16[512]{0:T(512)(128)(2,1)} %gain_ref.1, bf16[512,2048]{1,0:T(8,128)(2,1)} %w_ref.1), custom_call_target="tpu_custom_call" | custom-call | tf_op jit(solution)/shard_map/load/pallas_call | solution.py:82
  1.6 3.1 %collective-permute-start.10 = (bf16[256,2048]{1,0:T(8,128)(2,1)S(1)}, bf16[256,2048]{1,0:T(8,128)(2,1)S(1)}, u32[]{:S(2)}, u32[]{:S(2)}) collective-permute-start(bf16[256,2048]{1,0:T(8,128)(2,1)S(1)} %get-tuple-element.38), channel_id=1, source_target_pairs={{0,1},{1,0},{2,3},{3,2},{4,6},{5,7},{6,4},{7,5},{8,9},{9,8},{10,11... | collective-permute-start | bytes 3145736 | tf_op jit(solution)/shard_map/ppermute | solution.py:416
  4.8 3.3 %pushes.1 = (bf16[3,512,256]{2,1,0:T(8,128)(2,1)S(1)}, bf16[1024,512]{1,0:T(8,128)(2,1)S(1)}, bf16[1024,512]{1,0:T(8,128)(2,1)S(1)}, bf16[1024,512]{1,0:T(8,128)(2,1)S(1)}, bf16[1024,512]{1,0:T(8,128)(2,1)S(1)}) custom-call(bf16[1024,512]{1,0:T(8,128)(2,1)S(1)} %copy-done.1, bf16[1024,512]{1,0:T(8,128)(2,1)S(1)} %copy-done.2, f32[1,1024]{1,0:T(1,128)S(1)} %bitcast.1, ...), custom_call_target="tpu_custom_call" | custom-call | tf_op jit(solution)/shard_map/pushes/pallas_call | solution.py:127
  8.1 0.6 collective-permute-start.1
  8.7 19.7 %collective-permute-done.10.early_ref.near = bf16[256,2048]{1,0:T(8,128)(2,1)S(1)} collective-permute-done((bf16[256,2048]{1,0:T(8,128)(2,1)S(1)}, bf16[256,2048]{1,0:T(8,128)(2,1)S(1)}, u32[]{:S(2)}, u32[]{:S(2)}) %collective-permute-start.10) | collective-permute-done | bytes 1048608 | tf_op jit(solution)/shard_map/ppermute | solution.py:416
  28.8 1.0 kept.1.keep_ref
  30.1 1.6 %collective-permute-start.2 = (bf16[3,512,128]{2,1,0:T(8,128)(2,1)S(1)}, bf16[3,512,128]{2,1,0:T(8,128)(2,1)S(1)}, u32[]{:S(2)}, u32[]{:S(2)}) collective-permute-start(bf16[3,512,128]{2,1,0:T(8,128)(2,1)S(1)} %get-tuple-element.31), channel_id=1, source_target_pairs={{0,8},{4,12},{8,0},{12,4},{16,24},{20,28},{24,16},{28,20},{1,9},{5... | collective-permute-start | bytes 1179656 | tf_op jit(solution)/shard_map/ppermute | solution.py:32
  31.7 1.5 %collective-permute-start.3 = (bf16[3,512,128]{2,1,0:T(8,128)(2,1)S(1)}, bf16[3,512,128]{2,1,0:T(8,128)(2,1)S(1)}, u32[]{:S(2)}, u32[]{:S(2)}) collective-permute-start(bf16[3,512,128]{2,1,0:T(8,128)(2,1)S(1)} %get-tuple-element.32), channel_id=1, source_target_pairs={{0,16},{4,20},{8,24},{12,28},{16,0},{20,4},{24,8},{28,12},{1,17},{... | collective-permute-start | bytes 1179656 | tf_op jit(solution)/shard_map/ppermute | solution.py:32
  33.7 7.7 %collective-permute-done.2.got_a_ref = bf16[3,512,128]{2,1,0:T(8,128)(2,1)S(1)} collective-permute-done((bf16[3,512,128]{2,1,0:T(8,128)(2,1)S(1)}, bf16[3,512,128]{2,1,0:T(8,128)(2,1)S(1)}, u32[]{:S(2)}, u32[]{:S(2)}) %collective-permute-start.2) | collective-permute-done | bytes 393248 | tf_op jit(solution)/shard_map/ppermute | solution.py:32
  41.4 2.2 %collective-permute-done.3.got_b_ref = bf16[3,512,128]{2,1,0:T(8,128)(2,1)S(1)} collective-permute-done((bf16[3,512,128]{2,1,0:T(8,128)(2,1)S(1)}, bf16[3,512,128]{2,1,0:T(8,128)(2,1)S(1)}, u32[]{:S(2)}, u32[]{:S(2)}) %collective-permute-start.3) | collective-permute-done | bytes 393248 | tf_op jit(solution)/shard_map/ppermute | solution.py:32
  43.9 1.6 %collective-permute-start.4 = (bf16[3,512,128]{2,1,0:T(8,128)(2,1)S(1)}, bf16[3,512,128]{2,1,0:T(8,128)(2,1)S(1)}, u32[]{:S(2)}, u32[]{:S(2)}) collective-permute-start(bf16[3,512,128]{2,1,0:T(8,128)(2,1)S(1)} %get-tuple-element.34), channel_id=1, source_target_pairs={{0,16},{4,20},{8,24},{12,28},{16,0},{20,4},{24,8},{28,12},{1,17},{... | collective-permute-start | bytes 1179656 | tf_op jit(solution)/shard_map/ppermute | solution.py:32
  46.1 1.9 %collective-permute-start.12 = (bf16[256,1024]{1,0:T(8,128)(2,1)S(1)}, bf16[256,1024]{1,0:T(8,128)(2,1)S(1)}, u32[]{:S(2)}, u32[]{:S(2)}) collective-permute-start(bf16[256,1024]{1,0:T(8,128)(2,1)S(1)} %pick.1), channel_id=1, source_target_pairs={{0,1},{1,0},{2,3},{3,2},{4,5},{5,4},{6,7},{7,6},{8,9},{9,8},{10,11... | collective-permute-start | bytes 1572872 | tf_op jit(solution)/shard_map/ppermute | solution.py:32
  48.0 8.0 %collective-permute-done.4.got_a_ref = bf16[3,512,128]{2,1,0:T(8,128)(2,1)S(1)} collective-permute-done((bf16[3,512,128]{2,1,0:T(8,128)(2,1)S(1)}, bf16[3,512,128]{2,1,0:T(8,128)(2,1)S(1)}, u32[]{:S(2)}, u32[]{:S(2)}) %collective-permute-start.4) | collective-permute-done | bytes 393248 | tf_op jit(solution)/shard_map/ppermute | solution.py:32
  55.9 5.2 %collective-permute-done.5.got_b_ref = bf16[3,512,128]{2,1,0:T(8,128)(2,1)S(1)} collective-permute-done((bf16[3,512,128]{2,1,0:T(8,128)(2,1)S(1)}, bf16[3,512,128]{2,1,0:T(8,128)(2,1)S(1)}, u32[]{:S(2)}, u32[]{:S(2)}) %collective-permute-start.5) | collective-permute-done | bytes 393248 | tf_op jit(solution)/shard_map/ppermute | solution.py:32
  61.1 0.6 renorm.1.mine_ref
  61.7 1.4 %collective-permute-start.6 = (bf16[3,512,256]{2,1,0:T(8,128)(2,1)S(1)}, bf16[3,512,256]{2,1,0:T(8,128)(2,1)S(1)}, u32[]{:S(2)}, u32[]{:S(2)}) collective-permute-start(bf16[3,512,256]{2,1,0:T(8,128)(2,1)S(1)} %renorm.1.mine_ref), channel_id=1, source_target_pairs={{0,4},{4,0},{8,12},{12,8},{16,20},{20,16},{24,28},{28,24},{1,5},{5... | collective-permute-start | bytes 2359304 | tf_op jit(solution)/shard_map/ppermute | solution.py:32
  63.1 0.6 collective-permute-start.14
  63.6 3.0 %collective-permute-start = (bf16[512,512]{1,0:T(8,128)(2,1)S(1)}, bf16[512,512]{1,0:T(8,128)(2,1)S(1)}, u32[]{:S(2)}, u32[]{:S(2)}) collective-permute-start(bf16[512,512]{1,0:T(8,128)(2,1)S(1)} %get-tuple-element.24), channel_id=1, source_target_pairs={{0,4},{4,8},{8,12},{12,16},{16,20},{20,24},{24,28},{1,5},{5,9},{9,... | collective-permute-start | bytes 1572872 | tf_op jit(solution)/shard_map/ppermute | solution.py:413
  66.7 0.9 collective-permute-start.17
  67.6 7.3 %collective-permute-done.14.far = bf16[256,1024]{1,0:T(8,128)(2,1)S(1)} collective-permute-done((bf16[256,1024]{1,0:T(8,128)(2,1)S(1)}, bf16[256,1024]{1,0:T(8,128)(2,1)S(1)}, u32[]{:S(2)}, u32[]{:S(2)}) %collective-permute-start.14) | collective-permute-done | bytes 524320 | tf_op jit(solution)/shard_map/ppermute | solution.py:422
  74.9 4.4 %window.1.seen_ref = f32[1024,512]{1,0:T(8,128)S(1)} custom-call(bf16[1024,512]{1,0:T(8,128)(2,1)} %q_ref.7, bf16[1024,512]{1,0:T(8,128)(2,1)} %k_ref.3, bf16[1024,512]{1,0:T(8,128)(2,1)} %v_ref.1, bf16[512,512]{1,0:T(8,128)(2,1)S(1)} %collective-permute-done.tail_ref), custom_call_target="tpu_custom_call" | custom-call | tf_op jit(solution)/shard_map/window/pallas_call | solution.py:250
  79.3 0.6 apply.6
  79.9 3.9 %collective-permute-start.9 = (bf16[256,512]{1,0:T(8,128)(2,1)S(1)}, bf16[256,512]{1,0:T(8,128)(2,1)S(1)}, u32[]{:S(2)}, u32[]{:S(2)}) collective-permute-start(bf16[256,512]{1,0:T(8,128)(2,1)S(1)} %apply.6), channel_id=1, source_target_pairs={{0,3},{1,2},{2,1},{3,0},{4,7},{5,6},{6,5},{7,4},{8,11},{9,10},{10,... | collective-permute-start | bytes 786440 | tf_op jit(solution)/shard_map/ppermute | solution.py:32
  83.8 0.6 apply.5
  84.5 0.6 apply.4
  85.1 5.6 %collective-permute-done.9.x_ref = bf16[256,512]{1,0:T(8,128)(2,1)S(1)} collective-permute-done((bf16[256,512]{1,0:T(8,128)(2,1)S(1)}, bf16[256,512]{1,0:T(8,128)(2,1)S(1)}, u32[]{:S(2)}, u32[]{:S(2)}) %collective-permute-start.9) | collective-permute-done | bytes 262176 | tf_op jit(solution)/shard_map/ppermute | solution.py:32
  90.7 5.8 %collective-permute-start.7 = (bf16[256,512]{1,0:T(8,128)(2,1)S(1)}, bf16[256,512]{1,0:T(8,128)(2,1)S(1)}, u32[]{:S(2)}, u32[]{:S(2)}) collective-permute-start(bf16[256,512]{1,0:T(8,128)(2,1)S(1)} %apply.4), channel_id=1, source_target_pairs={{0,2},{1,3},{2,0},{3,1},{4,6},{5,7},{6,4},{7,5},{8,10},{9,11},{10,... | collective-permute-start | bytes 786440 | tf_op jit(solution)/shard_map/ppermute | solution.py:32
  97.1 0.7 own_project.1
  97.8 0.7 project.3
  98.6 0.8 project.4
  99.3 9.5 %collective-permute-done.7.x_ref = bf16[256,512]{1,0:T(8,128)(2,1)S(1)} collective-permute-done((bf16[256,512]{1,0:T(8,128)(2,1)S(1)}, bf16[256,512]{1,0:T(8,128)(2,1)S(1)}, u32[]{:S(2)}, u32[]{:S(2)}) %collective-permute-start.7) | collective-permute-done | bytes 262176 | tf_op jit(solution)/shard_map/ppermute | solution.py:32
  108.9 1.6 %project.5 = bf16[256,2048]{1,0:T(8,128)(2,1)} custom-call(bf16[256,512]{1,0:T(8,128)(2,1)S(1)} %collective-permute-done.7.x_ref, f32[256,2048]{1,0:T(8,128)S(1)} %get-tuple-element.41.base_ref, f32[256,1]{1,0:T(8,128)S(1)} %get-tuple-element.42.squares_ref, bf16[256,2048]{1,0:T(8,128)(2,1)S(1)} %collective-permute-done.10.early_ref.near, ...), custom_call_target="tpu_custom_call" | custom-call | tf_op jit(solution)/shard_map/project/pallas_call | solution.py:394
  (38 shorter events, 2.7 us)
Async XLA Ops:
  0.0 4.7 %copy-start.1 = (bf16[1024,512]{1,0:T(8,128)(2,1)S(1)}, bf16[1024,512]{1,0:T(8,128)(2,1)}, u32[]{:S(2)}) copy-start(bf16[1024,512]{1,0:T(8,128)(2,1)} %k_ref.3) | copy-start | bytes 3145732
  0.0 4.7 %copy-start.2 = (bf16[1024,512]{1,0:T(8,128)(2,1)S(1)}, bf16[1024,512]{1,0:T(8,128)(2,1)}, u32[]{:S(2)}) copy-start(bf16[1024,512]{1,0:T(8,128)(2,1)} %v_ref.1) | copy-start | bytes 3145732
  0.0 4.7 %copy-start.8 = (f32[1024,1]{0,1:T(1,128)S(1)}, f32[1024,1]{0,1:T(1,128)}, u32[]{:S(2)}) copy-start(f32[1024,1]{0,1:T(1,128)} %param.12) | copy-start | bytes 12292
  0.0 4.7 %copy-start.4 = (bf16[1,512,512]{2,1,0:T(8,128)(2,1)S(1)}, bf16[1,512,512]{2,1,0:T(8,128)(2,1)}, u32[]{:S(2)}) copy-start(bf16[1,512,512]{2,1,0:T(8,128)(2,1)} %w1_ref.3) | copy-start | bytes 1572868
  0.0 4.7 %copy-start.5 = (bf16[1,512,512]{2,1,0:T(8,128)(2,1)S(1)}, bf16[1,512,512]{2,1,0:T(8,128)(2,1)}, u32[]{:S(2)}) copy-start(bf16[1,512,512]{2,1,0:T(8,128)(2,1)} %w2_ref.3) | copy-start | bytes 1572868
  0.0 4.8 %copy-start.6 = (bf16[1,512,512]{2,1,0:T(8,128)(2,1)S(1)}, bf16[1,512,512]{2,1,0:T(8,128)(2,1)}, u32[]{:S(2)}) copy-start(bf16[1,512,512]{2,1,0:T(8,128)(2,1)} %w3_ref.3) | copy-start | bytes 1572868
  1.6 26.8 %collective-permute-start.10 = (bf16[256,2048]{1,0:T(8,128)(2,1)S(1)}, bf16[256,2048]{1,0:T(8,128)(2,1)S(1)}, u32[]{:S(2)}, u32[]{:S(2)}) collective-permute-start(bf16[256,2048]{1,0:T(8,128)(2,1)S(1)} %get-tuple-element.38), channel_id=1, source_target_pairs={{0,1},{1,0},{2,3},{3,2},{4,6},{5,7},{6,4},{7,5},{8,9},{9,8},{10,11... | collective-permute-start | bytes 3145736 | tf_op jit(solution)/shard_map/ppermute | solution.py:416
  8.1 21.7 %collective-permute-start.1 = (bf16[3,512,256]{2,1,0:T(8,128)(2,1)S(1)}, bf16[3,512,256]{2,1,0:T(8,128)(2,1)S(1)}, u32[]{:S(2)}, u32[]{:S(2)}) collective-permute-start(bf16[3,512,256]{2,1,0:T(8,128)(2,1)S(1)} %get-tuple-element.29), channel_id=1, source_target_pairs={{0,4},{4,0},{8,12},{12,8},{16,20},{20,16},{24,28},{28,24},{1,5},{5... | collective-permute-start | bytes 2359304 | tf_op jit(solution)/shard_map/ppermute | solution.py:32
  28.4 17.6 %collective-permute-start.11 = (bf16[256,2048]{1,0:T(8,128)(2,1)S(1)}, bf16[256,2048]{1,0:T(8,128)(2,1)S(1)}, u32[]{:S(2)}, u32[]{:S(2)}) collective-permute-start(bf16[256,2048]{1,0:T(8,128)(2,1)S(1)} %collective-permute-done.10.early_ref.near), channel_id=1, source_target_pairs={{0,4},{4,0},{8,12},{12,8},{16,20},{20,16},{24,28},{28,24},{1,5},{5... | collective-permute-start | bytes 3145736 | tf_op jit(solution)/shard_map/ppermute | solution.py:32
  30.1 11.4 %collective-permute-start.2 = (bf16[3,512,128]{2,1,0:T(8,128)(2,1)S(1)}, bf16[3,512,128]{2,1,0:T(8,128)(2,1)S(1)}, u32[]{:S(2)}, u32[]{:S(2)}) collective-permute-start(bf16[3,512,128]{2,1,0:T(8,128)(2,1)S(1)} %get-tuple-element.31), channel_id=1, source_target_pairs={{0,8},{4,12},{8,0},{12,4},{16,24},{20,28},{24,16},{28,20},{1,9},{5... | collective-permute-start | bytes 1179656 | tf_op jit(solution)/shard_map/ppermute | solution.py:32
  31.7 12.0 %collective-permute-start.3 = (bf16[3,512,128]{2,1,0:T(8,128)(2,1)S(1)}, bf16[3,512,128]{2,1,0:T(8,128)(2,1)S(1)}, u32[]{:S(2)}, u32[]{:S(2)}) collective-permute-start(bf16[3,512,128]{2,1,0:T(8,128)(2,1)S(1)} %get-tuple-element.32), channel_id=1, source_target_pairs={{0,16},{4,20},{8,24},{12,28},{16,0},{20,4},{24,8},{28,12},{1,17},{... | collective-permute-start | bytes 1179656 | tf_op jit(solution)/shard_map/ppermute | solution.py:32
  33.2 33.5 %collective-permute-start.16 = (bf16[256,2048]{1,0:T(8,128)(2,1)S(1)}, bf16[256,2048]{1,0:T(8,128)(2,1)S(1)}, u32[]{:S(2)}, u32[]{:S(2)}) collective-permute-start(bf16[256,2048]{1,0:T(8,128)(2,1)S(1)} %collective-permute-done.10.early_ref.near), channel_id=1, source_target_pairs={{0,8},{4,20},{8,0},{12,28},{16,24},{20,4},{24,16},{28,12},{1,9},{5... | collective-permute-start | bytes 3145736 | tf_op jit(solution)/shard_map/ppermute | solution.py:421
  43.9 12.1 %collective-permute-start.4 = (bf16[3,512,128]{2,1,0:T(8,128)(2,1)S(1)}, bf16[3,512,128]{2,1,0:T(8,128)(2,1)S(1)}, u32[]{:S(2)}, u32[]{:S(2)}) collective-permute-start(bf16[3,512,128]{2,1,0:T(8,128)(2,1)S(1)} %get-tuple-element.34), channel_id=1, source_target_pairs={{0,16},{4,20},{8,24},{12,28},{16,0},{20,4},{24,8},{28,12},{1,17},{... | collective-permute-start | bytes 1179656 | tf_op jit(solution)/shard_map/ppermute | solution.py:32
  45.4 15.7 %collective-permute-start.5 = (bf16[3,512,128]{2,1,0:T(8,128)(2,1)S(1)}, bf16[3,512,128]{2,1,0:T(8,128)(2,1)S(1)}, u32[]{:S(2)}, u32[]{:S(2)}) collective-permute-start(bf16[3,512,128]{2,1,0:T(8,128)(2,1)S(1)} %get-tuple-element.35), channel_id=1, source_target_pairs={{0,8},{4,12},{8,0},{12,4},{16,24},{20,28},{24,16},{28,20},{1,9},{5... | collective-permute-start | bytes 1179656 | tf_op jit(solution)/shard_map/ppermute | solution.py:32
  46.1 17.0 %collective-permute-start.12 = (bf16[256,1024]{1,0:T(8,128)(2,1)S(1)}, bf16[256,1024]{1,0:T(8,128)(2,1)S(1)}, u32[]{:S(2)}, u32[]{:S(2)}) collective-permute-start(bf16[256,1024]{1,0:T(8,128)(2,1)S(1)} %pick.1), channel_id=1, source_target_pairs={{0,1},{1,0},{2,3},{3,2},{4,5},{5,4},{6,7},{7,6},{8,9},{9,8},{10,11... | collective-permute-start | bytes 1572872 | tf_op jit(solution)/shard_map/ppermute | solution.py:32
  61.7 17.6 %collective-permute-start.6 = (bf16[3,512,256]{2,1,0:T(8,128)(2,1)S(1)}, bf16[3,512,256]{2,1,0:T(8,128)(2,1)S(1)}, u32[]{:S(2)}, u32[]{:S(2)}) collective-permute-start(bf16[3,512,256]{2,1,0:T(8,128)(2,1)S(1)} %renorm.1.mine_ref), channel_id=1, source_target_pairs={{0,4},{4,0},{8,12},{12,8},{16,20},{20,16},{24,28},{28,24},{1,5},{5... | collective-permute-start | bytes 2359304 | tf_op jit(solution)/shard_map/ppermute | solution.py:32
  63.1 11.8 %collective-permute-start.14 = (bf16[256,1024]{1,0:T(8,128)(2,1)S(1)}, bf16[256,1024]{1,0:T(8,128)(2,1)S(1)}, u32[]{:S(2)}, u32[]{:S(2)}) collective-permute-start(bf16[256,1024]{1,0:T(8,128)(2,1)S(1)} %collective-permute-done.12.near), channel_id=1, source_target_pairs={{0,8},{4,20},{8,0},{12,28},{16,24},{20,4},{24,16},{28,12},{1,9},{5... | collective-permute-start | bytes 1572872 | tf_op jit(solution)/shard_map/ppermute | solution.py:422
  63.6 15.6 %copy-start = (bf16[1024,512]{1,0:T(8,128)(2,1)S(1)}, bf16[1024,512]{1,0:T(8,128)(2,1)}, u32[]{:S(2)}) copy-start(bf16[1024,512]{1,0:T(8,128)(2,1)} %q_ref.7) | copy-start | bytes 3145732
  63.6 11.3 %collective-permute-start = (bf16[512,512]{1,0:T(8,128)(2,1)S(1)}, bf16[512,512]{1,0:T(8,128)(2,1)S(1)}, u32[]{:S(2)}, u32[]{:S(2)}) collective-permute-start(bf16[512,512]{1,0:T(8,128)(2,1)S(1)} %get-tuple-element.24), channel_id=1, source_target_pairs={{0,4},{4,8},{8,12},{12,16},{16,20},{20,24},{24,28},{1,5},{5,9},{9,... | collective-permute-start | bytes 1572872 | tf_op jit(solution)/shard_map/ppermute | solution.py:413
  66.7 31.9 %collective-permute-start.17 = (bf16[256,2048]{1,0:T(8,128)(2,1)S(1)}, bf16[256,2048]{1,0:T(8,128)(2,1)S(1)}, u32[]{:S(2)}, u32[]{:S(2)}) collective-permute-start(bf16[256,2048]{1,0:T(8,128)(2,1)S(1)} %collective-permute-done.16.far), channel_id=1, source_target_pairs={{0,4},{4,0},{8,12},{12,8},{16,20},{20,16},{24,28},{28,24},{1,5},{5... | collective-permute-start | bytes 3145736 | tf_op jit(solution)/shard_map/ppermute | solution.py:32
  67.5 30.3 %collective-permute-start.13 = (bf16[256,1024]{1,0:T(8,128)(2,1)S(1)}, bf16[256,1024]{1,0:T(8,128)(2,1)S(1)}, u32[]{:S(2)}, u32[]{:S(2)}) collective-permute-start(bf16[256,1024]{1,0:T(8,128)(2,1)S(1)} %collective-permute-done.12.near), channel_id=1, source_target_pairs={{0,4},{4,0},{8,12},{12,8},{16,20},{20,16},{24,28},{28,24},{1,5},{5... | collective-permute-start | bytes 1572872 | tf_op jit(solution)/shard_map/ppermute | solution.py:32
  74.9 22.9 %collective-permute-start.15 = (bf16[256,1024]{1,0:T(8,128)(2,1)S(1)}, bf16[256,1024]{1,0:T(8,128)(2,1)S(1)}, u32[]{:S(2)}, u32[]{:S(2)}) collective-permute-start(bf16[256,1024]{1,0:T(8,128)(2,1)S(1)} %collective-permute-done.14.far), channel_id=1, source_target_pairs={{0,4},{4,0},{8,12},{12,8},{16,20},{20,16},{24,28},{28,24},{1,5},{5... | collective-permute-start | bytes 1572872 | tf_op jit(solution)/shard_map/ppermute | solution.py:32
  79.9 10.8 %collective-permute-start.9 = (bf16[256,512]{1,0:T(8,128)(2,1)S(1)}, bf16[256,512]{1,0:T(8,128)(2,1)S(1)}, u32[]{:S(2)}, u32[]{:S(2)}) collective-permute-start(bf16[256,512]{1,0:T(8,128)(2,1)S(1)} %apply.6), channel_id=1, source_target_pairs={{0,3},{1,2},{2,1},{3,0},{4,7},{5,6},{6,5},{7,4},{8,11},{9,10},{10,... | collective-permute-start | bytes 786440 | tf_op jit(solution)/shard_map/ppermute | solution.py:32
  84.4 14.1 %collective-permute-start.8 = (bf16[256,512]{1,0:T(8,128)(2,1)S(1)}, bf16[256,512]{1,0:T(8,128)(2,1)S(1)}, u32[]{:S(2)}, u32[]{:S(2)}) collective-permute-start(bf16[256,512]{1,0:T(8,128)(2,1)S(1)} %apply.5), channel_id=1, source_target_pairs={{0,1},{1,0},{2,3},{3,2},{4,5},{5,4},{6,7},{7,6},{8,9},{9,8},{10,11... | collective-permute-start | bytes 786440 | tf_op jit(solution)/shard_map/ppermute | solution.py:32
  85.1 12.0 %copy-start.3 = (bf16[512,2048]{1,0:T(8,128)(2,1)S(1)}, bf16[512,2048]{1,0:T(8,128)(2,1)}, u32[]{:S(2)}) copy-start(bf16[512,2048]{1,0:T(8,128)(2,1)} %w_ref.1) | copy-start | bytes 6291460
  85.1 12.0 %copy-start.7 = (bf16[512]{0:T(512)(128)(2,1)S(1)}, bf16[512]{0:T(512)(128)(2,1)}, u32[]{:S(2)}) copy-start(bf16[512]{0:T(512)(128)(2,1)} %gain_ref.1) | copy-start | bytes 3076
  90.7 18.2 %collective-permute-start.7 = (bf16[256,512]{1,0:T(8,128)(2,1)S(1)}, bf16[256,512]{1,0:T(8,128)(2,1)S(1)}, u32[]{:S(2)}, u32[]{:S(2)}) collective-permute-start(bf16[256,512]{1,0:T(8,128)(2,1)S(1)} %apply.4), channel_id=1, source_target_pairs={{0,2},{1,3},{2,0},{3,1},{4,6},{5,7},{6,4},{7,5},{8,10},{9,11},{10,... | collective-permute-start | bytes 786440 | tf_op jit(solution)/shard_map/ppermute | solution.py:32
